TPU v7x, 512 devices: a whole 4x4x16 slice. The times are simulated.
512 devices in a mesh: tun: 128 (over z_lo, x, y, core), sec: 4 (over z_hi).
Axes of the slice: x: 4, y: 4, z: 16 (z_hi: 4, z_lo: 4; z = z_hi * 4 + z_lo), core: 2. Of those that a mesh axis runs over, the one named last changes fastest.
Arguments:
- wind_vector: float32 [3, 1024, 64, 128], P(None, 'tun', 'sec'), may hold values from -3 to 3
- thermal_surplus: float32 [1024, 64, 128], P('tun', 'sec'), may hold values from -4 to 4
- carbon_particulate: float32 [1024, 64, 128], P('tun', 'sec'), may hold values from 0 to 1
- particle_bin_weight: float32 [16, 1024, 64, 128], P(None, 'tun', 'sec'), may hold values from 0 to 1
- particle_bin_tally: int32 [1024, 64, 128], P('tun', 'sec'), may hold values from 0 to 16
- spray_region_label: int32 [1024, 64, 128], P('tun', 'sec'), may hold values from 0 to 8
- nozzle_onset_step: int32 [8], replicated, may hold values from 0 to 2
Outputs:
- velocity_out: float32 [3, 1024, 64, 128], P(None, 'tun', 'sec')
- temperature_out: float32 [1024, 64, 128], P('tun', 'sec')
- soot_out: float32 [1024, 64, 128], P('tun', 'sec')
- mass_out: float32 [16, 1024, 64, 128], P(None, 'tun', 'sec')
- count_out: int32 [1024, 64, 128], P('tun', 'sec')
Inputs may be any that keep to these rules, and one draw needn't show every extreme that they name: A cell's live slots are its first particle_bin_tally slots.
All inputs are finite; a program needn't handle non-finite values.
Results may differ from a plain program's by a relative error of at most 0.0003.
Values sent between devices are 32-bit elements; how exact they have to be, the bound alone decides.
No kernel may reach another device: no remote copies, remote signals or barrier semaphores. Data moves between devices by JAX's collectives and lax.ppermute only.
A program may use at most 64 MiB of HBM per device.

v0:
```python
import jax
import jax.numpy as jnp
from jax import lax
from jax.sharding import PartitionSpec as P

visc_base = 0.2
time_step = 0.1
buoyancy = 0.5
drag_rate = 0.3
vent_speed = 1.0
inject_rate = 0.5
evap_rate = 0.4
latent_heat = 0.5
scavenge = 0.3


def extended(cells, sides, width):
    for axis, dim in sides:
        count = lax.axis_size(axis)
        ends = count - 1
        head = lax.slice_in_dim(cells, 0, width, axis=dim)
        tail = lax.slice_in_dim(cells, cells.shape[dim] - width, cells.shape[dim], axis=dim)
        cells = jnp.concatenate(
            [
                lax.ppermute(tail, axis, [(i, (i + 1) % count) for i in range(ends)]),
                cells,
                lax.ppermute(head, axis, [((i + 1) % count, i) for i in range(ends)]),
            ],
            axis=dim,
        )
    return cells


def passed_along(block, axis, distance):
    devices = range(lax.axis_size(axis))
    route = [(i - distance, i) for i in devices if i - distance in devices]
    return lax.ppermute(block, axis, route)


def neighbour(array, dim, offset):
    result = array
    lead = array.ndim - 3
    for split_axis in range(3):
        full = array.shape[lead + split_axis]
        start = 1 + offset if split_axis == dim else 1
        result = lax.slice_in_dim(result, start, start + full - 2, axis=lead + split_axis)
    return result


def advance(padded):
    centre = neighbour(padded, 0, 0)
    viscous = visc_base * (1.0 + 0.5 * jnp.tanh(padded[3]))
    visc_centre = neighbour(viscous, 0, 0)
    diffusion = jnp.zeros_like(centre)
    advection = jnp.zeros_like(centre)
    for dim in range(3):
        upper = neighbour(padded, dim, 1)
        lower = neighbour(padded, dim, -1)
        diffusion = diffusion + 0.5 * (visc_centre + neighbour(viscous, dim, 1)) * (upper - centre)
        diffusion = diffusion + 0.5 * (visc_centre + neighbour(viscous, dim, -1)) * (lower - centre)
        advection = advection + 0.5 * centre[dim] * (upper - lower)
    fresh = centre + time_step * (diffusion - advection)
    along = fresh[0] + time_step * drag_rate * (vent_speed - centre[0])
    upward = fresh[2] + time_step * buoyancy * centre[3]
    return jnp.stack([along, fresh[1], upward, fresh[3], fresh[4]])


def mist(transport_state, mass, count, spray_region_label, nozzle_onset_step, substep):
    slots = jnp.arange(mass.shape[0], dtype=jnp.int32)
    live = (slots[:, None, None, None] < count[None]).astype(jnp.float32)
    zones = jnp.arange(1, nozzle_onset_step.shape[0] + 1, dtype=jnp.int32)
    spraying = (nozzle_onset_step <= substep).astype(jnp.float32)
    zone_hit = (spray_region_label[None] == zones[:, None, None, None]).astype(jnp.float32)
    active = jnp.sum(zone_hit * spraying[:, None, None, None], axis=0)
    mass = mass + inject_rate * live * active[None]
    loaded = jnp.sum(live * mass, axis=0)
    evaporated = evap_rate * live * mass * jax.nn.sigmoid(transport_state[3])[None]
    heat = transport_state[3] - latent_heat * jnp.sum(evaporated, axis=0)
    sooty = transport_state[4] / (1.0 + scavenge * loaded)
    transport_state = jnp.stack(
        [transport_state[0], transport_state[1], transport_state[2], heat, sooty]
    )
    return (transport_state, mass - evaporated)


def local(
    wind_vector,
    thermal_surplus,
    carbon_particulate,
    particle_bin_weight,
    particle_bin_tally,
    spray_region_label,
    nozzle_onset_step,
):
    transport_state = jnp.concatenate(
        [wind_vector, thermal_surplus[None], carbon_particulate[None]], axis=0
    )
    mass, count = (particle_bin_weight, particle_bin_tally)
    slot_total = mass.shape[0]
    for substep in range(2):
        moving = extended(transport_state[0:3], (("tun", 1), ("sec", 2)), 1)
        heated = extended(transport_state[3], (("tun", 0), ("sec", 1)), 1)
        smoke = extended(transport_state[4], (("tun", 0), ("sec", 1)), 1)
        padded = jnp.concatenate([moving, heated[None], smoke[None]], axis=0)
        outgoing = jnp.concatenate([mass[:, -1], count[-1][None].astype(jnp.float32)], axis=0)
        incoming = passed_along(outgoing, "tun", 1)
        padded = jnp.pad(padded, ((0, 0), (0, 0), (0, 0), (1, 1)))
        transport_state = advance(padded)
        mass = jnp.concatenate([incoming[:slot_total][:, None], mass[:, :-1]], axis=1)
        count = jnp.concatenate([incoming[slot_total][None].astype(jnp.int32), count[:-1]], axis=0)
        transport_state, mass = mist(
            transport_state, mass, count, spray_region_label, nozzle_onset_step, substep
        )
    return (transport_state[0:3], transport_state[3], transport_state[4], mass, count)


def solution(mesh):
    return jax.shard_map(
        local,
        mesh=mesh,
        in_specs=(
            P(None, "tun", "sec", None),
            P("tun", "sec", None),
            P("tun", "sec", None),
            P(None, "tun", "sec", None),
            P("tun", "sec", None),
            P("tun", "sec", None),
            P(),
        ),
        out_specs=(
            P(None, "tun", "sec", None),
            P("tun", "sec", None),
            P("tun", "sec", None),
            P(None, "tun", "sec", None),
            P("tun", "sec", None),
        ),
        check_vma=False,
    )
```

profile of v0, /device:TPU:32, one launch (start us, length us, event | category | flops | bytes accessed | tf_op | source)
XLA Modules:
  0.0 150.9 jit_solution(8153776433946837459)
XLA Ops:
  0.7 0.8 fusion.41
  1.4 6.1 %collective-permute-start.9 = (f32[1,16,128]{2,1,0:T(8,128)S(1)}, f32[1,16,128]{2,1,0:T(8,128)S(1)}, u32[]{:S(2)}, u32[]{:S(2)}) collective-permute-start(f32[1,16,128]{2,1,0:T(8,128)S(1)} %get-tuple-element.81), channel_id=1, source_target_pairs={{4,0},{8,4},{12,8},{16,12},{20,16},{24,20},{28,24},{32,28},{36,32}... | collective-permute-start | bytes 24584 | tf_op jit(solution)/shard_map/ppermute | solution.py:27
  7.5 1.9 %collective-permute-start.8 = (f32[1,16,128]{2,1,0:T(8,128)S(1)}, f32[1,16,128]{2,1,0:T(8,128)S(1)}, u32[]{:S(2)}, u32[]{:S(2)}) collective-permute-start(f32[1,16,128]{2,1,0:T(8,128)S(1)} %get-tuple-element.82), channel_id=1, source_target_pairs={{0,4},{4,8},{8,12},{12,16},{16,20},{20,24},{24,28},{28,32},{32,36}... | collective-permute-start | bytes 24584 | tf_op jit(solution)/shard_map/ppermute | solution.py:25
  9.5 0.7 fusion.40
  10.2 7.8 %collective-permute-start.5 = (f32[1,16,128]{2,1,0:T(8,128)S(1)}, f32[1,16,128]{2,1,0:T(8,128)S(1)}, u32[]{:S(2)}, u32[]{:S(2)}) collective-permute-start(f32[1,16,128]{2,1,0:T(8,128)S(1)} %get-tuple-element.79), channel_id=1, source_target_pairs={{4,0},{8,4},{12,8},{16,12},{20,16},{24,20},{28,24},{32,28},{36,32}... | collective-permute-start | bytes 24584 | tf_op jit(solution)/shard_map/ppermute | solution.py:27
  18.0 1.9 %collective-permute-start.4 = (f32[1,16,128]{2,1,0:T(8,128)S(1)}, f32[1,16,128]{2,1,0:T(8,128)S(1)}, u32[]{:S(2)}, u32[]{:S(2)}) collective-permute-start(f32[1,16,128]{2,1,0:T(8,128)S(1)} %get-tuple-element.80), channel_id=1, source_target_pairs={{0,4},{4,8},{8,12},{12,16},{16,20},{20,24},{24,28},{28,32},{32,36}... | collective-permute-start | bytes 24584 | tf_op jit(solution)/shard_map/ppermute | solution.py:25
  20.0 0.8 fusion.35
  20.7 7.8 %collective-permute-start.1 = (f32[3,1,16,128]{3,2,1,0:T(8,128)S(1)}, f32[3,1,16,128]{3,2,1,0:T(8,128)S(1)}, u32[]{:S(2)}, u32[]{:S(2)}) collective-permute-start(f32[3,1,16,128]{3,2,1,0:T(8,128)S(1)} %get-tuple-element.63), channel_id=1, source_target_pairs={{4,0},{8,4},{12,8},{16,12},{20,16},{24,20},{28,24},{32,28},{36,32}... | collective-permute-start | bytes 73736 | tf_op jit(solution)/shard_map/ppermute | solution.py:27
  28.6 0.9 multiply_bitcast_fusion.5
  29.5 0.7 compare_convert_fusion.1
  30.2 0.7 slice_convert_fusion.2
  30.9 0.9 slice_bitcast_fusion.3
  31.8 1.9 %collective-permute-start = (f32[3,1,16,128]{3,2,1,0:T(8,128)S(1)}, f32[3,1,16,128]{3,2,1,0:T(8,128)S(1)}, u32[]{:S(2)}, u32[]{:S(2)}) collective-permute-start(f32[3,1,16,128]{3,2,1,0:T(8,128)S(1)} %get-tuple-element.64), channel_id=1, source_target_pairs={{0,4},{4,8},{8,12},{12,16},{16,20},{20,24},{24,28},{28,32},{32,36}... | collective-permute-start | bytes 73736 | tf_op jit(solution)/shard_map/ppermute | solution.py:25
  33.8 1.9 %collective-permute-start.16 = (f32[17,16,128]{2,1,0:T(8,128)S(1)}, f32[17,16,128]{2,1,0:T(8,128)S(1)}, u32[]{:S(2)}, u32[]{:S(2)}) collective-permute-start(f32[17,16,128]{2,1,0:T(8,128)S(1)} %pad_maximum_fusion.3), channel_id=1, source_target_pairs={{0,4},{4,8},{8,12},{12,16},{16,20},{20,24},{24,28},{28,32},{32,36}... | collective-permute-start | bytes 417800 | tf_op jit(solution)/shard_map/ppermute | solution.py:37
  35.8 9.1 %collective-permute-start.6 = (f32[10,1,128]{2,1,0:T(1,128)S(1)}, f32[10,1,128]{2,1,0:T(1,128)S(1)}, u32[]{:S(2)}, u32[]{:S(2)}) collective-permute-start(f32[10,1,128]{2,1,0:T(1,128)S(1)} %get-tuple-element.69), channel_id=1, source_target_pairs={{0,1},{1,2},{2,3},{4,5},{5,6},{6,7},{8,9},{9,10},{10,11},{12,13},{... | collective-permute-start | bytes 15368 | tf_op jit(solution)/shard_map/ppermute | solution.py:25
  44.9 1.3 collective-permute-start.7
  46.3 9.7 %collective-permute-start.10 = (f32[10,1,128]{2,1,0:T(1,128)S(1)}, f32[10,1,128]{2,1,0:T(1,128)S(1)}, u32[]{:S(2)}, u32[]{:S(2)}) collective-permute-start(f32[10,1,128]{2,1,0:T(1,128)S(1)} %get-tuple-element.71), channel_id=1, source_target_pairs={{0,1},{1,2},{2,3},{4,5},{5,6},{6,7},{8,9},{9,10},{10,11},{12,13},{... | collective-permute-start | bytes 15368 | tf_op jit(solution)/shard_map/ppermute | solution.py:25
  56.0 1.3 collective-permute-start.11
  57.5 8.5 %collective-permute-start.2 = (f32[3,10,1,128]{3,2,1,0:T(1,128)S(1)}, f32[3,10,1,128]{3,2,1,0:T(1,128)S(1)}, u32[]{:S(2)}, u32[]{:S(2)}) collective-permute-start(f32[3,10,1,128]{3,2,1,0:T(1,128)S(1)} %get-tuple-element.56), channel_id=1, source_target_pairs={{0,1},{1,2},{2,3},{4,5},{5,6},{6,7},{8,9},{9,10},{10,11},{12,13},{... | collective-permute-start | bytes 46088 | tf_op jit(solution)/shard_map/ppermute | solution.py:25
  65.9 1.3 collective-permute-start.3
  67.3 8.1 %collective-permute-done.3 = f32[3,10,1,128]{3,2,1,0:T(1,128)S(1)} collective-permute-done((f32[3,10,1,128]{3,2,1,0:T(1,128)S(1)}, f32[3,10,1,128]{3,2,1,0:T(1,128)S(1)}, u32[]{:S(2)}, u32[]{:S(2)}) %collective-permute-start.3) | collective-permute-done | bytes 15392 | tf_op jit(solution)/shard_map/ppermute | solution.py:27
  75.5 0.1 fusion.10
  75.7 0.2 fusion.31
  75.9 0.4 multiply_add_fusion.1
  76.4 2.1 %collective-permute-start.12 = (f32[3,1,16,128]{3,2,1,0:T(8,128)S(1)}, f32[3,1,16,128]{3,2,1,0:T(8,128)S(1)}, u32[]{:S(2)}, u32[]{:S(2)}) collective-permute-start(f32[3,1,16,128]{3,2,1,0:T(8,128)S(1)} %get-tuple-element.58), channel_id=1, source_target_pairs={{0,4},{4,8},{8,12},{12,16},{16,20},{20,24},{24,28},{28,32},{32,36}... | collective-permute-start | bytes 73736 | tf_op jit(solution)/shard_map/ppermute | solution.py:25
  78.5 7.9 %collective-permute-start.13 = (f32[3,1,16,128]{3,2,1,0:T(8,128)S(1)}, f32[3,1,16,128]{3,2,1,0:T(8,128)S(1)}, u32[]{:S(2)}, u32[]{:S(2)}) collective-permute-start(f32[3,1,16,128]{3,2,1,0:T(8,128)S(1)} %get-tuple-element.59), channel_id=1, source_target_pairs={{4,0},{8,4},{12,8},{16,12},{20,16},{24,20},{28,24},{32,28},{36,32}... | collective-permute-start | bytes 73736 | tf_op jit(solution)/shard_map/ppermute | solution.py:27
  86.3 0.2 fusion.5
  86.5 1.3 collective-permute-done.13
  87.9 7.8 %collective-permute-start.14 = (f32[3,10,1,128]{3,2,1,0:T(1,128)S(1)}, f32[3,10,1,128]{3,2,1,0:T(1,128)S(1)}, u32[]{:S(2)}, u32[]{:S(2)}) collective-permute-start(f32[3,10,1,128]{3,2,1,0:T(1,128)S(1)} %get-tuple-element.48), channel_id=1, source_target_pairs={{0,1},{1,2},{2,3},{4,5},{5,6},{6,7},{8,9},{9,10},{10,11},{12,13},{... | collective-permute-start | bytes 46088 | tf_op jit(solution)/shard_map/ppermute | solution.py:25
  95.7 1.3 collective-permute-start.15
  97.1 0.4 select_reduce_fusion.1
  97.5 1.9 %collective-permute-start.17 = (f32[1,16,128]{2,1,0:T(8,128)S(1)}, f32[1,16,128]{2,1,0:T(8,128)S(1)}, u32[]{:S(2)}, u32[]{:S(2)}) collective-permute-start(f32[1,16,128]{2,1,0:T(8,128)S(1)} %get-tuple-element.77), channel_id=1, source_target_pairs={{0,4},{4,8},{8,12},{12,16},{16,20},{20,24},{24,28},{28,32},{32,36}... | collective-permute-start | bytes 24584 | tf_op jit(solution)/shard_map/ppermute | solution.py:25
  99.4 7.9 %collective-permute-start.18 = (f32[1,16,128]{2,1,0:T(8,128)S(1)}, f32[1,16,128]{2,1,0:T(8,128)S(1)}, u32[]{:S(2)}, u32[]{:S(2)}) collective-permute-start(f32[1,16,128]{2,1,0:T(8,128)S(1)} %get-tuple-element.78), channel_id=1, source_target_pairs={{4,0},{8,4},{12,8},{16,12},{20,16},{24,20},{28,24},{32,28},{36,32}... | collective-permute-start | bytes 24584 | tf_op jit(solution)/shard_map/ppermute | solution.py:27
  107.4 1.9 %collective-permute-start.21 = (f32[1,16,128]{2,1,0:T(8,128)S(1)}, f32[1,16,128]{2,1,0:T(8,128)S(1)}, u32[]{:S(2)}, u32[]{:S(2)}) collective-permute-start(f32[1,16,128]{2,1,0:T(8,128)S(1)} %get-tuple-element.75), channel_id=1, source_target_pairs={{0,4},{4,8},{8,12},{12,16},{16,20},{20,24},{24,28},{28,32},{32,36}... | collective-permute-start | bytes 24584 | tf_op jit(solution)/shard_map/ppermute | solution.py:25
  109.3 7.9 %collective-permute-start.22 = (f32[1,16,128]{2,1,0:T(8,128)S(1)}, f32[1,16,128]{2,1,0:T(8,128)S(1)}, u32[]{:S(2)}, u32[]{:S(2)}) collective-permute-start(f32[1,16,128]{2,1,0:T(8,128)S(1)} %get-tuple-element.76), channel_id=1, source_target_pairs={{4,0},{8,4},{12,8},{16,12},{20,16},{24,20},{28,24},{32,28},{36,32}... | collective-permute-start | bytes 24584 | tf_op jit(solution)/shard_map/ppermute | solution.py:27
  117.2 1.9 %collective-permute-start.25 = (f32[17,16,128]{2,1,0:T(8,128)S(1)}, f32[17,16,128]{2,1,0:T(8,128)S(1)}, u32[]{:S(2)}, u32[]{:S(2)}) collective-permute-start(f32[17,16,128]{2,1,0:T(8,128)S(1)} %pad_maximum_fusion.4), channel_id=1, source_target_pairs={{0,4},{4,8},{8,12},{12,16},{16,20},{20,24},{24,28},{28,32},{32,36}... | collective-permute-start | bytes 417800 | tf_op jit(solution)/shard_map/ppermute | solution.py:37
  119.2 8.5 %collective-permute-start.19 = (f32[10,1,128]{2,1,0:T(1,128)S(1)}, f32[10,1,128]{2,1,0:T(1,128)S(1)}, u32[]{:S(2)}, u32[]{:S(2)}) collective-permute-start(f32[10,1,128]{2,1,0:T(1,128)S(1)} %get-tuple-element.67), channel_id=1, source_target_pairs={{0,1},{1,2},{2,3},{4,5},{5,6},{6,7},{8,9},{9,10},{10,11},{12,13},{... | collective-permute-start | bytes 15368 | tf_op jit(solution)/shard_map/ppermute | solution.py:25
  127.7 1.3 collective-permute-start.20
  129.0 8.5 %collective-permute-start.23 = (f32[10,1,128]{2,1,0:T(1,128)S(1)}, f32[10,1,128]{2,1,0:T(1,128)S(1)}, u32[]{:S(2)}, u32[]{:S(2)}) collective-permute-start(f32[10,1,128]{2,1,0:T(1,128)S(1)} %get-tuple-element.65), channel_id=1, source_target_pairs={{0,1},{1,2},{2,3},{4,5},{5,6},{6,7},{8,9},{9,10},{10,11},{12,13},{... | collective-permute-start | bytes 15368 | tf_op jit(solution)/shard_map/ppermute | solution.py:25
  137.5 1.3 collective-permute-start.24
  138.8 8.1 %collective-permute-done.24 = f32[10,1,128]{2,1,0:T(1,128)S(1)} collective-permute-done((f32[10,1,128]{2,1,0:T(1,128)S(1)}, f32[10,1,128]{2,1,0:T(1,128)S(1)}, u32[]{:S(2)}, u32[]{:S(2)}) %collective-permute-start.24) | collective-permute-done | bytes 5152 | tf_op jit(solution)/shard_map/ppermute | solution.py:27
  147.1 0.2 fusion.23
  147.3 0.4 multiply_add_fusion
  147.8 0.7 pad_maximum_fusion.2
  148.6 0.4 select_reduce_fusion
  149.0 0.2 copy-done.2
  149.2 1.1 copy.17
  150.2 0.7 fusion.16
  (77 shorter events, 1.0 us)
Async XLA Ops:
  0.6 44.3 %copy-start.4 = (f32[8,16,128]{2,1,0:T(8,128)S(1)}, f32[8,16,128]{2,1,0:T(8,128)}, u32[]{:S(2)}) copy-start(f32[8,16,128]{2,1,0:T(8,128)} %param.9) | copy-start | bytes 196612
  0.6 33.1 %copy-start.3 = (f32[8,16,128]{2,1,0:T(8,128)S(1)}, f32[8,16,128]{2,1,0:T(8,128)}, u32[]{:S(2)}) copy-start(f32[8,16,128]{2,1,0:T(8,128)} %param.8) | copy-start | bytes 196612
  0.7 56.7 %copy-start = (f32[3,8,16,128]{3,2,1,0:T(8,128)S(1)}, f32[3,8,16,128]{3,2,1,0:T(8,128)}, u32[]{:S(2)}) copy-start(f32[3,8,16,128]{3,2,1,0:T(8,128)} %param.7) | copy-start | bytes 589828
  1.4 43.5 %collective-permute-start.9 = (f32[1,16,128]{2,1,0:T(8,128)S(1)}, f32[1,16,128]{2,1,0:T(8,128)S(1)}, u32[]{:S(2)}, u32[]{:S(2)}) collective-permute-start(f32[1,16,128]{2,1,0:T(8,128)S(1)} %get-tuple-element.81), channel_id=1, source_target_pairs={{4,0},{8,4},{12,8},{16,12},{20,16},{24,20},{28,24},{32,28},{36,32}... | collective-permute-start | bytes 24584 | tf_op jit(solution)/shard_map/ppermute | solution.py:27
  7.5 28.3 %collective-permute-start.8 = (f32[1,16,128]{2,1,0:T(8,128)S(1)}, f32[1,16,128]{2,1,0:T(8,128)S(1)}, u32[]{:S(2)}, u32[]{:S(2)}) collective-permute-start(f32[1,16,128]{2,1,0:T(8,128)S(1)} %get-tuple-element.82), channel_id=1, source_target_pairs={{0,4},{4,8},{8,12},{12,16},{16,20},{20,24},{24,28},{28,32},{32,36}... | collective-permute-start | bytes 24584 | tf_op jit(solution)/shard_map/ppermute | solution.py:25
  10.2 23.6 %collective-permute-start.5 = (f32[1,16,128]{2,1,0:T(8,128)S(1)}, f32[1,16,128]{2,1,0:T(8,128)S(1)}, u32[]{:S(2)}, u32[]{:S(2)}) collective-permute-start(f32[1,16,128]{2,1,0:T(8,128)S(1)} %get-tuple-element.79), channel_id=1, source_target_pairs={{4,0},{8,4},{12,8},{16,12},{20,16},{24,20},{28,24},{32,28},{36,32}... | collective-permute-start | bytes 24584 | tf_op jit(solution)/shard_map/ppermute | solution.py:27
  18.0 13.8 %collective-permute-start.4 = (f32[1,16,128]{2,1,0:T(8,128)S(1)}, f32[1,16,128]{2,1,0:T(8,128)S(1)}, u32[]{:S(2)}, u32[]{:S(2)}) collective-permute-start(f32[1,16,128]{2,1,0:T(8,128)S(1)} %get-tuple-element.80), channel_id=1, source_target_pairs={{0,4},{4,8},{8,12},{12,16},{16,20},{20,24},{24,28},{28,32},{32,36}... | collective-permute-start | bytes 24584 | tf_op jit(solution)/shard_map/ppermute | solution.py:25
  20.7 36.7 %collective-permute-start.1 = (f32[3,1,16,128]{3,2,1,0:T(8,128)S(1)}, f32[3,1,16,128]{3,2,1,0:T(8,128)S(1)}, u32[]{:S(2)}, u32[]{:S(2)}) collective-permute-start(f32[3,1,16,128]{3,2,1,0:T(8,128)S(1)} %get-tuple-element.63), channel_id=1, source_target_pairs={{4,0},{8,4},{12,8},{16,12},{20,16},{24,20},{28,24},{32,28},{36,32}... | collective-permute-start | bytes 73736 | tf_op jit(solution)/shard_map/ppermute | solution.py:27
  31.8 25.5 %collective-permute-start = (f32[3,1,16,128]{3,2,1,0:T(8,128)S(1)}, f32[3,1,16,128]{3,2,1,0:T(8,128)S(1)}, u32[]{:S(2)}, u32[]{:S(2)}) collective-permute-start(f32[3,1,16,128]{3,2,1,0:T(8,128)S(1)} %get-tuple-element.64), channel_id=1, source_target_pairs={{0,4},{4,8},{8,12},{12,16},{16,20},{20,24},{24,28},{28,32},{32,36}... | collective-permute-start | bytes 73736 | tf_op jit(solution)/shard_map/ppermute | solution.py:25
  33.8 63.2 %collective-permute-start.16 = (f32[17,16,128]{2,1,0:T(8,128)S(1)}, f32[17,16,128]{2,1,0:T(8,128)S(1)}, u32[]{:S(2)}, u32[]{:S(2)}) collective-permute-start(f32[17,16,128]{2,1,0:T(8,128)S(1)} %pad_maximum_fusion.3), channel_id=1, source_target_pairs={{0,4},{4,8},{8,12},{12,16},{16,20},{20,24},{24,28},{28,32},{32,36}... | collective-permute-start | bytes 417800 | tf_op jit(solution)/shard_map/ppermute | solution.py:37
  35.8 10.5 %collective-permute-start.6 = (f32[10,1,128]{2,1,0:T(1,128)S(1)}, f32[10,1,128]{2,1,0:T(1,128)S(1)}, u32[]{:S(2)}, u32[]{:S(2)}) collective-permute-start(f32[10,1,128]{2,1,0:T(1,128)S(1)} %get-tuple-element.69), channel_id=1, source_target_pairs={{0,1},{1,2},{2,3},{4,5},{5,6},{6,7},{8,9},{9,10},{10,11},{12,13},{... | collective-permute-start | bytes 15368 | tf_op jit(solution)/shard_map/ppermute | solution.py:25
  44.9 11.1 %collective-permute-start.7 = (f32[10,1,128]{2,1,0:T(1,128)S(1)}, f32[10,1,128]{2,1,0:T(1,128)S(1)}, u32[]{:S(2)}, u32[]{:S(2)}) collective-permute-start(f32[10,1,128]{2,1,0:T(1,128)S(1)} %get-tuple-element.70), channel_id=1, source_target_pairs={{1,0},{2,1},{3,2},{5,4},{6,5},{7,6},{9,8},{10,9},{11,10},{13,12},{... | collective-permute-start | bytes 15368 | tf_op jit(solution)/shard_map/ppermute | solution.py:27
  46.3 21.0 %collective-permute-start.10 = (f32[10,1,128]{2,1,0:T(1,128)S(1)}, f32[10,1,128]{2,1,0:T(1,128)S(1)}, u32[]{:S(2)}, u32[]{:S(2)}) collective-permute-start(f32[10,1,128]{2,1,0:T(1,128)S(1)} %get-tuple-element.71), channel_id=1, source_target_pairs={{0,1},{1,2},{2,3},{4,5},{5,6},{6,7},{8,9},{9,10},{10,11},{12,13},{... | collective-permute-start | bytes 15368 | tf_op jit(solution)/shard_map/ppermute | solution.py:25
  56.0 11.2 %collective-permute-start.11 = (f32[10,1,128]{2,1,0:T(1,128)S(1)}, f32[10,1,128]{2,1,0:T(1,128)S(1)}, u32[]{:S(2)}, u32[]{:S(2)}) collective-permute-start(f32[10,1,128]{2,1,0:T(1,128)S(1)} %get-tuple-element.72), channel_id=1, source_target_pairs={{1,0},{2,1},{3,2},{5,4},{6,5},{7,6},{9,8},{10,9},{11,10},{13,12},{... | collective-permute-start | bytes 15368 | tf_op jit(solution)/shard_map/ppermute | solution.py:27
  57.5 9.9 %collective-permute-start.2 = (f32[3,10,1,128]{3,2,1,0:T(1,128)S(1)}, f32[3,10,1,128]{3,2,1,0:T(1,128)S(1)}, u32[]{:S(2)}, u32[]{:S(2)}) collective-permute-start(f32[3,10,1,128]{3,2,1,0:T(1,128)S(1)} %get-tuple-element.56), channel_id=1, source_target_pairs={{0,1},{1,2},{2,3},{4,5},{5,6},{6,7},{8,9},{9,10},{10,11},{12,13},{... | collective-permute-start | bytes 46088 | tf_op jit(solution)/shard_map/ppermute | solution.py:25
  65.9 9.5 %collective-permute-start.3 = (f32[3,10,1,128]{3,2,1,0:T(1,128)S(1)}, f32[3,10,1,128]{3,2,1,0:T(1,128)S(1)}, u32[]{:S(2)}, u32[]{:S(2)}) collective-permute-start(f32[3,10,1,128]{3,2,1,0:T(1,128)S(1)} %get-tuple-element.57), channel_id=1, source_target_pairs={{1,0},{2,1},{3,2},{5,4},{6,5},{7,6},{9,8},{10,9},{11,10},{13,12},{... | collective-permute-start | bytes 46088 | tf_op jit(solution)/shard_map/ppermute | solution.py:27
  75.8 10.5 %copy-start.6 = (s32[8,16,128]{2,1,0:T(8,128)S(1)}, s32[8,16,128]{2,1,0:T(8,128)}, u32[]{:S(2)}) copy-start(s32[8,16,128]{2,1,0:T(8,128)} %param.12) | copy-start | bytes 196612
  76.3 10.2 %copy-start.5 = (s32[8,16,128]{2,1,0:T(8,128)S(1)}, s32[8,16,128]{2,1,0:T(8,128)}, u32[]{:S(2)}) copy-start(s32[8,16,128]{2,1,0:T(8,128)} %param.11) | copy-start | bytes 196612
  76.3 20.7 %copy-start.1 = (f32[16,8,16,128]{3,2,1,0:T(8,128)S(1)}, f32[16,8,16,128]{3,2,1,0:T(8,128)}, u32[]{:S(2)}) copy-start(f32[16,8,16,128]{3,2,1,0:T(8,128)} %param.10) | copy-start | bytes 3145732
  76.4 10.1 %collective-permute-start.12 = (f32[3,1,16,128]{3,2,1,0:T(8,128)S(1)}, f32[3,1,16,128]{3,2,1,0:T(8,128)S(1)}, u32[]{:S(2)}, u32[]{:S(2)}) collective-permute-start(f32[3,1,16,128]{3,2,1,0:T(8,128)S(1)} %get-tuple-element.58), channel_id=1, source_target_pairs={{0,4},{4,8},{8,12},{12,16},{16,20},{20,24},{24,28},{28,32},{32,36}... | collective-permute-start | bytes 73736 | tf_op jit(solution)/shard_map/ppermute | solution.py:25
  78.5 9.4 %collective-permute-start.13 = (f32[3,1,16,128]{3,2,1,0:T(8,128)S(1)}, f32[3,1,16,128]{3,2,1,0:T(8,128)S(1)}, u32[]{:S(2)}, u32[]{:S(2)}) collective-permute-start(f32[3,1,16,128]{3,2,1,0:T(8,128)S(1)} %get-tuple-element.59), channel_id=1, source_target_pairs={{4,0},{8,4},{12,8},{16,12},{20,16},{24,20},{28,24},{32,28},{36,32}... | collective-permute-start | bytes 73736 | tf_op jit(solution)/shard_map/ppermute | solution.py:27
  87.9 59.1 %collective-permute-start.14 = (f32[3,10,1,128]{3,2,1,0:T(1,128)S(1)}, f32[3,10,1,128]{3,2,1,0:T(1,128)S(1)}, u32[]{:S(2)}, u32[]{:S(2)}) collective-permute-start(f32[3,10,1,128]{3,2,1,0:T(1,128)S(1)} %get-tuple-element.48), channel_id=1, source_target_pairs={{0,1},{1,2},{2,3},{4,5},{5,6},{6,7},{8,9},{9,10},{10,11},{12,13},{... | collective-permute-start | bytes 46088 | tf_op jit(solution)/shard_map/ppermute | solution.py:25
  95.7 51.2 %collective-permute-start.15 = (f32[3,10,1,128]{3,2,1,0:T(1,128)S(1)}, f32[3,10,1,128]{3,2,1,0:T(1,128)S(1)}, u32[]{:S(2)}, u32[]{:S(2)}) collective-permute-start(f32[3,10,1,128]{3,2,1,0:T(1,128)S(1)} %get-tuple-element.49), channel_id=1, source_target_pairs={{1,0},{2,1},{3,2},{5,4},{6,5},{7,6},{9,8},{10,9},{11,10},{13,12},{... | collective-permute-start | bytes 46088 | tf_op jit(solution)/shard_map/ppermute | solution.py:27
  97.5 11.8 %collective-permute-start.17 = (f32[1,16,128]{2,1,0:T(8,128)S(1)}, f32[1,16,128]{2,1,0:T(8,128)S(1)}, u32[]{:S(2)}, u32[]{:S(2)}) collective-permute-start(f32[1,16,128]{2,1,0:T(8,128)S(1)} %get-tuple-element.77), channel_id=1, source_target_pairs={{0,4},{4,8},{8,12},{12,16},{16,20},{20,24},{24,28},{28,32},{32,36}... | collective-permute-start | bytes 24584 | tf_op jit(solution)/shard_map/ppermute | solution.py:25
  99.4 17.8 %collective-permute-start.18 = (f32[1,16,128]{2,1,0:T(8,128)S(1)}, f32[1,16,128]{2,1,0:T(8,128)S(1)}, u32[]{:S(2)}, u32[]{:S(2)}) collective-permute-start(f32[1,16,128]{2,1,0:T(8,128)S(1)} %get-tuple-element.78), channel_id=1, source_target_pairs={{4,0},{8,4},{12,8},{16,12},{20,16},{24,20},{28,24},{32,28},{36,32}... | collective-permute-start | bytes 24584 | tf_op jit(solution)/shard_map/ppermute | solution.py:27
  107.4 11.8 %collective-permute-start.21 = (f32[1,16,128]{2,1,0:T(8,128)S(1)}, f32[1,16,128]{2,1,0:T(8,128)S(1)}, u32[]{:S(2)}, u32[]{:S(2)}) collective-permute-start(f32[1,16,128]{2,1,0:T(8,128)S(1)} %get-tuple-element.75), channel_id=1, source_target_pairs={{0,4},{4,8},{8,12},{12,16},{16,20},{20,24},{24,28},{28,32},{32,36}... | collective-permute-start | bytes 24584 | tf_op jit(solution)/shard_map/ppermute | solution.py:25
  109.3 18.3 %collective-permute-start.22 = (f32[1,16,128]{2,1,0:T(8,128)S(1)}, f32[1,16,128]{2,1,0:T(8,128)S(1)}, u32[]{:S(2)}, u32[]{:S(2)}) collective-permute-start(f32[1,16,128]{2,1,0:T(8,128)S(1)} %get-tuple-element.76), channel_id=1, source_target_pairs={{4,0},{8,4},{12,8},{16,12},{20,16},{24,20},{28,24},{32,28},{36,32}... | collective-permute-start | bytes 24584 | tf_op jit(solution)/shard_map/ppermute | solution.py:27
  117.2 31.3 %collective-permute-start.25 = (f32[17,16,128]{2,1,0:T(8,128)S(1)}, f32[17,16,128]{2,1,0:T(8,128)S(1)}, u32[]{:S(2)}, u32[]{:S(2)}) collective-permute-start(f32[17,16,128]{2,1,0:T(8,128)S(1)} %pad_maximum_fusion.4), channel_id=1, source_target_pairs={{0,4},{4,8},{8,12},{12,16},{16,20},{20,24},{24,28},{28,32},{32,36}... | collective-permute-start | bytes 417800 | tf_op jit(solution)/shard_map/ppermute | solution.py:37
  119.2 9.8 %collective-permute-start.19 = (f32[10,1,128]{2,1,0:T(1,128)S(1)}, f32[10,1,128]{2,1,0:T(1,128)S(1)}, u32[]{:S(2)}, u32[]{:S(2)}) collective-permute-start(f32[10,1,128]{2,1,0:T(1,128)S(1)} %get-tuple-element.67), channel_id=1, source_target_pairs={{0,1},{1,2},{2,3},{4,5},{5,6},{6,7},{8,9},{9,10},{10,11},{12,13},{... | collective-permute-start | bytes 15368 | tf_op jit(solution)/shard_map/ppermute | solution.py:25
  127.7 9.8 %collective-permute-start.20 = (f32[10,1,128]{2,1,0:T(1,128)S(1)}, f32[10,1,128]{2,1,0:T(1,128)S(1)}, u32[]{:S(2)}, u32[]{:S(2)}) collective-permute-start(f32[10,1,128]{2,1,0:T(1,128)S(1)} %get-tuple-element.68), channel_id=1, source_target_pairs={{1,0},{2,1},{3,2},{5,4},{6,5},{7,6},{9,8},{10,9},{11,10},{13,12},{... | collective-permute-start | bytes 15368 | tf_op jit(solution)/shard_map/ppermute | solution.py:27
  129.0 9.8 %collective-permute-start.23 = (f32[10,1,128]{2,1,0:T(1,128)S(1)}, f32[10,1,128]{2,1,0:T(1,128)S(1)}, u32[]{:S(2)}, u32[]{:S(2)}) collective-permute-start(f32[10,1,128]{2,1,0:T(1,128)S(1)} %get-tuple-element.65), channel_id=1, source_target_pairs={{0,1},{1,2},{2,3},{4,5},{5,6},{6,7},{8,9},{9,10},{10,11},{12,13},{... | collective-permute-start | bytes 15368 | tf_op jit(solution)/shard_map/ppermute | solution.py:25
  137.5 9.4 %collective-permute-start.24 = (f32[10,1,128]{2,1,0:T(1,128)S(1)}, f32[10,1,128]{2,1,0:T(1,128)S(1)}, u32[]{:S(2)}, u32[]{:S(2)}) collective-permute-start(f32[10,1,128]{2,1,0:T(1,128)S(1)} %get-tuple-element.66), channel_id=1, source_target_pairs={{1,0},{2,1},{3,2},{5,4},{6,5},{7,6},{9,8},{10,9},{11,10},{13,12},{... | collective-permute-start | bytes 15368 | tf_op jit(solution)/shard_map/ppermute | solution.py:27
  148.5 0.6 copy-start.2
where the time goes:
time: 152 us; the launch traced here: 151 us
  starting transfers between devices  121 us (80%)
  waiting for transfers between devices  17.6 us (12%)
  other arithmetic  6.55 us (4%)
  local copies, waits for them, and re-layouts  4.69 us (3%)
    ppermute x12, starting transfers between devices, extended(): lax.ppermute(tail, axis, [(i, (i + 1) % count) for i in range(ends)])  63.7 us
    ppermute x12, starting transfers between devices, extended(): lax.ppermute(head, axis, [((i + 1) % count, i) for i in range(ends)])  53.1 us
    ppermute x12, waiting for transfers between devices, extended(): lax.ppermute(head, axis, [((i + 1) % count, i) for i in range(ends)])  17.5 us
    ppermute x2, starting transfers between devices, passed_along(): return lax.ppermute(block, axis, route)  3.84 us
  transfers between devices with their start and end apart: 26, of which 4 were waited for; matrix products, arithmetic and copies ran while one was open for 5% of the time, Pallas kernels for 0%

commit v1 on v0

v1 whole, which is shorter than its diff:
```python
import jax
import jax.numpy as jnp
from jax import lax
from jax.experimental import pallas as pl
from jax.experimental.pallas import tpu as pltpu
from jax.sharding import PartitionSpec as P

visc_base = 0.2
time_step = 0.1
buoyancy = 0.5
drag_rate = 0.3
vent_speed = 1.0
inject_rate = 0.5
evap_rate = 0.4
latent_heat = 0.5
scavenge = 0.3

NF = 5
F32 = jnp.float32
VMEM = pl.BlockSpec(memory_space=pltpu.VMEM)
SMEM = pl.BlockSpec(memory_space=pltpu.SMEM)
ANY = pl.BlockSpec(memory_space=pl.ANY)
ROW = 8


def copies(pairs, sems):
    started = []
    for n, (src, dst) in enumerate(pairs):
        copy = pltpu.make_async_copy(src, dst, sems.at[n])
        copy.start()
        started.append(copy)
    return started


def live_sum(mass, count):
    total = jnp.zeros(count.shape, F32)
    for k in range(mass.shape[0]):
        total = total + jnp.where(count > k, mass[k], 0.0)
    return total


def pack_tun_kernel(wind, heat, soot, mass, count, label, msg_a, msg_b, total, fields, masses, counts, labels, sems):
    depth = heat.shape[0]
    pending = copies(
        [
            (mass, masses),
            (count, counts),
            (wind, fields.at[0:3]),
            (heat, fields.at[3]),
            (soot, fields.at[4]),
            (label, labels),
        ],
        sems,
    )
    odd = lax.axis_index("tun") % 2
    high = depth - 2
    start_a = jnp.where(odd == 1, 0, high)
    start_b = high - start_a
    for copy in pending[1:]:
        copy.wait()
    for start, msg in ((start_a, msg_a), (start_b, msg_b)):
        for f in range(NF):
            msg[f] = fields[f, pl.ds(start, 2)]
        msg[NF] = labels[pl.ds(start, 2)].astype(F32)
        msg[NF + 1] = counts[pl.ds(start, 2)].astype(F32)
    pending[0].wait()
    for x in range(depth):
        total[x] = live_sum(masses[:, x], counts[x])
    for start, msg in ((start_a, msg_a), (start_b, msg_b)):
        msg[NF + 2] = total[pl.ds(start, 2)]


def pack_tun(wind, heat, soot, mass, count, label):
    block = heat.shape
    msg = jax.ShapeDtypeStruct((NF + 3, 2) + block[1:], F32)
    return pl.pallas_call(
        pack_tun_kernel,
        out_shape=(msg, msg, jax.ShapeDtypeStruct(block, F32)),
        in_specs=[ANY] * 6,
        out_specs=(VMEM,) * 3,
        scratch_shapes=[
            pltpu.VMEM((NF,) + block, F32),
            pltpu.VMEM(mass.shape, F32),
            pltpu.VMEM(block, jnp.int32),
            pltpu.VMEM(block, jnp.int32),
            pltpu.SemaphoreType.DMA((6,)),
        ],
        name="pack_tun",
    )(wind, heat, soot, mass, count, label)


def onset_of(label, onset):
    first = jnp.full(label.shape, 1 << 20, jnp.int32)
    for z in range(onset.shape[0]):
        first = jnp.where(label == z + 1, onset[z], first)
    return first


def pack_sec_kernel(onset, wind, heat, soot, count, label, total, got_a, got_b, to_low, to_high, up, down):
    depth, rows = heat.shape[0], heat.shape[1]
    odd = lax.axis_index("tun") % 2 == 1
    for n in range(NF + 3):
        up[n] = jnp.where(odd, got_a[n], got_b[n])
        down[n] = jnp.where(odd, got_b[n], got_a[n])
    fields = [wind.at[0], wind.at[1], wind.at[2], heat, soot]
    for msg, first, second in ((to_low, 0, 1), (to_high, rows - 1, rows - 2)):
        for f in range(NF):
            for n, row in ((f, first), (NF + f, second)):
                msg[n, 0:2, :] = up[f, :, row, :]
                msg[n, 2 : 2 + depth, :] = fields[f][:, row, :]
                msg[n, 2 + depth : 4 + depth, :] = down[f, :, row, :]
        counts = count[:, first, :].astype(F32)
        sums = total[:, first, :]
        counts = jnp.concatenate([up[NF + 1, 1, first : first + 1, :], counts[: depth - 1]], axis=0)
        sums = jnp.concatenate([up[NF + 2, 1, first : first + 1, :], sums[: depth - 1]], axis=0)
        sprays = onset_of(label[:, first, :], onset) <= 0
        msg[2 * NF, 2 : 2 + depth, :] = sums + jnp.where(sprays, inject_rate * counts, 0.0)


def pack_sec(onset, wind, heat, soot, count, label, total, got_a, got_b):
    depth, rows, lanes = heat.shape
    msg = jax.ShapeDtypeStruct((2 * NF + 1, depth + 4, lanes), F32)
    halo = jax.ShapeDtypeStruct(got_a.shape, F32)
    return pl.pallas_call(
        pack_sec_kernel,
        out_shape=(msg, msg, halo, halo),
        in_specs=[SMEM] + [VMEM] * 8,
        out_specs=(VMEM,) * 4,
        name="pack_sec",
    )(onset, wind, heat, soot, count, label, total, got_a, got_b)


def pack_mass_kernel(mass, after, msg, sem):
    depth = mass.shape[1]
    copy = pltpu.make_async_copy(mass.at[:, depth - 2 : depth], msg, sem)
    copy.start()
    copy.wait()


def pack_mass(mass, after):
    return pl.pallas_call(
        pack_mass_kernel,
        out_shape=jax.ShapeDtypeStruct((mass.shape[0], 2) + mass.shape[2:], F32),
        in_specs=[ANY, ANY],
        out_specs=VMEM,
        scratch_shapes=[pltpu.SemaphoreType.DMA(())],
        name="pack_mass",
    )(mass, after)


def viscosity(heat):
    return visc_base * (1.0 + 0.5 * jnp.tanh(heat))


def stencil(centre, nu, sides, nu_sides):
    lane = lax.broadcasted_iota(jnp.int32, nu.shape, 1)
    last = nu.shape[1] - 1
    rest = None
    weights = []
    for d in range(3):
        for side, sign in ((0, -1.0), (1, 1.0)):
            weight = (0.5 * time_step) * ((nu + nu_sides[d][side]) - sign * centre[d])
            rest = weight if rest is None else rest + weight
            if d == 2:
                weight = jnp.where(lane == (last if side else 0), 0.0, weight)
            weights.append(weight)
    rest = 1.0 - rest
    out = []
    for f in range(NF):
        value = rest * centre[f]
        for d in range(3):
            for side in (0, 1):
                value = value + weights[2 * d + side] * sides[d][side](f)
        out.append(value)
    out[0] = out[0] + (time_step * drag_rate) * (vent_speed - centre[0])
    out[2] = out[2] + (time_step * buoyancy) * centre[3]
    return out


def around(plane):
    return pltpu.roll(plane, 1, 1), pltpu.roll(plane, plane.shape[1] - 1, 1)


def nu_around(nu):
    lane = lax.broadcasted_iota(jnp.int32, nu.shape, 1)
    low, high = around(nu)
    return jnp.where(lane == 0, visc_base, low), jnp.where(lane == nu.shape[1] - 1, visc_base, high)


def tail_kernel(
    onset, wind, heat, soot, mass, count, label, total, up, down, to_low, to_high, low, high, above,
    wind_out, heat_out, soot_out, mass_out, count_out,
    ext, ext_nu, nxt, nxt_nu, damp, loads, fields, masses, counts, sems,
):
    depth, rows, lanes = heat.shape
    slots = mass.shape[0]
    tun, sec = lax.axis_index("tun"), lax.axis_index("sec")
    inside_up, inside_down = tun > 0, tun < lax.axis_size("tun") - 1
    inside_low, inside_high = sec > 0, sec < lax.axis_size("sec") - 1
    body = slice(ROW, ROW + rows)
    own = [wind.at[0], wind.at[1], wind.at[2], heat, soot]

    for f in range(NF):
        for x in range(depth + 4):
            if x < 2:
                plane = up[f, x]
            elif x < depth + 2:
                plane = own[f][x - 2]
            else:
                plane = down[f, x - depth - 2]
            ext[f, x, body, :] = plane
            if f == 3:
                ext_nu[x, body, :] = viscosity(plane)
        for x in range(1, depth + 3):
            ext[f, x, ROW - 1 : ROW, :] = low[f, x : x + 1, :]
            ext[f, x, ROW + rows : ROW + rows + 1, :] = high[f, x : x + 1, :]
    nu_low, nu_high = viscosity(low[3]), viscosity(high[3])
    for x in range(1, depth + 3):
        ext_nu[x, ROW - 1 : ROW, :] = nu_low[x : x + 1, :]
        ext_nu[x, ROW + rows : ROW + rows + 1, :] = nu_high[x : x + 1, :]

    def first(x):
        return onset_of(label[x], onset)

    for x in range(-1, depth + 1):
        centre = [ext[f, x + 2, body, :] for f in range(NF)]
        nu = ext_nu[x + 2, body, :]
        lifted = [around(c) for c in centre]
        sides = [
            (lambda f: ext[f, x + 1, body, :], lambda f: ext[f, x + 3, body, :]),
            (lambda f: ext[f, x + 2, ROW - 1 : ROW + rows - 1, :], lambda f: ext[f, x + 2, ROW + 1 : ROW + rows + 1, :]),
            (lambda f: lifted[f][0], lambda f: lifted[f][1]),
        ]
        nu_sides = [
            (ext_nu[x + 1, body, :], ext_nu[x + 3, body, :]),
            (ext_nu[x + 2, ROW - 1 : ROW + rows - 1, :], ext_nu[x + 2, ROW + 1 : ROW + rows + 1, :]),
            nu_around(nu),
        ]
        new = stencil(centre, nu, sides, nu_sides)
        if x < 1:
            moved_total, moved_count = up[NF + 2, x + 1], up[NF + 1, x + 1]
        else:
            moved_total, moved_count = total[x - 1], count[x - 1].astype(F32)
        if x < 0:
            zone = up[NF, 1].astype(jnp.int32)
        elif x < depth:
            zone = label[x]
        else:
            zone = down[NF, 0].astype(jnp.int32)
        sprays = jnp.where(onset_of(zone, onset) <= 0, inject_rate, 0.0)
        load = moved_total + sprays * moved_count
        evap = evap_rate * jax.nn.sigmoid(new[3])
        new[3] = new[3] - latent_heat * (evap * load)
        new[4] = new[4] / (1.0 + scavenge * load)
        if x < depth:
            damp[0, x + 1] = 1.0 - evap
            damp[1, x + 1] = sprays * (1.0 - evap)
            loads[x + 1] = load * (1.0 - evap)
        keep = inside_up if x < 0 else inside_down if x == depth else None
        for f in range(NF):
            value = new[f] if keep is None else jnp.where(keep, new[f], 0.0)
            nxt[f, x + 1, body, :] = value
            if f == 3:
                nxt_nu[x + 1, body, :] = viscosity(value)

    for got, sent, row, flip, keep in ((low, to_low, ROW - 1, False, inside_low), (high, to_high, ROW + rows, True, inside_high)):
        here = slice(2, 2 + depth)
        centre = [got[f, here, :] for f in range(NF)]
        nu_all = nu_high if flip else nu_low
        nu = nu_all[2 : 2 + depth]
        lifted = [around(c) for c in centre]
        inner = lambda f, sent=sent: sent[f, here, :]
        outer = lambda f, got=got: got[NF + f, here, :]
        nu_inner, nu_outer = viscosity(sent[3, here, :]), viscosity(got[NF + 3, here, :])
        sides = [
            (lambda f, got=got: got[f, 1 : 1 + depth, :], lambda f, got=got: got[f, 3 : 3 + depth, :]),
            (inner, outer) if flip else (outer, inner),
            (lambda f: lifted[f][0], lambda f: lifted[f][1]),
        ]
        nu_sides = [
            (viscosity(got[3, 1 : 1 + depth, :]), viscosity(got[3, 3 : 3 + depth, :])),
            (nu_inner, nu_outer) if flip else (nu_outer, nu_inner),
            nu_around(nu),
        ]
        new = stencil(centre, nu, sides, nu_sides)
        load = got[2 * NF, here, :]
        evap = evap_rate * jax.nn.sigmoid(new[3])
        new[3] = new[3] - latent_heat * (evap * load)
        new[4] = new[4] / (1.0 + scavenge * load)
        for f in range(NF):
            value = jnp.where(keep, new[f], 0.0)
            for x in range(depth):
                nxt[f, x + 1, row : row + 1, :] = value[x : x + 1]
            if f == 3:
                value = viscosity(value)
                for x in range(depth):
                    nxt_nu[x + 1, row : row + 1, :] = value[x : x + 1]

    pending = []
    for x in range(depth):
        centre = [nxt[f, x + 1, body, :] for f in range(NF)]
        nu = nxt_nu[x + 1, body, :]
        lifted = [around(c) for c in centre]
        sides = [
            (lambda f: nxt[f, x, body, :], lambda f: nxt[f, x + 2, body, :]),
            (lambda f: nxt[f, x + 1, ROW - 1 : ROW + rows - 1, :], lambda f: nxt[f, x + 1, ROW + 1 : ROW + rows + 1, :]),
            (lambda f: lifted[f][0], lambda f: lifted[f][1]),
        ]
        nu_sides = [
            (nxt_nu[x, body, :], nxt_nu[x + 2, body, :]),
            (nxt_nu[x + 1, ROW - 1 : ROW + rows - 1, :], nxt_nu[x + 1, ROW + 1 : ROW + rows + 1, :]),
            nu_around(nu),
        ]
        new = stencil(centre, nu, sides, nu_sides)
        moved = up[NF + 1, x].astype(jnp.int32) if x < 2 else count[x - 2]
        sprays = jnp.where(first(x) <= 1, inject_rate, 0.0)
        load = loads[x] + sprays * moved.astype(F32)
        evap = evap_rate * jax.nn.sigmoid(new[3])
        new[3] = new[3] - latent_heat * (evap * load)
        new[4] = new[4] / (1.0 + scavenge * load)
        for f in range(NF):
            fields[f, x] = new[f]
        counts[x] = moved
        scale = damp[0, x] * (1.0 - evap)
        gain = (damp[1, x] + sprays) * (1.0 - evap)
        for k in range(slots):
            before = above[k, x] if x < 2 else mass[k, x - 2]
            masses[k, x] = jnp.where(moved > k, before * scale + gain, before)
    pending = copies(
        [
            (masses, mass_out),
            (fields.at[0:3], wind_out),
            (fields.at[3], heat_out),
            (fields.at[4], soot_out),
            (counts, count_out),
        ],
        sems,
    )
    for copy in pending:
        copy.wait()


def tail(onset, wind, heat, soot, mass, count, label, total, up, down, to_low, to_high, low, high, above):
    depth, rows, lanes = heat.shape
    tall = rows + 2 * ROW
    return pl.pallas_call(
        tail_kernel,
        out_shape=(
            jax.ShapeDtypeStruct(wind.shape, F32),
            jax.ShapeDtypeStruct(heat.shape, F32),
            jax.ShapeDtypeStruct(heat.shape, F32),
            jax.ShapeDtypeStruct(mass.shape, F32),
            jax.ShapeDtypeStruct(heat.shape, jnp.int32),
        ),
        in_specs=[SMEM] + [VMEM] * 14,
        out_specs=(ANY,) * 5,
        scratch_shapes=[
            pltpu.VMEM((NF, depth + 4, tall, lanes), F32),
            pltpu.VMEM((depth + 4, tall, lanes), F32),
            pltpu.VMEM((NF, depth + 2, tall, lanes), F32),
            pltpu.VMEM((depth + 2, tall, lanes), F32),
            pltpu.VMEM((2, depth + 1, rows, lanes), F32),
            pltpu.VMEM((depth + 1, rows, lanes), F32),
            pltpu.VMEM((NF, depth, rows, lanes), F32),
            pltpu.VMEM(mass.shape, F32),
            pltpu.VMEM((depth, rows, lanes), jnp.int32),
            pltpu.SemaphoreType.DMA((5,)),
        ],
        name="tail",
    )(onset, wind, heat, soot, mass, count, label, total, up, down, to_low, to_high, low, high, above)


def local(wind, heat, soot, mass, count, label, onset):
    chain, width = lax.axis_size("tun"), lax.axis_size("sec")
    pairs_a = [(i, i ^ 1) for i in range(chain)]
    pairs_b = [(i, ((i + 1) ^ 1) - 1) for i in range(1, chain - 1)]
    msg_a, msg_b, total = pack_tun(wind, heat, soot, mass, count, label)
    got_a = lax.ppermute(msg_a, "tun", pairs_a)
    got_b = lax.ppermute(msg_b, "tun", pairs_b)
    to_low, to_high, up, down = pack_sec(onset, wind, heat, soot, count, label, total, got_a, got_b)
    low = lax.ppermute(to_high, "sec", [(i, i + 1) for i in range(width - 1)])
    high = lax.ppermute(to_low, "sec", [(i + 1, i) for i in range(width - 1)])
    above = lax.ppermute(pack_mass(mass, up), "tun", [(i, i + 1) for i in range(chain - 1)])
    return tail(onset, wind, heat, soot, mass, count, label, total, up, down, to_low, to_high, low, high, above)


def solution(mesh):
    return jax.shard_map(
        local,
        mesh=mesh,
        in_specs=(
            P(None, "tun", "sec", None),
            P("tun", "sec", None),
            P("tun", "sec", None),
            P(None, "tun", "sec", None),
            P("tun", "sec", None),
            P("tun", "sec", None),
            P(),
        ),
        out_specs=(
            P(None, "tun", "sec", None),
            P("tun", "sec", None),
            P("tun", "sec", None),
            P(None, "tun", "sec", None),
            P("tun", "sec", None),
        ),
        check_vma=False,
    )
```

time: 152 us -> 46.5 us (0.31)
  the two profiles are of different devices: /device:TPU:32 before, /device:TPU:414 now
where the time goes in v1:
time: 46.5 us; the launch traced here: 46.2 us
  starting transfers between devices  18 us (39%)
  waiting for transfers between devices  16.2 us (35%)
  Pallas kernels  9.76 us (21%)
  local copies, waits for them, and re-layouts  1.4 us (3%)
  between operations  0.74 us (2%)
    ppermute x1, waiting for transfers between devices, local(): low = lax.ppermute(to_high, 'sec', [(i, i + 1) for i in range(width - 1)])  7.75 us
    ppermute x1, starting transfers between devices, local(): lax.ppermute(pack_mass(mass, up), 'tun', [(i, i + 1) for i in range(chain...  6.62 us
    ppermute x1, starting transfers between devices, local(): high = lax.ppermute(to_low, 'sec', [(i + 1, i) for i in range(width - 1)])  5.46 us
    ppermute x1, waiting for transfers between devices, local(): high = lax.ppermute(to_low, 'sec', [(i + 1, i) for i in range(width - 1)])  4.78 us
    pallas_call x1, Pallas kernels, tail(): pl.pallas_call(tail_kernel, out_shape=(jax.ShapeDtypeStruct(wind.shape, F...  3.88 us
    ppermute x1, waiting for transfers between devices, local(): got_b = lax.ppermute(msg_b, 'tun', pairs_b)  3.71 us
    ppermute x1, starting transfers between devices, local(): got_b = lax.ppermute(msg_b, 'tun', pairs_b)  2.75 us
    pallas_call x1, Pallas kernels, pack_tun(): pl.pallas_call(pack_tun_kernel, out_shape=(msg, msg, jax.ShapeDtypeStruct...  2.12 us
  transfers between devices with their start and end apart: 5, of which 3 were waited for; matrix products, arithmetic and copies ran while one was open for 0% of the time, Pallas kernels for 0%

profile of v1, /device:TPU:414, one launch (start us, length us, event | category | flops | bytes accessed | tf_op | source)
XLA Modules:
  0.0 46.2 jit_solution(16522892641222004293)
XLA Ops:
  0.6 2.1 %pack_tun.1 = (f32[8,2,16,128]{3,2,1,0:T(8,128)}, f32[8,2,16,128]{3,2,1,0:T(8,128)}, f32[8,16,128]{2,1,0:T(8,128)}) custom-call(f32[3,8,16,128]{3,2,1,0:T(8,128)} %wind.5, f32[8,16,128]{2,1,0:T(8,128)} %heat.5, f32[8,16,128]{2,1,0:T(8,128)} %soot.5, f32[16,8,16,128]{3,2,1,0:T(8,128)} %mass.5, s32[8,16,128]{2,1,0:T(8,128)} %count.5, s32[8,16,128]{2,1,0:T(8,128)} %label.5), custom_call_target="tpu_custom_call" | custom-call | tf_op jit(solution)/shard_map/pack_tun/pallas_call | solution.py:76
  2.8 1.9 %collective-permute-start = (f32[8,2,16,128]{3,2,1,0:T(8,128)}, f32[8,2,16,128]{3,2,1,0:T(8,128)S(1)}, u32[]{:S(2)}, u32[]{:S(2)}) collective-permute-start(f32[8,2,16,128]{3,2,1,0:T(8,128)} %get-tuple-element.13), channel_id=1, source_target_pairs={{0,4},{4,0},{8,12},{12,8},{16,20},{20,16},{24,28},{28,24},{32,36},... | collective-permute-start | bytes 393224 | tf_op jit(solution)/shard_map/ppermute | solution.py:378
  4.7 2.8 %collective-permute-start.1 = (f32[8,2,16,128]{3,2,1,0:T(8,128)}, f32[8,2,16,128]{3,2,1,0:T(8,128)S(1)}, u32[]{:S(2)}, u32[]{:S(2)}) collective-permute-start(f32[8,2,16,128]{3,2,1,0:T(8,128)} %get-tuple-element.14), channel_id=1, source_target_pairs={{4,8},{8,4},{12,16},{16,12},{20,24},{24,20},{28,32},{32,28},{36,40... | collective-permute-start | bytes 393224 | tf_op jit(solution)/shard_map/ppermute | solution.py:379
  7.4 0.0 collective-permute-done.got_a
  7.5 0.0 copy-start.1
  7.5 3.7 %collective-permute-done.1.got_b = f32[8,2,16,128]{3,2,1,0:T(8,128)S(1)} collective-permute-done((f32[8,2,16,128]{3,2,1,0:T(8,128)}, f32[8,2,16,128]{3,2,1,0:T(8,128)S(1)}, u32[]{:S(2)}, u32[]{:S(2)}) %collective-permute-start.1) | collective-permute-done | bytes 131104 | tf_op jit(solution)/shard_map/ppermute | solution.py:379
  11.2 0.0 copy-start.2
  11.2 0.0 copy-done.1
  11.2 0.7 %copy-done.2 = f32[8,2,16,128]{3,2,1,0:T(8,128)} copy-done((f32[8,2,16,128]{3,2,1,0:T(8,128)}, f32[8,2,16,128]{3,2,1,0:T(8,128)S(1)}, u32[]{:S(2)}) %copy-start.2) | copy-done | bytes 131096
  11.8 2.1 %pack_sec.1 = (f32[11,12,128]{2,1,0:T(8,128)}, f32[11,12,128]{2,1,0:T(8,128)}, f32[8,2,16,128]{3,2,1,0:T(8,128)}, f32[8,2,16,128]{3,2,1,0:T(8,128)}) custom-call(s32[8]{0:T(128)} %onset.3, f32[3,8,16,128]{3,2,1,0:T(8,128)} %wind.5, f32[8,16,128]{2,1,0:T(8,128)} %heat.5, f32[8,16,128]{2,1,0:T(8,128)} %soot.5, s32[8,16,128]{2,1,0:T(8,128)} %count.5, ...), custom_call_target="tpu_custom_call" | custom-call | tf_op jit(solution)/shard_map/pack_sec/pallas_call | solution.py:124
  13.9 0.0 copy-start.3
  13.9 0.0 copy-start.4
  13.9 1.7 %pack_mass.1 = f32[16,2,16,128]{3,2,1,0:T(8,128)} custom-call(f32[16,8,16,128]{3,2,1,0:T(8,128)} %mass.5, f32[8,2,16,128]{3,2,1,0:T(8,128)} %get-tuple-element.15.after.up), custom_call_target="tpu_custom_call" | custom-call | tf_op jit(solution)/shard_map/pack_mass/pallas_call | solution.py:141
  15.6 6.6 %collective-permute-start.4 = (f32[16,2,16,128]{3,2,1,0:T(8,128)}, f32[16,2,16,128]{3,2,1,0:T(8,128)S(1)}, u32[]{:S(2)}, u32[]{:S(2)}) collective-permute-start(f32[16,2,16,128]{3,2,1,0:T(8,128)} %pack_mass.1), channel_id=1, source_target_pairs={{0,4},{4,8},{8,12},{12,16},{16,20},{20,24},{24,28},{28,32},{32,36}... | collective-permute-start | bytes 786440 | tf_op jit(solution)/shard_map/ppermute | solution.py:383
  22.3 0.0 copy-done.3
  22.3 5.5 %collective-permute-start.3 = (f32[11,12,128]{2,1,0:T(8,128)S(1)}, f32[11,12,128]{2,1,0:T(8,128)S(1)}, u32[]{:S(2)}, u32[]{:S(2)}) collective-permute-start(f32[11,12,128]{2,1,0:T(8,128)S(1)} %copy-done.3), channel_id=1, source_target_pairs={{1,0},{2,1},{3,2},{5,4},{6,5},{7,6},{9,8},{10,9},{11,10},{13,12},{... | collective-permute-start | bytes 202760 | tf_op jit(solution)/shard_map/ppermute | solution.py:382
  27.7 0.0 copy-done.4
  27.7 1.3 %collective-permute-start.2 = (f32[11,12,128]{2,1,0:T(8,128)S(1)}, f32[11,12,128]{2,1,0:T(8,128)S(1)}, u32[]{:S(2)}, u32[]{:S(2)}) collective-permute-start(f32[11,12,128]{2,1,0:T(8,128)S(1)} %copy-done.4), channel_id=1, source_target_pairs={{0,1},{1,2},{2,3},{4,5},{5,6},{6,7},{8,9},{9,10},{10,11},{12,13},{... | collective-permute-start | bytes 202760 | tf_op jit(solution)/shard_map/ppermute | solution.py:381
  29.0 4.8 %collective-permute-done.3.high = f32[11,12,128]{2,1,0:T(8,128)S(1)} collective-permute-done((f32[11,12,128]{2,1,0:T(8,128)S(1)}, f32[11,12,128]{2,1,0:T(8,128)S(1)}, u32[]{:S(2)}, u32[]{:S(2)}) %collective-permute-start.3) | collective-permute-done | bytes 67616 | tf_op jit(solution)/shard_map/ppermute | solution.py:382
  33.8 0.0 copy-start.5
  33.8 7.7 %collective-permute-done.2.low = f32[11,12,128]{2,1,0:T(8,128)S(1)} collective-permute-done((f32[11,12,128]{2,1,0:T(8,128)S(1)}, f32[11,12,128]{2,1,0:T(8,128)S(1)}, u32[]{:S(2)}, u32[]{:S(2)}) %collective-permute-start.2) | collective-permute-done | bytes 67616 | tf_op jit(solution)/shard_map/ppermute | solution.py:381
  41.6 0.0 copy-start.6
  41.6 0.0 collective-permute-done.4.above
  41.6 0.0 copy-start
  41.6 0.0 copy-done.5
  41.6 0.6 %copy-done.6 = f32[11,12,128]{2,1,0:T(8,128)} copy-done((f32[11,12,128]{2,1,0:T(8,128)}, f32[11,12,128]{2,1,0:T(8,128)S(1)}, u32[]{:S(2)}) %copy-start.6) | copy-done | bytes 67608
  42.2 0.1 copy-done
  42.3 3.9 %tail.1 = (f32[3,8,16,128]{3,2,1,0:T(8,128)}, f32[8,16,128]{2,1,0:T(8,128)}, f32[8,16,128]{2,1,0:T(8,128)}, f32[16,8,16,128]{3,2,1,0:T(8,128)}, s32[8,16,128]{2,1,0:T(8,128)}) custom-call(s32[8]{0:T(128)} %onset.3, f32[3,8,16,128]{3,2,1,0:T(8,128)} %wind.5, f32[8,16,128]{2,1,0:T(8,128)} %heat.5, f32[8,16,128]{2,1,0:T(8,128)} %soot.5, ...), custom_call_target="tpu_custom_call" | custom-call | tf_op jit(solution)/shard_map/tail/pallas_call | solution.py:346
Async XLA Ops:
  2.8 4.7 %collective-permute-start = (f32[8,2,16,128]{3,2,1,0:T(8,128)}, f32[8,2,16,128]{3,2,1,0:T(8,128)S(1)}, u32[]{:S(2)}, u32[]{:S(2)}) collective-permute-start(f32[8,2,16,128]{3,2,1,0:T(8,128)} %get-tuple-element.13), channel_id=1, source_target_pairs={{0,4},{4,0},{8,12},{12,8},{16,20},{20,16},{24,28},{28,24},{32,36},... | collective-permute-start | bytes 393224 | tf_op jit(solution)/shard_map/ppermute | solution.py:378
  4.7 6.5 %collective-permute-start.1 = (f32[8,2,16,128]{3,2,1,0:T(8,128)}, f32[8,2,16,128]{3,2,1,0:T(8,128)S(1)}, u32[]{:S(2)}, u32[]{:S(2)}) collective-permute-start(f32[8,2,16,128]{3,2,1,0:T(8,128)} %get-tuple-element.14), channel_id=1, source_target_pairs={{4,8},{8,4},{12,16},{16,12},{20,24},{24,20},{28,32},{32,28},{36,40... | collective-permute-start | bytes 393224 | tf_op jit(solution)/shard_map/ppermute | solution.py:379
  7.5 3.7 %copy-start.1 = (f32[8,2,16,128]{3,2,1,0:T(8,128)}, f32[8,2,16,128]{3,2,1,0:T(8,128)S(1)}, u32[]{:S(2)}) copy-start(f32[8,2,16,128]{3,2,1,0:T(8,128)S(1)} %collective-permute-done.got_a) | copy-start | bytes 393220
  11.2 0.7 %copy-start.2 = (f32[8,2,16,128]{3,2,1,0:T(8,128)}, f32[8,2,16,128]{3,2,1,0:T(8,128)S(1)}, u32[]{:S(2)}) copy-start(f32[8,2,16,128]{3,2,1,0:T(8,128)S(1)} %collective-permute-done.1.got_b) | copy-start | bytes 393220
  13.9 8.4 %copy-start.3 = (f32[11,12,128]{2,1,0:T(8,128)S(1)}, f32[11,12,128]{2,1,0:T(8,128)}, u32[]{:S(2)}) copy-start(f32[11,12,128]{2,1,0:T(8,128)} %get-tuple-element.17.to_low) | copy-start | bytes 202756
  13.9 13.8 %copy-start.4 = (f32[11,12,128]{2,1,0:T(8,128)S(1)}, f32[11,12,128]{2,1,0:T(8,128)}, u32[]{:S(2)}) copy-start(f32[11,12,128]{2,1,0:T(8,128)} %get-tuple-element.18.to_high) | copy-start | bytes 202756
  15.6 26.0 %collective-permute-start.4 = (f32[16,2,16,128]{3,2,1,0:T(8,128)}, f32[16,2,16,128]{3,2,1,0:T(8,128)S(1)}, u32[]{:S(2)}, u32[]{:S(2)}) collective-permute-start(f32[16,2,16,128]{3,2,1,0:T(8,128)} %pack_mass.1), channel_id=1, source_target_pairs={{0,4},{4,8},{8,12},{12,16},{16,20},{20,24},{24,28},{28,32},{32,36}... | collective-permute-start | bytes 786440 | tf_op jit(solution)/shard_map/ppermute | solution.py:383
  22.3 11.6 %collective-permute-start.3 = (f32[11,12,128]{2,1,0:T(8,128)S(1)}, f32[11,12,128]{2,1,0:T(8,128)S(1)}, u32[]{:S(2)}, u32[]{:S(2)}) collective-permute-start(f32[11,12,128]{2,1,0:T(8,128)S(1)} %copy-done.3), channel_id=1, source_target_pairs={{1,0},{2,1},{3,2},{5,4},{6,5},{7,6},{9,8},{10,9},{11,10},{13,12},{... | collective-permute-start | bytes 202760 | tf_op jit(solution)/shard_map/ppermute | solution.py:382
  27.7 13.8 %collective-permute-start.2 = (f32[11,12,128]{2,1,0:T(8,128)S(1)}, f32[11,12,128]{2,1,0:T(8,128)S(1)}, u32[]{:S(2)}, u32[]{:S(2)}) collective-permute-start(f32[11,12,128]{2,1,0:T(8,128)S(1)} %copy-done.4), channel_id=1, source_target_pairs={{0,1},{1,2},{2,3},{4,5},{5,6},{6,7},{8,9},{9,10},{10,11},{12,13},{... | collective-permute-start | bytes 202760 | tf_op jit(solution)/shard_map/ppermute | solution.py:381
  33.8 7.8 %copy-start.5 = (f32[11,12,128]{2,1,0:T(8,128)}, f32[11,12,128]{2,1,0:T(8,128)S(1)}, u32[]{:S(2)}) copy-start(f32[11,12,128]{2,1,0:T(8,128)S(1)} %collective-permute-done.3.high) | copy-start | bytes 202756
  41.6 0.7 %copy-start.6 = (f32[11,12,128]{2,1,0:T(8,128)}, f32[11,12,128]{2,1,0:T(8,128)S(1)}, u32[]{:S(2)}) copy-start(f32[11,12,128]{2,1,0:T(8,128)S(1)} %collective-permute-done.2.low) | copy-start | bytes 202756
  41.6 0.7 %copy-start = (f32[16,2,16,128]{3,2,1,0:T(8,128)}, f32[16,2,16,128]{3,2,1,0:T(8,128)S(1)}, u32[]{:S(2)}) copy-start(f32[16,2,16,128]{3,2,1,0:T(8,128)S(1)} %collective-permute-done.4.above) | copy-start | bytes 786436

commit v2 on v0

v2 whole, which is shorter than its diff:
```python
import jax
import jax.numpy as jnp
from jax import lax
from jax.experimental import pallas as pl
from jax.experimental.pallas import tpu as pltpu
from jax.sharding import PartitionSpec as P

visc_base = 0.2
time_step = 0.1
buoyancy = 0.5
drag_rate = 0.3
vent_speed = 1.0
inject_rate = 0.5
evap_rate = 0.4
latent_heat = 0.5
scavenge = 0.3

NF = 5
F32 = jnp.float32
VMEM = pl.BlockSpec(memory_space=pltpu.VMEM)
SMEM = pl.BlockSpec(memory_space=pltpu.SMEM)
HBM = pl.BlockSpec(memory_space=pltpu.HBM)
ANY = pl.BlockSpec(memory_space=pl.ANY)
ROW = 8


FIRST_COST, LAST_COST = 0, 100


def cost(units):
    return pl.CostEstimate(flops=int(units * 1e9), transcendentals=0, bytes_accessed=int(units * 1e6))


LIMIT = pltpu.CompilerParams(vmem_limit_bytes=12 << 20)


def on_chip(*arrays):
    return tuple(pltpu.with_memory_space_constraint(a, pltpu.VMEM) for a in arrays)


def copies(pairs, sems):
    started = []
    for n, (src, dst) in enumerate(pairs):
        copy = pltpu.make_async_copy(src, dst, sems.at[n])
        copy.start()
        started.append(copy)
    return started

def live_sum(mass, count):
    total = jnp.zeros(count.shape, F32)
    for k in range(len(mass)):
        total = total + jnp.where(count > k, mass[k], 0.0)
    return total


def onset_of(label, onset):
    first = jnp.full(label.shape, 1 << 20, jnp.int32)
    for z in range(onset.shape[0]):
        first = jnp.where(label == z + 1, onset[z], first)
    return first


def pack_tun_kernel(
    onset, wind, heat, soot, mass, count, label, msg_b, msg_a, masses, counts, labels, onsets, sems
):
    depth = heat.shape[0]
    odd = lax.axis_index("tun") % 2 == 1
    top = depth - 2
    start_a = jnp.where(odd, 0, top)
    start_b = top - start_a
    pairs = [(onset, onsets), (mass.at[:, top:depth], masses), (count.at[top:depth], counts)]
    for n, (start, msg) in enumerate(((start_b, msg_b), (start_a, msg_a))):
        here = pl.ds(start, 2)
        pairs += [
            (label.at[here], labels.at[n]),
            (wind.at[:, here], msg.at[0:3]),
            (heat.at[here], msg.at[3]),
            (soot.at[here], msg.at[4]),
        ]
    for copy in copies(pairs, sems):
        copy.wait()
    held = counts[...]
    total = live_sum([masses[k] for k in range(masses.shape[0])], held)
    for n, msg in enumerate((msg_b, msg_a)):
        msg[NF] = onset_of(labels[n], onsets).astype(F32)
        msg[NF + 1] = held.astype(F32)
        msg[NF + 2] = total


def in_hbm(*arrays):
    return tuple(pltpu.with_memory_space_constraint(a, pltpu.HBM) for a in arrays)


def pack_tun(onset, wind, heat, soot, mass, count, label):
    plane = heat.shape[1:]
    msg = pltpu.VMEM((NF + 3, 2) + plane, F32)
    return pl.pallas_call(
        pack_tun_kernel,
        out_shape=(msg, msg),
        in_specs=[HBM] * 7,
        out_specs=(VMEM,) * 2,
        scratch_shapes=[
            pltpu.VMEM((mass.shape[0], 2) + plane, F32),
            pltpu.VMEM((2,) + plane, jnp.int32),
            pltpu.VMEM((2, 2) + plane, jnp.int32),
            pltpu.SMEM(onset.shape, jnp.int32),
            pltpu.SemaphoreType.DMA((11,)),
        ],
        compiler_params=LIMIT,
        name="pack_tun",
    )(*in_hbm(onset, wind, heat, soot, mass, count, label))


def load_kernel(onset, wind, heat, soot, mass, count, label, after, winds, heats, soots, masses, counts, begins, labels, onsets, sems):
    pairs = [
        (onset, onsets), (label, labels), (mass, masses), (wind, winds), (heat, heats), (soot, soots), (count, counts)
    ]
    pending = copies(pairs, sems)
    pending[0].wait()
    pending[1].wait()
    for x in range(label.shape[0]):
        begins[x] = onset_of(labels[x], onsets)
    for copy in pending[2:]:
        copy.wait()


def load(onset, wind, heat, soot, mass, count, label, after):
    arrays = (wind, heat, soot, mass, count, label)
    return pl.pallas_call(
        load_kernel,
        out_shape=tuple(pltpu.VMEM(a.shape, a.dtype) for a in arrays),
        in_specs=[HBM] * 7 + [ANY],
        out_specs=(VMEM,) * 6,
        scratch_shapes=[
            pltpu.VMEM(label.shape, jnp.int32),
            pltpu.SMEM(onset.shape, jnp.int32),
            pltpu.SemaphoreType.DMA((7,)),
        ],
        compiler_params=LIMIT,
        name="load",
    )(*in_hbm(onset, *arrays), after)


def pack_mass_kernel(mass, after, msg):
    depth = mass.shape[1]
    for k in range(mass.shape[0]):
        msg[k] = mass[k, depth - 2 : depth]


def pack_mass(mass, after):
    return pl.pallas_call(
        pack_mass_kernel,
        out_shape=pltpu.VMEM((mass.shape[0], 2) + mass.shape[2:], F32),
        in_specs=[VMEM] * 2,
        out_specs=VMEM,
        compiler_params=LIMIT,
        name="pack_mass",
    )(*on_chip(mass, after))


def pack_sec_kernel(got_b, got_a, wind, heat, soot, mass, count, begins, to_low, to_high):
    depth, rows, lanes = heat.shape
    slots = mass.shape[0]
    odd = lax.axis_index("tun") % 2 == 1

    def flat(ref):
        return ref.reshape(-1, lanes)

    winds, heats, soots, massed = flat(wind), flat(heat), flat(soot), flat(mass)
    counted, begun, from_a, from_b = flat(count), flat(begins), flat(got_a), flat(got_b)

    def own(f, row):
        ref, base = ((winds, f * depth * rows), (heats, 0), (soots, 0))[max(f - 2, 0)]
        return ref[pl.ds(base + row, depth, stride=rows), :]

    def beside(f, row):
        here = pl.ds(f * 2 * rows + row, 2, stride=rows)
        a, b = from_a[here, :], from_b[here, :]
        return jnp.where(odd, a, b), jnp.where(odd, b, a)

    for msg, first, second in ((to_low, 0, 1), (to_high, rows - 1, rows - 2)):
        for f in range(NF):
            for n, row in ((f, first), (NF + f, second)):
                before, after = beside(f, row)
                msg[n] = jnp.concatenate([before, own(f, row), after], axis=0)
        here = pl.ds(first, depth, stride=rows)
        held = counted[here, :]
        sums = live_sum([massed[pl.ds(k * depth * rows + first, depth, stride=rows), :] for k in range(slots)], held)
        begins_up, begins_down = beside(NF, first)
        held_up, _ = beside(NF + 1, first)
        sums_up, _ = beside(NF + 2, first)
        starts = jnp.concatenate([begins_up[1:], begun[here, :].astype(F32), begins_down[:1]], axis=0)
        held = jnp.concatenate([held_up, held.astype(F32)], axis=0)
        sums = jnp.concatenate([sums_up, sums], axis=0)
        msg[2 * NF, 1 : 3 + depth, :] = sums + jnp.where(starts <= 0.0, inject_rate * held, 0.0)


def pack_sec(wind, heat, soot, mass, count, begins, got_a, got_b):
    depth, rows, lanes = heat.shape
    msg = pltpu.VMEM((2 * NF + 1, depth + 4, lanes), F32)
    return pl.pallas_call(
        pack_sec_kernel,
        out_shape=(msg, msg),
        in_specs=[VMEM] * 8,
        out_specs=(VMEM,) * 2,
        compiler_params=LIMIT,
        name="pack_sec",
    )(*on_chip(got_b, got_a, wind, heat, soot, mass, count, begins))


def viscosity(heat):
    return visc_base * (1.0 + 0.5 * jnp.tanh(heat))


def stencil(centre, nu, sides, nu_sides):
    lane = lax.broadcasted_iota(jnp.int32, nu.shape, 1)
    last = nu.shape[1] - 1
    rest = None
    weights = []
    for d in range(3):
        for side, sign in ((0, -1.0), (1, 1.0)):
            weight = (0.5 * time_step) * ((nu + nu_sides[d][side]) - sign * centre[d])
            rest = weight if rest is None else rest + weight
            if d == 2:
                weight = jnp.where(lane == (last if side else 0), 0.0, weight)
            weights.append(weight)
    rest = 1.0 - rest
    out = []
    for f in range(NF):
        value = rest * centre[f]
        for d in range(3):
            for side in (0, 1):
                value = value + weights[2 * d + side] * sides[d][side](f)
        out.append(value)
    out[0] = out[0] + (time_step * drag_rate) * (vent_speed - centre[0])
    out[2] = out[2] + (time_step * buoyancy) * centre[3]
    return out


def around(plane):
    return pltpu.roll(plane, 1, 1), pltpu.roll(plane, plane.shape[1] - 1, 1)


def nu_around(nu):
    lane = lax.broadcasted_iota(jnp.int32, nu.shape, 1)
    low, high = around(nu)
    return jnp.where(lane == 0, visc_base, low), jnp.where(lane == nu.shape[1] - 1, visc_base, high)


def first_kernel(
    wind, heat, soot, mass, count, begins, got_a, got_b, after,
    count_out, nxt, nxt_nu, keep, loads, spray_0, spray_1,
    ext, ext_nu, counts, sems,
):
    depth, rows, lanes = heat.shape
    slots = mass.shape[0]
    tall = rows + 2 * ROW
    tun = lax.axis_index("tun")
    odd = tun % 2 == 1
    own = [wind.at[0], wind.at[1], wind.at[2], heat, soot]

    def beside(n, x):
        return jnp.where(odd, got_a[n, x], got_b[n, x]), jnp.where(odd, got_b[n, x], got_a[n, x])

    def put(ref, plane, value):
        ref[plane * tall + ROW : plane * tall + ROW + rows, :] = value

    def at(ref, plane, shift=0):
        return ref[plane * tall + ROW + shift : plane * tall + ROW + shift + rows, :]

    planes = depth + 4
    for f in range(NF):
        for x in range(depth):
            put(ext, f * planes + x + 2, own[f][x])
        for x in (0, 1):
            before, behind = beside(f, x)
            put(ext, f * planes + x, before)
            put(ext, f * planes + depth + 2 + x, behind)
    for x in range(planes):
        put(ext_nu, x, viscosity(at(ext, 3 * planes + x)))

    for x in (0, 1):
        counts[x] = beside(NF + 1, x)[0].astype(jnp.int32)
    for x in range(depth - 2):
        counts[x + 2] = count[x]
    pending = copies([(counts, count_out)], sems)

    for x in range(-1, depth + 1):
        centre = [at(ext, f * planes + x + 2) for f in range(NF)]
        nu = at(ext_nu, x + 2)
        lifted = [around(c) for c in centre]
        sides = [
            (lambda f: at(ext, f * planes + x + 1), lambda f: at(ext, f * planes + x + 3)),
            (lambda f: at(ext, f * planes + x + 2, -1), lambda f: at(ext, f * planes + x + 2, 1)),
            (lambda f: lifted[f][0], lambda f: lifted[f][1]),
        ]
        nu_sides = [
            (at(ext_nu, x + 1), at(ext_nu, x + 3)),
            (at(ext_nu, x + 2, -1), at(ext_nu, x + 2, 1)),
            nu_around(nu),
        ]
        new = stencil(centre, nu, sides, nu_sides)
        if x < 1:
            moved_total, moved_count = beside(NF + 2, x + 1)[0], beside(NF + 1, x + 1)[0]
        else:
            held = count[x - 1]
            moved_total, moved_count = live_sum([mass[k, x - 1] for k in range(slots)], held), held.astype(F32)
        if x < 0:
            start = beside(NF, 1)[0].astype(jnp.int32)
        elif x < depth:
            start = begins[x]
        else:
            start = beside(NF, 0)[1].astype(jnp.int32)
        sprays = jnp.where(start <= 0, inject_rate, 0.0)
        load = moved_total + sprays * moved_count
        evap = evap_rate * jax.nn.sigmoid(new[3])
        new[3] = new[3] - latent_heat * (evap * load)
        new[4] = new[4] / (1.0 + scavenge * load)
        if x < depth:
            keep[(x + 1) * rows : (x + 2) * rows, :] = 1.0 - evap
            loads[x + 1] = load
            spray_0[x + 1] = sprays
        if 0 <= x < depth:
            spray_1[x] = jnp.where(start <= 1, inject_rate, 0.0)
        inside = tun > 0 if x < 0 else tun < lax.axis_size("tun") - 1 if x == depth else None
        for f in range(NF):
            value = new[f] if inside is None else jnp.where(inside, new[f], 0.0)
            put(nxt, f * (depth + 2) + x + 1, value)
            if f == 3:
                put(nxt_nu, x + 1, viscosity(value))
    for copy in pending:
        copy.wait()


def first(wind, heat, soot, mass, count, begins, got_a, got_b, after):
    depth, rows, lanes = heat.shape
    tall = rows + 2 * ROW
    return pl.pallas_call(
        first_kernel,
        out_shape=(
            jax.ShapeDtypeStruct(count.shape, jnp.int32),
            pltpu.VMEM((NF * (depth + 2) * tall, lanes), F32),
            pltpu.VMEM(((depth + 2) * tall, lanes), F32),
            pltpu.VMEM(((depth + 1) * rows, lanes), F32),
            pltpu.VMEM((depth + 1, rows, lanes), F32),
            pltpu.VMEM((depth + 1, rows, lanes), F32),
            pltpu.VMEM((depth, rows, lanes), F32),
        ),
        in_specs=[VMEM] * 8 + [ANY],
        out_specs=(ANY,) + (VMEM,) * 6,
        scratch_shapes=[
            pltpu.VMEM((NF * (depth + 4) * tall, lanes), F32),
            pltpu.VMEM(((depth + 4) * tall, lanes), F32),
            pltpu.VMEM((depth, rows, lanes), jnp.int32),
            pltpu.SemaphoreType.DMA((1,)),
        ],
        compiler_params=LIMIT,
        cost_estimate=cost(FIRST_COST),
        name="first_substep",
    )(*on_chip(wind, heat, soot, mass, count, begins, got_a, got_b), after)


def last_kernel(
    high, low, to_low, to_high, count, got_a, got_b, loads, spray_0, spray_1, nxt_in, nxt_nu_in, keep_in,
    wind_out, heat_out, soot_out, scale, gain, moved, nxt, nxt_nu, keep,
    fields, sems,
):
    depth, rows, lanes = count.shape
    tall = rows + 2 * ROW
    planes = depth + 2
    tun, sec = lax.axis_index("tun"), lax.axis_index("sec")
    odd = tun % 2 == 1
    inside_up, inside_down = tun > 0, tun < lax.axis_size("tun") - 1
    sides_of = (
        (low, to_low, ROW - 1, 0, sec > 0),
        (high, to_high, ROW + rows, rows - 1, sec < lax.axis_size("sec") - 1),
    )

    place = lax.broadcasted_iota(jnp.int32, (planes, lanes), 0)
    inside = ((place > 0) | inside_up) & ((place < planes - 1) | inside_down)
    mid = slice(1, 1 + planes)
    for flip, (got, sent, outer_row, inner_row, there) in enumerate(sides_of):
        got_nu, sent_nu = viscosity(got[3]), viscosity(sent[3])
        got_nu_2, sent_nu_2 = viscosity(got[NF + 3, mid, :]), viscosity(sent[NF + 3, mid, :])
        for ref, ref_nu, near, near_nu, far, far_nu, row, valid in (
            (got, got_nu, lambda f, sent=sent: sent[f, mid, :], sent_nu[mid], lambda f, got=got: got[NF + f, mid, :], got_nu_2, outer_row, there),
            (sent, sent_nu, lambda f, got=got: got[f, mid, :], got_nu[mid], lambda f, sent=sent: sent[NF + f, mid, :], sent_nu_2, ROW + inner_row, inside),
        ):
            is_outer = ref is got
            centre = [ref[f, mid, :] for f in range(NF)]
            nu = ref_nu[mid]
            lifted = [around(c) for c in centre]
            swap = bool(flip) == is_outer
            sides = [
                (lambda f, ref=ref: ref[f, 0:planes, :], lambda f, ref=ref: ref[f, 2 : 2 + planes, :]),
                (near, far) if swap else (far, near),
                (lambda f: lifted[f][0], lambda f: lifted[f][1]),
            ]
            nu_sides = [
                (ref_nu[0:planes], ref_nu[2 : 2 + planes]),
                (near_nu, far_nu) if swap else (far_nu, near_nu),
                nu_around(nu),
            ]
            new = stencil(centre, nu, sides, nu_sides)
            load = ref[2 * NF, mid, :]
            evap = evap_rate * jax.nn.sigmoid(new[3])
            new[3] = new[3] - latent_heat * (evap * load)
            new[4] = new[4] / (1.0 + scavenge * load)
            for f in range(NF):
                value = jnp.where(valid, new[f], 0.0)
                nxt[pl.ds(f * planes * tall + row, planes, stride=tall), :] = value
                if f == 3:
                    nxt_nu[pl.ds(row, planes, stride=tall), :] = viscosity(value)
            if not is_outer:
                keep[pl.ds(inner_row, depth + 1, stride=rows), :] = (1.0 - evap)[: depth + 1]

    def at(ref, plane, shift=0):
        return ref[plane * tall + ROW + shift : plane * tall + ROW + shift + rows, :]

    for x in range(depth):
        centre = [at(nxt, f * planes + x + 1) for f in range(NF)]
        nu = at(nxt_nu, x + 1)
        lifted = [around(c) for c in centre]
        sides = [
            (lambda f: at(nxt, f * planes + x), lambda f: at(nxt, f * planes + x + 2)),
            (lambda f: at(nxt, f * planes + x + 1, -1), lambda f: at(nxt, f * planes + x + 1, 1)),
            (lambda f: lifted[f][0], lambda f: lifted[f][1]),
        ]
        nu_sides = [
            (at(nxt_nu, x), at(nxt_nu, x + 2)),
            (at(nxt_nu, x + 1, -1), at(nxt_nu, x + 1, 1)),
            nu_around(nu),
        ]
        new = stencil(centre, nu, sides, nu_sides)
        if x < 2:
            held = jnp.where(odd, got_a[NF + 1, x], got_b[NF + 1, x]).astype(jnp.int32)
        else:
            held = count[x - 2]
        kept = keep[x * rows : (x + 1) * rows, :]
        sprays = spray_1[x]
        load = loads[x] * kept + sprays * held.astype(F32)
        evap = evap_rate * jax.nn.sigmoid(new[3])
        new[3] = new[3] - latent_heat * (evap * load)
        new[4] = new[4] / (1.0 + scavenge * load)
        for f in range(NF):
            fields[f, x] = new[f]
        moved[x] = held
        scale[x] = kept * (1.0 - evap)
        gain[x] = (spray_0[x] * kept + sprays) * (1.0 - evap)
    for copy in copies([(fields.at[0:3], wind_out), (fields.at[3], heat_out), (fields.at[4], soot_out)], sems):
        copy.wait()


def last(high, low, to_low, to_high, count, got_a, got_b, loads, spray_0, spray_1, nxt, nxt_nu, keep):
    block = count.shape
    operands = on_chip(high, low, to_low, to_high, count, got_a, got_b, loads, spray_0, spray_1, nxt, nxt_nu, keep)
    return pl.pallas_call(
        last_kernel,
        out_shape=(
            jax.ShapeDtypeStruct((3,) + block, F32),
            jax.ShapeDtypeStruct(block, F32),
            jax.ShapeDtypeStruct(block, F32),
            pltpu.VMEM(block, F32),
            pltpu.VMEM(block, F32),
            pltpu.VMEM(block, jnp.int32),
            pltpu.VMEM(nxt.shape, F32),
            pltpu.VMEM(nxt_nu.shape, F32),
            pltpu.VMEM(keep.shape, F32),
        ),
        in_specs=[VMEM] * 13,
        out_specs=(ANY,) * 3 + (VMEM,) * 6,
        input_output_aliases={10: 6, 11: 7, 12: 8},
        scratch_shapes=[pltpu.VMEM((NF,) + block, F32), pltpu.SemaphoreType.DMA((3,))],
        compiler_params=LIMIT,
        cost_estimate=cost(LAST_COST),
        name="last_substep",
    )(*operands)[:6]


def droplets_kernel(mass, above, scale, gain, moved, mass_out, masses, sems):
    slots, depth = mass.shape[:2]
    pending = []
    for x in range(depth):
        held, by, plus = moved[x], scale[x], gain[x]
        for k in range(slots):
            before = above[k, x] if x < 2 else mass[k, x - 2]
            masses[k, x] = jnp.where(held > k, before * by + plus, before)
        copy = pltpu.make_async_copy(masses.at[:, x], mass_out.at[:, x], sems.at[x])
        copy.start()
        pending.append(copy)
    for copy in pending:
        copy.wait()


def droplets(mass, above, scale, gain, moved):
    return pl.pallas_call(
        droplets_kernel,
        out_shape=jax.ShapeDtypeStruct(mass.shape, F32),
        in_specs=[VMEM] * 5,
        out_specs=ANY,
        scratch_shapes=[pltpu.VMEM(mass.shape, F32), pltpu.SemaphoreType.DMA((mass.shape[1],))],
        compiler_params=LIMIT,
        name="droplets",
    )(*on_chip(mass, above, scale, gain, moved))


def local(wind, heat, soot, mass, count, label, onset):
    chain, width = lax.axis_size("tun"), lax.axis_size("sec")
    pairs_a = [(i, i ^ 1) for i in range(chain)]
    pairs_b = [(i, ((i + 1) ^ 1) - 1) for i in range(1, chain - 1)]
    msg_b, msg_a = pack_tun(onset, wind, heat, soot, mass, count, label)
    wind, heat, soot, mass, count, begins = load(onset, wind, heat, soot, mass, count, label, msg_b)
    got_b = lax.ppermute(msg_b, "tun", pairs_b)
    got_a = lax.ppermute(msg_a, "tun", pairs_a)
    to_low, to_high = pack_sec(wind, heat, soot, mass, count, begins, got_a, got_b)
    high = lax.ppermute(to_low, "sec", [(i + 1, i) for i in range(width - 1)])
    low = lax.ppermute(to_high, "sec", [(i, i + 1) for i in range(width - 1)])
    above = lax.ppermute(pack_mass(mass, to_low), "tun", [(i, i + 1) for i in range(chain - 1)])
    count_out, nxt, nxt_nu, keep, loads, spray_0, spray_1 = first(
        wind, heat, soot, mass, count, begins, got_a, got_b, to_low
    )
    wind_out, heat_out, soot_out, scale, gain, moved = last(
        high, low, to_low, to_high, count, got_a, got_b, loads, spray_0, spray_1, nxt, nxt_nu, keep
    )
    mass_out = droplets(mass, above, scale, gain, moved)
    return wind_out, heat_out, soot_out, mass_out, count_out


def solution(mesh):
    return jax.shard_map(
        local,
        mesh=mesh,
        in_specs=(
            P(None, "tun", "sec", None),
            P("tun", "sec", None),
            P("tun", "sec", None),
            P(None, "tun", "sec", None),
            P("tun", "sec", None),
            P("tun", "sec", None),
            P(),
        ),
        out_specs=(
            P(None, "tun", "sec", None),
            P("tun", "sec", None),
            P("tun", "sec", None),
            P(None, "tun", "sec", None),
            P("tun", "sec", None),
        ),
        check_vma=False,
    )
```

time: 152 us -> 36.7 us (0.24)
  the two profiles are of different devices: /device:TPU:32 before, /device:TPU:96 now
where the time goes in v2:
time: 36.7 us; the launch traced here: 36.4 us
  starting transfers between devices  21 us (57%)
  waiting for transfers between devices  8.42 us (23%)
  Pallas kernels  6.33 us (17%)
  between operations  0.72 us (2%)
    ppermute x1, starting transfers between devices, local(): low = lax.ppermute(to_high, 'sec', [(i, i + 1) for i in range(width - 1)])  9.73 us
    ppermute x1, starting transfers between devices, local(): got_b = lax.ppermute(msg_b, 'tun', pairs_b)  6.1 us
    ppermute x1, waiting for transfers between devices, local(): lax.ppermute(pack_mass(mass, to_low), 'tun', [(i, i + 1) for i in range(c...  6.07 us
    ppermute x1, starting transfers between devices, local(): got_a = lax.ppermute(msg_a, 'tun', pairs_a)  1.92 us
    ppermute x1, starting transfers between devices, local(): lax.ppermute(pack_mass(mass, to_low), 'tun', [(i, i + 1) for i in range(c...  1.92 us
    pallas_call x1, Pallas kernels, last(): pl.pallas_call(last_kernel, out_shape=(jax.ShapeDtypeStruct((3,) + block,...  1.42 us
    pallas_call x1, Pallas kernels, load(): pl.pallas_call(load_kernel, out_shape=tuple((pltpu.VMEM(a.shape, a.dtype)...  1.36 us
    ppermute x1, starting transfers between devices, local(): high = lax.ppermute(to_low, 'sec', [(i + 1, i) for i in range(width - 1)])  1.29 us
  transfers between devices with their start and end apart: 5, of which 3 were waited for; matrix products, arithmetic and copies ran while one was open for 0% of the time, Pallas kernels for 11%

profile of v2, /device:TPU:96, one launch (start us, length us, event | category | flops | bytes accessed | tf_op | source)
XLA Modules:
  0.0 36.4 jit_solution(10715507347308775626)
XLA Ops:
  0.6 1.1 %pack_tun.1 = (f32[8,2,16,128]{3,2,1,0:T(8,128)S(1)}, f32[8,2,16,128]{3,2,1,0:T(8,128)S(1)}) custom-call(s32[8]{0:T(128)} %onset.3, f32[3,8,16,128]{3,2,1,0:T(8,128)} %wind.3, f32[8,16,128]{2,1,0:T(8,128)} %heat.3, f32[8,16,128]{2,1,0:T(8,128)} %soot.3, f32[16,8,16,128]{3,2,1,0:T(8,128)} %mass.3, s32[8,16,128]{2,1,0:T(8,128)} %count.3, s32[8,16,128]{2,1,0:T(8,128)} %label.3), custom_call_target="tpu_custom_call" | custom-call | tf_op jit(solution)/shard_map/pack_tun/pallas_call | solution.py:97
  1.8 6.1 %collective-permute-start = (f32[8,2,16,128]{3,2,1,0:T(8,128)S(1)}, f32[8,2,16,128]{3,2,1,0:T(8,128)S(1)}, u32[]{:S(2)}, u32[]{:S(2)}) collective-permute-start(f32[8,2,16,128]{3,2,1,0:T(8,128)S(1)} %get-tuple-element.28.after), channel_id=1, source_target_pairs={{4,8},{8,4},{12,16},{16,12},{20,24},{24,20},{28,32},{32,28},{36,40... | collective-permute-start | bytes 393224 | tf_op jit(solution)/shard_map/ppermute | solution.py:513
  7.9 1.9 %collective-permute-start.1 = (f32[8,2,16,128]{3,2,1,0:T(8,128)S(1)}, f32[8,2,16,128]{3,2,1,0:T(8,128)S(1)}, u32[]{:S(2)}, u32[]{:S(2)}) collective-permute-start(f32[8,2,16,128]{3,2,1,0:T(8,128)S(1)} %get-tuple-element.29), channel_id=1, source_target_pairs={{0,4},{4,0},{8,12},{12,8},{16,20},{20,16},{24,28},{28,24},{32,36},... | collective-permute-start | bytes 393224 | tf_op jit(solution)/shard_map/ppermute | solution.py:514
  9.8 1.4 %load.1 = (f32[3,8,16,128]{3,2,1,0:T(8,128)S(1)}, f32[8,16,128]{2,1,0:T(8,128)S(1)}, f32[8,16,128]{2,1,0:T(8,128)S(1)}, f32[16,8,16,128]{3,2,1,0:T(8,128)S(1)}, ...) custom-call(s32[8]{0:T(128)} %onset.3, f32[3,8,16,128]{3,2,1,0:T(8,128)} %wind.3, f32[8,16,128]{2,1,0:T(8,128)} %heat.3, ...), custom_call_target="tpu_custom_call" | custom-call | tf_op jit(solution)/shard_map/load/pallas_call | solution.py:129
  11.2 1.1 %collective-permute-done.got_b = f32[8,2,16,128]{3,2,1,0:T(8,128)S(1)} collective-permute-done((f32[8,2,16,128]{3,2,1,0:T(8,128)S(1)}, f32[8,2,16,128]{3,2,1,0:T(8,128)S(1)}, u32[]{:S(2)}, u32[]{:S(2)}) %collective-permute-start) | collective-permute-done | bytes 131104 | tf_op jit(solution)/shard_map/ppermute | solution.py:513
  12.3 0.0 collective-permute-done.1.got_a
  12.3 0.1 pack_sec.1
  12.4 1.3 %collective-permute-start.2 = (f32[11,12,128]{2,1,0:T(8,128)S(1)}, f32[11,12,128]{2,1,0:T(8,128)S(1)}, u32[]{:S(2)}, u32[]{:S(2)}) collective-permute-start(f32[11,12,128]{2,1,0:T(8,128)S(1)} %get-tuple-element.36.after.to_low), channel_id=1, source_target_pairs={{1,0},{2,1},{3,2},{5,4},{6,5},{7,6},{9,8},{10,9},{11,10},{13,12},{... | collective-permute-start | bytes 202760 | tf_op jit(solution)/shard_map/ppermute | solution.py:516
  13.7 9.7 %collective-permute-start.3 = (f32[11,12,128]{2,1,0:T(8,128)S(1)}, f32[11,12,128]{2,1,0:T(8,128)S(1)}, u32[]{:S(2)}, u32[]{:S(2)}) collective-permute-start(f32[11,12,128]{2,1,0:T(8,128)S(1)} %get-tuple-element.37.to_high), channel_id=1, source_target_pairs={{0,1},{1,2},{2,3},{4,5},{5,6},{6,7},{8,9},{9,10},{10,11},{12,13},{... | collective-permute-start | bytes 202760 | tf_op jit(solution)/shard_map/ppermute | solution.py:517
  23.5 1.9 %collective-permute-start.4 = (f32[16,2,16,128]{3,2,1,0:T(8,128)S(1)}, f32[16,2,16,128]{3,2,1,0:T(8,128)S(1)}, u32[]{:S(2)}, u32[]{:S(2)}) collective-permute-start(f32[16,2,16,128]{3,2,1,0:T(8,128)S(1)} %pack_mass.1), channel_id=1, source_target_pairs={{0,4},{4,8},{8,12},{12,16},{16,20},{20,24},{24,28},{28,32},{32,36}... | collective-permute-start | bytes 786440 | tf_op jit(solution)/shard_map/ppermute | solution.py:518
  25.4 1.2 %first_substep.1 = (s32[8,16,128]{2,1,0:T(8,128)}, f32[1600,128]{1,0:T(8,128)S(1)}, f32[320,128]{1,0:T(8,128)S(1)}, f32[144,128]{1,0:T(8,128)S(1)}, f32[9,16,128...) custom-call(f32[3,8,16,128]{3,2,1,0:T(8,128)S(1)} %get-tuple-element.30.wind, ...), custom_call_target="tpu_custom_call" | custom-call | tf_op jit(solution)/shard_map/first_substep/pallas_call | solution.py:338
  26.6 0.0 collective-permute-done.2.high
  26.6 1.2 %collective-permute-done.3.low = f32[11,12,128]{2,1,0:T(8,128)S(1)} collective-permute-done((f32[11,12,128]{2,1,0:T(8,128)S(1)}, f32[11,12,128]{2,1,0:T(8,128)S(1)}, u32[]{:S(2)}, u32[]{:S(2)}) %collective-permute-start.3) | collective-permute-done | bytes 67616 | tf_op jit(solution)/shard_map/ppermute | solution.py:517
  27.9 1.4 %last_substep.1 = (f32[3,8,16,128]{3,2,1,0:T(8,128)}, f32[8,16,128]{2,1,0:T(8,128)}, f32[8,16,128]{2,1,0:T(8,128)}, f32[8,16,128]{2,1,0:T(8,128)S(1)}, f32[8,16,...) custom-call(f32[11,12,128]{2,1,0:T(8,128)S(1)} %collective-permute-d, ...), custom_call_target="tpu_custom_call", output_to_operand_aliasing={{6}: (10, {}), {7}: (11, {}), {8}: (12, {})} | custom-call | flops 99999997952 | bytes 100000000 | tf_op jit(solution)/shard_map/last_substep/pallas_call | solution.py:457
  29.3 6.1 %collective-permute-done.4.above = f32[16,2,16,128]{3,2,1,0:T(8,128)S(1)} collective-permute-done((f32[16,2,16,128]{3,2,1,0:T(8,128)S(1)}, f32[16,2,16,128]{3,2,1,0:T(8,128)S(1)}, u32[]{:S(2)}, u32[]{:S(2)}) %collective-permute-start.4) | collective-permute-done | bytes 262176 | tf_op jit(solution)/shard_map/ppermute | solution.py:518
  35.4 1.0 %droplets.1 = f32[16,8,16,128]{3,2,1,0:T(8,128)} custom-call(f32[16,8,16,128]{3,2,1,0:T(8,128)S(1)} %get-tuple-element.33.mass, f32[16,2,16,128]{3,2,1,0:T(8,128)S(1)} %collective-permute-done.4.above, f32[8,16,128]{2,1,0:T(8,128)S(1)} %get-tuple-element.47.scale, f32[8,16,128]{2,1,0:T(8,128)S(1)} %get-tuple-element.48.gain, ...), custom_call_target="tpu_custom_call" | custom-call | tf_op jit(solution)/shard_map/droplets/pallas_call | solution.py:496
  (1 shorter events, 0.0 us)
Async XLA Ops:
  1.8 10.5 %collective-permute-start = (f32[8,2,16,128]{3,2,1,0:T(8,128)S(1)}, f32[8,2,16,128]{3,2,1,0:T(8,128)S(1)}, u32[]{:S(2)}, u32[]{:S(2)}) collective-permute-start(f32[8,2,16,128]{3,2,1,0:T(8,128)S(1)} %get-tuple-element.28.after), channel_id=1, source_target_pairs={{4,8},{8,4},{12,16},{16,12},{20,24},{24,20},{28,32},{32,28},{36,40... | collective-permute-start | bytes 393224 | tf_op jit(solution)/shard_map/ppermute | solution.py:513
  7.9 4.4 %collective-permute-start.1 = (f32[8,2,16,128]{3,2,1,0:T(8,128)S(1)}, f32[8,2,16,128]{3,2,1,0:T(8,128)S(1)}, u32[]{:S(2)}, u32[]{:S(2)}) collective-permute-start(f32[8,2,16,128]{3,2,1,0:T(8,128)S(1)} %get-tuple-element.29), channel_id=1, source_target_pairs={{0,4},{4,0},{8,12},{12,8},{16,20},{20,16},{24,28},{28,24},{32,36},... | collective-permute-start | bytes 393224 | tf_op jit(solution)/shard_map/ppermute | solution.py:514
  12.4 14.2 %collective-permute-start.2 = (f32[11,12,128]{2,1,0:T(8,128)S(1)}, f32[11,12,128]{2,1,0:T(8,128)S(1)}, u32[]{:S(2)}, u32[]{:S(2)}) collective-permute-start(f32[11,12,128]{2,1,0:T(8,128)S(1)} %get-tuple-element.36.after.to_low), channel_id=1, source_target_pairs={{1,0},{2,1},{3,2},{5,4},{6,5},{7,6},{9,8},{10,9},{11,10},{13,12},{... | collective-permute-start | bytes 202760 | tf_op jit(solution)/shard_map/ppermute | solution.py:516
  13.7 14.2 %collective-permute-start.3 = (f32[11,12,128]{2,1,0:T(8,128)S(1)}, f32[11,12,128]{2,1,0:T(8,128)S(1)}, u32[]{:S(2)}, u32[]{:S(2)}) collective-permute-start(f32[11,12,128]{2,1,0:T(8,128)S(1)} %get-tuple-element.37.to_high), channel_id=1, source_target_pairs={{0,1},{1,2},{2,3},{4,5},{5,6},{6,7},{8,9},{9,10},{10,11},{12,13},{... | collective-permute-start | bytes 202760 | tf_op jit(solution)/shard_map/ppermute | solution.py:517
  23.5 11.9 %collective-permute-start.4 = (f32[16,2,16,128]{3,2,1,0:T(8,128)S(1)}, f32[16,2,16,128]{3,2,1,0:T(8,128)S(1)}, u32[]{:S(2)}, u32[]{:S(2)}) collective-permute-start(f32[16,2,16,128]{3,2,1,0:T(8,128)S(1)} %pack_mass.1), channel_id=1, source_target_pairs={{0,4},{4,8},{8,12},{12,16},{16,20},{20,24},{24,28},{28,32},{32,36}... | collective-permute-start | bytes 786440 | tf_op jit(solution)/shard_map/ppermute | solution.py:518

commit v3 on v2

--- a/solution.py
+++ b/solution.py
@@ -24,7 +24,7 @@
 ROW = 8
 
 
-FIRST_COST, LAST_COST = 0, 100
+FIRST_COST, LAST_COST = 0, 1
 
 
 def cost(units):
@@ -158,7 +158,7 @@
     )(*on_chip(mass, after))
 
 
-def pack_sec_kernel(got_b, got_a, wind, heat, soot, mass, count, begins, to_low, to_high):
+def pack_sec_kernel(got_b, got_a, wind, heat, soot, mass, count, begins, to_low, to_high, own_low, own_high):
     depth, rows, lanes = heat.shape
     slots = mass.shape[0]
     odd = lax.axis_index("tun") % 2 == 1
@@ -178,11 +178,16 @@
         a, b = from_a[here, :], from_b[here, :]
         return jnp.where(odd, a, b), jnp.where(odd, b, a)
 
-    for msg, first, second in ((to_low, 0, 1), (to_high, rows - 1, rows - 2)):
+    for msg, kept, first, second in ((to_low, own_low, 0, 1), (to_high, own_high, rows - 1, rows - 2)):
         for f in range(NF):
             for n, row in ((f, first), (NF + f, second)):
                 before, after = beside(f, row)
-                msg[n] = jnp.concatenate([before, own(f, row), after], axis=0)
+                centre = own(f, row)
+                kept[n] = jnp.concatenate([before, centre, after], axis=0)
+                msg[n] = centre
+                if n < NF:
+                    corner, place = 2 * NF + 1 + n // 4, 2 * (n % 4)
+                    msg[corner, place : place + 2, :] = jnp.concatenate([before[1:], after[:1]], axis=0)
         here = pl.ds(first, depth, stride=rows)
         held = counted[here, :]
         sums = live_sum([massed[pl.ds(k * depth * rows + first, depth, stride=rows), :] for k in range(slots)], held)
@@ -192,17 +197,20 @@
         starts = jnp.concatenate([begins_up[1:], begun[here, :].astype(F32), begins_down[:1]], axis=0)
         held = jnp.concatenate([held_up, held.astype(F32)], axis=0)
         sums = jnp.concatenate([sums_up, sums], axis=0)
-        msg[2 * NF, 1 : 3 + depth, :] = sums + jnp.where(starts <= 0.0, inject_rate * held, 0.0)
+        loads = sums + jnp.where(starts <= 0.0, inject_rate * held, 0.0)
+        kept[2 * NF, 1 : 3 + depth, :] = loads
+        msg[2 * NF] = loads[1 : 1 + depth]
 
 
 def pack_sec(wind, heat, soot, mass, count, begins, got_a, got_b):
     depth, rows, lanes = heat.shape
-    msg = pltpu.VMEM((2 * NF + 1, depth + 4, lanes), F32)
+    msg = pltpu.VMEM((2 * NF + 3, depth, lanes), F32)
+    kept = pltpu.VMEM((2 * NF + 1, depth + 4, lanes), F32)
     return pl.pallas_call(
         pack_sec_kernel,
-        out_shape=(msg, msg),
+        out_shape=(msg, msg, kept, kept),
         in_specs=[VMEM] * 8,
-        out_specs=(VMEM,) * 2,
+        out_specs=(VMEM,) * 4,
         compiler_params=LIMIT,
         name="pack_sec",
     )(*on_chip(got_b, got_a, wind, heat, soot, mass, count, begins))
@@ -361,9 +369,9 @@
 
 
 def last_kernel(
-    high, low, to_low, to_high, count, got_a, got_b, loads, spray_0, spray_1, nxt_in, nxt_nu_in, keep_in,
+    high, low, own_low, own_high, count, got_a, got_b, loads, spray_0, spray_1, nxt_in, nxt_nu_in, keep_in,
     wind_out, heat_out, soot_out, scale, gain, moved, nxt, nxt_nu, keep,
-    fields, sems,
+    fields, beside, sems,
 ):
     depth, rows, lanes = count.shape
     tall = rows + 2 * ROW
@@ -371,48 +379,83 @@
     tun, sec = lax.axis_index("tun"), lax.axis_index("sec")
     odd = tun % 2 == 1
     inside_up, inside_down = tun > 0, tun < lax.axis_size("tun") - 1
-    sides_of = (
-        (low, to_low, ROW - 1, 0, sec > 0),
-        (high, to_high, ROW + rows, rows - 1, sec < lax.axis_size("sec") - 1),
-    )
-
     place = lax.broadcasted_iota(jnp.int32, (planes, lanes), 0)
     inside = ((place > 0) | inside_up) & ((place < planes - 1) | inside_down)
-    mid = slice(1, 1 + planes)
-    for flip, (got, sent, outer_row, inner_row, there) in enumerate(sides_of):
-        got_nu, sent_nu = viscosity(got[3]), viscosity(sent[3])
-        got_nu_2, sent_nu_2 = viscosity(got[NF + 3, mid, :]), viscosity(sent[NF + 3, mid, :])
-        for ref, ref_nu, near, near_nu, far, far_nu, row, valid in (
-            (got, got_nu, lambda f, sent=sent: sent[f, mid, :], sent_nu[mid], lambda f, got=got: got[NF + f, mid, :], got_nu_2, outer_row, there),
-            (sent, sent_nu, lambda f, got=got: got[f, mid, :], got_nu[mid], lambda f, sent=sent: sent[NF + f, mid, :], sent_nu_2, ROW + inner_row, inside),
-        ):
-            is_outer = ref is got
-            centre = [ref[f, mid, :] for f in range(NF)]
-            nu = ref_nu[mid]
-            lifted = [around(c) for c in centre]
-            swap = bool(flip) == is_outer
-            sides = [
-                (lambda f, ref=ref: ref[f, 0:planes, :], lambda f, ref=ref: ref[f, 2 : 2 + planes, :]),
-                (near, far) if swap else (far, near),
+
+    def step(centre, nu, sides, nu_sides, load):
+        new = stencil(centre, nu, sides, nu_sides)
+        evap = evap_rate * jax.nn.sigmoid(new[3])
+        new[3] = new[3] - latent_heat * (evap * load)
+        new[4] = new[4] / (1.0 + scavenge * load)
+        return new, 1.0 - evap
+
+    for flip, (got, own, outer_row, inner_row, there) in enumerate(
+        (
+            (low, own_low, ROW - 1, 0, sec > 0),
+            (high, own_high, ROW + rows, rows - 1, sec < lax.axis_size("sec") - 1),
+        )
+    ):
+        line = beside.at[flip]
+        for f in range(NF):
+            corner, spot = 2 * NF + 1 + f // 4, 2 * (f % 4)
+            line[f, 8 : 8 + depth, :] = got[f]
+            line[f, 7:8, :] = got[corner, spot : spot + 1, :]
+            line[f, 8 + depth : 9 + depth, :] = got[corner, spot + 1 : spot + 2, :]
+        wide, block = slice(7, 9 + depth), slice(8, 8 + depth)
+        line_nu, own_nu = viscosity(line[3, wide, :]), viscosity(own[3])
+
+        def ordered(near, far, swap):
+            return (near, far) if swap else (far, near)
+
+        centre = [line[f, block, :] for f in range(NF)]
+        lifted = [around(c) for c in centre]
+        nu = line_nu[1 : 1 + depth]
+        new, _ = step(
+            centre,
+            nu,
+            [
+                (lambda f: line[f, 7 : 7 + depth, :], lambda f: line[f, 9 : 9 + depth, :]),
+                ordered(lambda f: own[f, 2 : 2 + depth, :], lambda f: got[NF + f], flip == 1),
                 (lambda f: lifted[f][0], lambda f: lifted[f][1]),
-            ]
-            nu_sides = [
-                (ref_nu[0:planes], ref_nu[2 : 2 + planes]),
-                (near_nu, far_nu) if swap else (far_nu, near_nu),
+            ],
+            [
+                (line_nu[0:depth], line_nu[2 : 2 + depth]),
+                ordered(own_nu[2 : 2 + depth], viscosity(got[NF + 3]), flip == 1),
                 nu_around(nu),
-            ]
-            new = stencil(centre, nu, sides, nu_sides)
-            load = ref[2 * NF, mid, :]
-            evap = evap_rate * jax.nn.sigmoid(new[3])
-            new[3] = new[3] - latent_heat * (evap * load)
-            new[4] = new[4] / (1.0 + scavenge * load)
-            for f in range(NF):
-                value = jnp.where(valid, new[f], 0.0)
-                nxt[pl.ds(f * planes * tall + row, planes, stride=tall), :] = value
-                if f == 3:
-                    nxt_nu[pl.ds(row, planes, stride=tall), :] = viscosity(value)
-            if not is_outer:
-                keep[pl.ds(inner_row, depth + 1, stride=rows), :] = (1.0 - evap)[: depth + 1]
+            ],
+            got[2 * NF],
+        )
+        for f in range(NF):
+            value = jnp.where(there, new[f], 0.0)
+            nxt[pl.ds((f * planes + 1) * tall + outer_row, depth, stride=tall), :] = value
+            if f == 3:
+                nxt_nu[pl.ds(tall + outer_row, depth, stride=tall), :] = viscosity(value)
+
+        mid = slice(1, 1 + planes)
+        centre = [own[f, mid, :] for f in range(NF)]
+        lifted = [around(c) for c in centre]
+        nu = own_nu[mid]
+        new, left = step(
+            centre,
+            nu,
+            [
+                (lambda f: own[f, 0:planes, :], lambda f: own[f, 2 : 2 + planes, :]),
+                ordered(lambda f: line[f, wide, :], lambda f: own[NF + f, mid, :], flip == 0),
+                (lambda f: lifted[f][0], lambda f: lifted[f][1]),
+            ],
+            [
+                (own_nu[0:planes], own_nu[2 : 2 + planes]),
+                ordered(line_nu, viscosity(own[NF + 3, mid, :]), flip == 0),
+                nu_around(nu),
+            ],
+            own[2 * NF, mid, :],
+        )
+        for f in range(NF):
+            value = jnp.where(inside, new[f], 0.0)
+            nxt[pl.ds(f * planes * tall + ROW + inner_row, planes, stride=tall), :] = value
+            if f == 3:
+                nxt_nu[pl.ds(ROW + inner_row, planes, stride=tall), :] = viscosity(value)
+        keep[pl.ds(inner_row, depth + 1, stride=rows), :] = left[: depth + 1]
 
     def at(ref, plane, shift=0):
         return ref[plane * tall + ROW + shift : plane * tall + ROW + shift + rows, :]
@@ -451,9 +494,9 @@
         copy.wait()
 
 
-def last(high, low, to_low, to_high, count, got_a, got_b, loads, spray_0, spray_1, nxt, nxt_nu, keep):
+def last(high, low, own_low, own_high, count, got_a, got_b, loads, spray_0, spray_1, nxt, nxt_nu, keep):
     block = count.shape
-    operands = on_chip(high, low, to_low, to_high, count, got_a, got_b, loads, spray_0, spray_1, nxt, nxt_nu, keep)
+    operands = on_chip(high, low, own_low, own_high, count, got_a, got_b, loads, spray_0, spray_1, nxt, nxt_nu, keep)
     return pl.pallas_call(
         last_kernel,
         out_shape=(
@@ -470,7 +513,11 @@
         in_specs=[VMEM] * 13,
         out_specs=(ANY,) * 3 + (VMEM,) * 6,
         input_output_aliases={10: 6, 11: 7, 12: 8},
-        scratch_shapes=[pltpu.VMEM((NF,) + block, F32), pltpu.SemaphoreType.DMA((3,))],
+        scratch_shapes=[
+            pltpu.VMEM((NF,) + block, F32),
+            pltpu.VMEM((2, NF, block[0] + 16, block[2]), F32),
+            pltpu.SemaphoreType.DMA((3,)),
+        ],
         compiler_params=LIMIT,
         cost_estimate=cost(LAST_COST),
         name="last_substep",
@@ -512,15 +559,15 @@
     wind, heat, soot, mass, count, begins = load(onset, wind, heat, soot, mass, count, label, msg_b)
     got_b = lax.ppermute(msg_b, "tun", pairs_b)
     got_a = lax.ppermute(msg_a, "tun", pairs_a)
-    to_low, to_high = pack_sec(wind, heat, soot, mass, count, begins, got_a, got_b)
+    to_low, to_high, own_low, own_high = pack_sec(wind, heat, soot, mass, count, begins, got_a, got_b)
     high = lax.ppermute(to_low, "sec", [(i + 1, i) for i in range(width - 1)])
     low = lax.ppermute(to_high, "sec", [(i, i + 1) for i in range(width - 1)])
-    above = lax.ppermute(pack_mass(mass, to_low), "tun", [(i, i + 1) for i in range(chain - 1)])
+    above = lax.ppermute(pack_mass(mass, got_b), "tun", [(i, i + 1) for i in range(chain - 1)])
     count_out, nxt, nxt_nu, keep, loads, spray_0, spray_1 = first(
         wind, heat, soot, mass, count, begins, got_a, got_b, to_low
     )
     wind_out, heat_out, soot_out, scale, gain, moved = last(
-        high, low, to_low, to_high, count, got_a, got_b, loads, spray_0, spray_1, nxt, nxt_nu, keep
+        high, low, own_low, own_high, count, got_a, got_b, loads, spray_0, spray_1, nxt, nxt_nu, keep
     )
     mass_out = droplets(mass, above, scale, gain, moved)
     return wind_out, heat_out, soot_out, mass_out, count_out

time: 36.7 us -> 34.9 us (0.951)
  the two profiles are of different devices: /device:TPU:96 before, /device:TPU:446 now
where the time goes in v3:
time: 34.9 us; the launch traced here: 34.6 us
  starting transfers between devices  17.2 us (49%)
  waiting for transfers between devices  10.2 us (29%)
  Pallas kernels  6.38 us (18%)
  between operations  0.73 us (2%)
    ppermute x1, waiting for transfers between devices, local(): low = lax.ppermute(to_high, 'sec', [(i, i + 1) for i in range(width - 1)])  9.06 us
    ppermute x1, starting transfers between devices, local(): lax.ppermute(pack_mass(mass, got_b), 'tun', [(i, i + 1) for i in range(ch...  5.96 us
    ppermute x1, starting transfers between devices, local(): high = lax.ppermute(to_low, 'sec', [(i + 1, i) for i in range(width - 1)])  5.46 us
    ppermute x1, starting transfers between devices, local(): got_a = lax.ppermute(msg_a, 'tun', pairs_a)  2.43 us
    ppermute x1, starting transfers between devices, local(): got_b = lax.ppermute(msg_b, 'tun', pairs_b)  2.09 us
    pallas_call x1, Pallas kernels, last(): pl.pallas_call(last_kernel, out_shape=(jax.ShapeDtypeStruct((3,) + block,...  1.44 us
    pallas_call x1, Pallas kernels, load(): pl.pallas_call(load_kernel, out_shape=tuple((pltpu.VMEM(a.shape, a.dtype)...  1.36 us
    ppermute x1, starting transfers between devices, local(): low = lax.ppermute(to_high, 'sec', [(i, i + 1) for i in range(width - 1)])  1.29 us
  transfers between devices with their start and end apart: 5, of which 3 were waited for; matrix products, arithmetic and copies ran while one was open for 0% of the time, Pallas kernels for 12%

profile of v3, /device:TPU:446, one launch (start us, length us, event | category | flops | bytes accessed | tf_op | source)
XLA Modules:
  0.0 34.6 jit_solution(3724641476986780029)
XLA Ops:
  0.6 1.1 %pack_tun.1 = (f32[8,2,16,128]{3,2,1,0:T(8,128)S(1)}, f32[8,2,16,128]{3,2,1,0:T(8,128)S(1)}) custom-call(s32[8]{0:T(128)} %onset.3, f32[3,8,16,128]{3,2,1,0:T(8,128)} %wind.3, f32[8,16,128]{2,1,0:T(8,128)} %heat.3, f32[8,16,128]{2,1,0:T(8,128)} %soot.3, f32[16,8,16,128]{3,2,1,0:T(8,128)} %mass.3, s32[8,16,128]{2,1,0:T(8,128)} %count.3, s32[8,16,128]{2,1,0:T(8,128)} %label.3), custom_call_target="tpu_custom_call" | custom-call | tf_op jit(solution)/shard_map/pack_tun/pallas_call | solution.py:97
  1.8 2.1 %collective-permute-start = (f32[8,2,16,128]{3,2,1,0:T(8,128)S(1)}, f32[8,2,16,128]{3,2,1,0:T(8,128)S(1)}, u32[]{:S(2)}, u32[]{:S(2)}) collective-permute-start(f32[8,2,16,128]{3,2,1,0:T(8,128)S(1)} %get-tuple-element.30.after), channel_id=1, source_target_pairs={{4,8},{8,4},{12,16},{16,12},{20,24},{24,20},{28,32},{32,28},{36,40... | collective-permute-start | bytes 393224 | tf_op jit(solution)/shard_map/ppermute | solution.py:560
  3.9 2.4 %collective-permute-start.1 = (f32[8,2,16,128]{3,2,1,0:T(8,128)S(1)}, f32[8,2,16,128]{3,2,1,0:T(8,128)S(1)}, u32[]{:S(2)}, u32[]{:S(2)}) collective-permute-start(f32[8,2,16,128]{3,2,1,0:T(8,128)S(1)} %get-tuple-element.31), channel_id=1, source_target_pairs={{0,4},{4,0},{8,12},{12,8},{16,20},{20,16},{24,28},{28,24},{32,36},... | collective-permute-start | bytes 393224 | tf_op jit(solution)/shard_map/ppermute | solution.py:561
  6.3 1.4 %load.1 = (f32[3,8,16,128]{3,2,1,0:T(8,128)S(1)}, f32[8,16,128]{2,1,0:T(8,128)S(1)}, f32[8,16,128]{2,1,0:T(8,128)S(1)}, f32[16,8,16,128]{3,2,1,0:T(8,128)S(1)}, ...) custom-call(s32[8]{0:T(128)} %onset.3, f32[3,8,16,128]{3,2,1,0:T(8,128)} %wind.3, f32[8,16,128]{2,1,0:T(8,128)} %heat.3, ...), custom_call_target="tpu_custom_call" | custom-call | tf_op jit(solution)/shard_map/load/pallas_call | solution.py:129
  7.7 0.4 %collective-permute-done.got_b.after = f32[8,2,16,128]{3,2,1,0:T(8,128)S(1)} collective-permute-done((f32[8,2,16,128]{3,2,1,0:T(8,128)S(1)}, f32[8,2,16,128]{3,2,1,0:T(8,128)S(1)}, u32[]{:S(2)}, u32[]{:S(2)}) %collective-permute-start) | collective-permute-done | bytes 131104 | tf_op jit(solution)/shard_map/ppermute | solution.py:560
  8.1 6.0 %collective-permute-start.4 = (f32[16,2,16,128]{3,2,1,0:T(8,128)S(1)}, f32[16,2,16,128]{3,2,1,0:T(8,128)S(1)}, u32[]{:S(2)}, u32[]{:S(2)}) collective-permute-start(f32[16,2,16,128]{3,2,1,0:T(8,128)S(1)} %pack_mass.1), channel_id=1, source_target_pairs={{0,4},{4,8},{8,12},{12,16},{16,20},{20,24},{24,28},{28,32},{32,36}... | collective-permute-start | bytes 786440 | tf_op jit(solution)/shard_map/ppermute | solution.py:565
  14.1 0.0 collective-permute-done.1.got_a
  14.1 0.1 pack_sec.1
  14.2 5.5 %collective-permute-start.2 = (f32[13,8,128]{2,1,0:T(8,128)S(1)}, f32[13,8,128]{2,1,0:T(8,128)S(1)}, u32[]{:S(2)}, u32[]{:S(2)}) collective-permute-start(f32[13,8,128]{2,1,0:T(8,128)S(1)} %get-tuple-element.38.after), channel_id=1, source_target_pairs={{1,0},{2,1},{3,2},{5,4},{6,5},{7,6},{9,8},{10,9},{11,10},{13,12},{... | collective-permute-start | bytes 159752 | tf_op jit(solution)/shard_map/ppermute | solution.py:563
  19.7 1.3 %collective-permute-start.3 = (f32[13,8,128]{2,1,0:T(8,128)S(1)}, f32[13,8,128]{2,1,0:T(8,128)S(1)}, u32[]{:S(2)}, u32[]{:S(2)}) collective-permute-start(f32[13,8,128]{2,1,0:T(8,128)S(1)} %get-tuple-element.39), channel_id=1, source_target_pairs={{0,1},{1,2},{2,3},{4,5},{5,6},{6,7},{8,9},{9,10},{10,11},{12,13},{... | collective-permute-start | bytes 159752 | tf_op jit(solution)/shard_map/ppermute | solution.py:564
  21.0 1.2 %first_substep.1 = (s32[8,16,128]{2,1,0:T(8,128)}, f32[1600,128]{1,0:T(8,128)S(1)}, f32[320,128]{1,0:T(8,128)S(1)}, f32[144,128]{1,0:T(8,128)S(1)}, f32[9,16,128...) custom-call(f32[3,8,16,128]{3,2,1,0:T(8,128)S(1)} %get-tuple-element.32.wind, ...), custom_call_target="tpu_custom_call" | custom-call | tf_op jit(solution)/shard_map/first_substep/pallas_call | solution.py:346
  22.2 0.8 %collective-permute-done.2.high = f32[13,8,128]{2,1,0:T(8,128)S(1)} collective-permute-done((f32[13,8,128]{2,1,0:T(8,128)S(1)}, f32[13,8,128]{2,1,0:T(8,128)S(1)}, u32[]{:S(2)}, u32[]{:S(2)}) %collective-permute-start.2) | collective-permute-done | bytes 53280 | tf_op jit(solution)/shard_map/ppermute | solution.py:563
  23.0 9.1 %collective-permute-done.3.low = f32[13,8,128]{2,1,0:T(8,128)S(1)} collective-permute-done((f32[13,8,128]{2,1,0:T(8,128)S(1)}, f32[13,8,128]{2,1,0:T(8,128)S(1)}, u32[]{:S(2)}, u32[]{:S(2)}) %collective-permute-start.3) | collective-permute-done | bytes 53280 | tf_op jit(solution)/shard_map/ppermute | solution.py:564
  32.1 1.4 %last_substep.1 = (f32[3,8,16,128]{3,2,1,0:T(8,128)}, f32[8,16,128]{2,1,0:T(8,128)}, f32[8,16,128]{2,1,0:T(8,128)}, f32[8,16,128]{2,1,0:T(8,128)S(1)}, f32[8,16,...) custom-call(f32[13,8,128]{2,1,0:T(8,128)S(1)} %collective-permute-do, ...), custom_call_target="tpu_custom_call", output_to_operand_aliasing={{6}: (10, {}), {7}: (11, {}), {8}: (12, {})} | custom-call | flops 1000000000 | bytes 1000000 | tf_op jit(solution)/shard_map/last_substep/pallas_call | solution.py:500
  33.5 0.0 collective-permute-done.4.above
  33.5 1.0 %droplets.1 = f32[16,8,16,128]{3,2,1,0:T(8,128)} custom-call(f32[16,8,16,128]{3,2,1,0:T(8,128)S(1)} %get-tuple-element.35.mass, f32[16,2,16,128]{3,2,1,0:T(8,128)S(1)} %collective-permute-done.4.above, f32[8,16,128]{2,1,0:T(8,128)S(1)} %get-tuple-element.51.scale, f32[8,16,128]{2,1,0:T(8,128)S(1)} %get-tuple-element.52.gain, ...), custom_call_target="tpu_custom_call" | custom-call | tf_op jit(solution)/shard_map/droplets/pallas_call | solution.py:543
  (1 shorter events, 0.0 us)
Async XLA Ops:
  1.8 6.3 %collective-permute-start = (f32[8,2,16,128]{3,2,1,0:T(8,128)S(1)}, f32[8,2,16,128]{3,2,1,0:T(8,128)S(1)}, u32[]{:S(2)}, u32[]{:S(2)}) collective-permute-start(f32[8,2,16,128]{3,2,1,0:T(8,128)S(1)} %get-tuple-element.30.after), channel_id=1, source_target_pairs={{4,8},{8,4},{12,16},{16,12},{20,24},{24,20},{28,32},{32,28},{36,40... | collective-permute-start | bytes 393224 | tf_op jit(solution)/shard_map/ppermute | solution.py:560
  3.9 10.2 %collective-permute-start.1 = (f32[8,2,16,128]{3,2,1,0:T(8,128)S(1)}, f32[8,2,16,128]{3,2,1,0:T(8,128)S(1)}, u32[]{:S(2)}, u32[]{:S(2)}) collective-permute-start(f32[8,2,16,128]{3,2,1,0:T(8,128)S(1)} %get-tuple-element.31), channel_id=1, source_target_pairs={{0,4},{4,0},{8,12},{12,8},{16,20},{20,16},{24,28},{28,24},{32,36},... | collective-permute-start | bytes 393224 | tf_op jit(solution)/shard_map/ppermute | solution.py:561
  8.1 25.4 %collective-permute-start.4 = (f32[16,2,16,128]{3,2,1,0:T(8,128)S(1)}, f32[16,2,16,128]{3,2,1,0:T(8,128)S(1)}, u32[]{:S(2)}, u32[]{:S(2)}) collective-permute-start(f32[16,2,16,128]{3,2,1,0:T(8,128)S(1)} %pack_mass.1), channel_id=1, source_target_pairs={{0,4},{4,8},{8,12},{12,16},{16,20},{20,24},{24,28},{28,32},{32,36}... | collective-permute-start | bytes 786440 | tf_op jit(solution)/shard_map/ppermute | solution.py:565
  14.2 8.8 %collective-permute-start.2 = (f32[13,8,128]{2,1,0:T(8,128)S(1)}, f32[13,8,128]{2,1,0:T(8,128)S(1)}, u32[]{:S(2)}, u32[]{:S(2)}) collective-permute-start(f32[13,8,128]{2,1,0:T(8,128)S(1)} %get-tuple-element.38.after), channel_id=1, source_target_pairs={{1,0},{2,1},{3,2},{5,4},{6,5},{7,6},{9,8},{10,9},{11,10},{13,12},{... | collective-permute-start | bytes 159752 | tf_op jit(solution)/shard_map/ppermute | solution.py:563
  19.7 12.4 %collective-permute-start.3 = (f32[13,8,128]{2,1,0:T(8,128)S(1)}, f32[13,8,128]{2,1,0:T(8,128)S(1)}, u32[]{:S(2)}, u32[]{:S(2)}) collective-permute-start(f32[13,8,128]{2,1,0:T(8,128)S(1)} %get-tuple-element.39), channel_id=1, source_target_pairs={{0,1},{1,2},{2,3},{4,5},{5,6},{6,7},{8,9},{9,10},{10,11},{12,13},{... | collective-permute-start | bytes 159752 | tf_op jit(solution)/shard_map/ppermute | solution.py:564

commit v4 on v3

--- a/solution.py
+++ b/solution.py
@@ -61,28 +61,37 @@
 
 
 def pack_tun_kernel(
-    onset, wind, heat, soot, mass, count, label, msg_b, msg_a, masses, counts, labels, onsets, sems
+    onset, wind, heat, soot, mass, count, label,
+    msg_b, msg_a, winds, heats, soots, masses, counts, begins, labels, onsets, sems,
 ):
     depth = heat.shape[0]
     odd = lax.axis_index("tun") % 2 == 1
     top = depth - 2
     start_a = jnp.where(odd, 0, top)
     start_b = top - start_a
-    pairs = [(onset, onsets), (mass.at[:, top:depth], masses), (count.at[top:depth], counts)]
-    for n, (start, msg) in enumerate(((start_b, msg_b), (start_a, msg_a))):
+    onset_copy, label_copy, count_copy, *others = copies(
+        [
+            (onset, onsets), (label, labels), (count, counts), (mass, masses), (wind, winds), (heat, heats), (soot, soots)
+        ],
+        sems,
+    )
+    onset_copy.wait()
+    label_copy.wait()
+    for x in range(depth):
+        begins[x] = onset_of(labels[x], onsets)
+    count_copy.wait()
+    others[0].wait()
+    held = counts[top:depth]
+    total = live_sum([masses[k, top:depth] for k in range(masses.shape[0])], held)
+    for copy in others[1:]:
+        copy.wait()
+    for start, msg in ((start_b, msg_b), (start_a, msg_a)):
         here = pl.ds(start, 2)
-        pairs += [
-            (label.at[here], labels.at[n]),
-            (wind.at[:, here], msg.at[0:3]),
-            (heat.at[here], msg.at[3]),
-            (soot.at[here], msg.at[4]),
-        ]
-    for copy in copies(pairs, sems):
-        copy.wait()
-    held = counts[...]
-    total = live_sum([masses[k] for k in range(masses.shape[0])], held)
-    for n, msg in enumerate((msg_b, msg_a)):
-        msg[NF] = onset_of(labels[n], onsets).astype(F32)
+        for f in range(3):
+            msg[f] = winds[f, here]
+        msg[3] = heats[here]
+        msg[4] = soots[here]
+        msg[NF] = begins[here].astype(F32)
         msg[NF + 1] = held.astype(F32)
         msg[NF + 2] = total
 
@@ -92,53 +101,21 @@
 
 
 def pack_tun(onset, wind, heat, soot, mass, count, label):
-    plane = heat.shape[1:]
-    msg = pltpu.VMEM((NF + 3, 2) + plane, F32)
+    arrays = (wind, heat, soot, mass, count, label)
+    msg = pltpu.VMEM((NF + 3, 2) + heat.shape[1:], F32)
     return pl.pallas_call(
         pack_tun_kernel,
-        out_shape=(msg, msg),
+        out_shape=(msg, msg) + tuple(pltpu.VMEM(a.shape, a.dtype) for a in arrays),
         in_specs=[HBM] * 7,
-        out_specs=(VMEM,) * 2,
-        scratch_shapes=[
-            pltpu.VMEM((mass.shape[0], 2) + plane, F32),
-            pltpu.VMEM((2,) + plane, jnp.int32),
-            pltpu.VMEM((2, 2) + plane, jnp.int32),
-            pltpu.SMEM(onset.shape, jnp.int32),
-            pltpu.SemaphoreType.DMA((11,)),
-        ],
-        compiler_params=LIMIT,
-        name="pack_tun",
-    )(*in_hbm(onset, wind, heat, soot, mass, count, label))
-
-
-def load_kernel(onset, wind, heat, soot, mass, count, label, after, winds, heats, soots, masses, counts, begins, labels, onsets, sems):
-    pairs = [
-        (onset, onsets), (label, labels), (mass, masses), (wind, winds), (heat, heats), (soot, soots), (count, counts)
-    ]
-    pending = copies(pairs, sems)
-    pending[0].wait()
-    pending[1].wait()
-    for x in range(label.shape[0]):
-        begins[x] = onset_of(labels[x], onsets)
-    for copy in pending[2:]:
-        copy.wait()
-
-
-def load(onset, wind, heat, soot, mass, count, label, after):
-    arrays = (wind, heat, soot, mass, count, label)
-    return pl.pallas_call(
-        load_kernel,
-        out_shape=tuple(pltpu.VMEM(a.shape, a.dtype) for a in arrays),
-        in_specs=[HBM] * 7 + [ANY],
-        out_specs=(VMEM,) * 6,
+        out_specs=(VMEM,) * 8,
         scratch_shapes=[
             pltpu.VMEM(label.shape, jnp.int32),
             pltpu.SMEM(onset.shape, jnp.int32),
             pltpu.SemaphoreType.DMA((7,)),
         ],
         compiler_params=LIMIT,
-        name="load",
-    )(*in_hbm(onset, *arrays), after)
+        name="pack_tun",
+    )(*in_hbm(onset, *arrays))
 
 
 def pack_mass_kernel(mass, after, msg):
@@ -158,7 +135,7 @@
     )(*on_chip(mass, after))
 
 
-def pack_sec_kernel(got_b, got_a, wind, heat, soot, mass, count, begins, to_low, to_high, own_low, own_high):
+def pack_sec_kernel(got_b, got_a, wind, heat, soot, mass, count, begins, msg_x, msg_y, own_low, own_high, to_low, to_high):
     depth, rows, lanes = heat.shape
     slots = mass.shape[0]
     odd = lax.axis_index("tun") % 2 == 1
@@ -200,6 +177,11 @@
         loads = sums + jnp.where(starts <= 0.0, inject_rate * held, 0.0)
         kept[2 * NF, 1 : 3 + depth, :] = loads
         msg[2 * NF] = loads[1 : 1 + depth]
+    odd_row = lax.axis_index("sec") % 2 == 1
+    for n in range(2 * NF + 3):
+        lower, upper = to_low[n], to_high[n]
+        msg_x[n] = jnp.where(odd_row, lower, upper)
+        msg_y[n] = jnp.where(odd_row, upper, lower)
 
 
 def pack_sec(wind, heat, soot, mass, count, begins, got_a, got_b):
@@ -211,6 +193,7 @@
         out_shape=(msg, msg, kept, kept),
         in_specs=[VMEM] * 8,
         out_specs=(VMEM,) * 4,
+        scratch_shapes=[pltpu.VMEM((2 * NF + 3, depth, lanes), F32)] * 2,
         compiler_params=LIMIT,
         name="pack_sec",
     )(*on_chip(got_b, got_a, wind, heat, soot, mass, count, begins))
@@ -369,9 +352,9 @@
 
 
 def last_kernel(
-    high, low, own_low, own_high, count, got_a, got_b, loads, spray_0, spray_1, nxt_in, nxt_nu_in, keep_in,
-    wind_out, heat_out, soot_out, scale, gain, moved, nxt, nxt_nu, keep,
-    fields, beside, sems,
+    got_x, got_y, own_low, own_high, count, got_a, got_b, loads, spray_0, spray_1, nxt_in, nxt_nu_in, keep_in,
+    fields, scale, gain, moved, nxt, nxt_nu, keep,
+    beside, low, high,
 ):
     depth, rows, lanes = count.shape
     tall = rows + 2 * ROW
@@ -379,6 +362,12 @@
     tun, sec = lax.axis_index("tun"), lax.axis_index("sec")
     odd = tun % 2 == 1
     inside_up, inside_down = tun > 0, tun < lax.axis_size("tun") - 1
+    odd_row = sec % 2 == 1
+    for n in range(2 * NF + 3):
+        x, y = got_x[n], got_y[n]
+        low[n] = jnp.where(odd_row, x, y)
+        high[n] = jnp.where(odd_row, y, x)
+
     place = lax.broadcasted_iota(jnp.int32, (planes, lanes), 0)
     inside = ((place > 0) | inside_up) & ((place < planes - 1) | inside_down)
 
@@ -490,19 +479,14 @@
         moved[x] = held
         scale[x] = kept * (1.0 - evap)
         gain[x] = (spray_0[x] * kept + sprays) * (1.0 - evap)
-    for copy in copies([(fields.at[0:3], wind_out), (fields.at[3], heat_out), (fields.at[4], soot_out)], sems):
-        copy.wait()
-
-
-def last(high, low, own_low, own_high, count, got_a, got_b, loads, spray_0, spray_1, nxt, nxt_nu, keep):
+
+def last(got_x, got_y, own_low, own_high, count, got_a, got_b, loads, spray_0, spray_1, nxt, nxt_nu, keep):
     block = count.shape
-    operands = on_chip(high, low, own_low, own_high, count, got_a, got_b, loads, spray_0, spray_1, nxt, nxt_nu, keep)
+    operands = on_chip(got_x, got_y, own_low, own_high, count, got_a, got_b, loads, spray_0, spray_1, nxt, nxt_nu, keep)
     return pl.pallas_call(
         last_kernel,
         out_shape=(
-            jax.ShapeDtypeStruct((3,) + block, F32),
-            jax.ShapeDtypeStruct(block, F32),
-            jax.ShapeDtypeStruct(block, F32),
+            pltpu.VMEM((NF,) + block, F32),
             pltpu.VMEM(block, F32),
             pltpu.VMEM(block, F32),
             pltpu.VMEM(block, jnp.int32),
@@ -511,65 +495,66 @@
             pltpu.VMEM(keep.shape, F32),
         ),
         in_specs=[VMEM] * 13,
-        out_specs=(ANY,) * 3 + (VMEM,) * 6,
-        input_output_aliases={10: 6, 11: 7, 12: 8},
-        scratch_shapes=[
-            pltpu.VMEM((NF,) + block, F32),
-            pltpu.VMEM((2, NF, block[0] + 16, block[2]), F32),
-            pltpu.SemaphoreType.DMA((3,)),
-        ],
+        out_specs=(VMEM,) * 7,
+        input_output_aliases={10: 4, 11: 5, 12: 6},
+        scratch_shapes=[pltpu.VMEM((2, NF, block[0] + 16, block[2]), F32)] + [pltpu.VMEM(got_x.shape, F32)] * 2,
         compiler_params=LIMIT,
         cost_estimate=cost(LAST_COST),
         name="last_substep",
-    )(*operands)[:6]
-
-
-def droplets_kernel(mass, above, scale, gain, moved, mass_out, masses, sems):
+    )(*operands)[:4]
+
+
+def droplets_kernel(fields, mass, above, scale, gain, moved, wind_out, heat_out, soot_out, mass_out, masses, sems):
     slots, depth = mass.shape[:2]
-    pending = []
+    pending = copies([(fields.at[0:3], wind_out), (fields.at[3], heat_out), (fields.at[4], soot_out)], sems)
     for x in range(depth):
         held, by, plus = moved[x], scale[x], gain[x]
         for k in range(slots):
             before = above[k, x] if x < 2 else mass[k, x - 2]
             masses[k, x] = jnp.where(held > k, before * by + plus, before)
-        copy = pltpu.make_async_copy(masses.at[:, x], mass_out.at[:, x], sems.at[x])
+        copy = pltpu.make_async_copy(masses.at[:, x], mass_out.at[:, x], sems.at[3 + x])
         copy.start()
         pending.append(copy)
     for copy in pending:
         copy.wait()
 
 
-def droplets(mass, above, scale, gain, moved):
+def droplets(fields, mass, above, scale, gain, moved):
+    block = moved.shape
     return pl.pallas_call(
         droplets_kernel,
-        out_shape=jax.ShapeDtypeStruct(mass.shape, F32),
-        in_specs=[VMEM] * 5,
-        out_specs=ANY,
-        scratch_shapes=[pltpu.VMEM(mass.shape, F32), pltpu.SemaphoreType.DMA((mass.shape[1],))],
+        out_shape=(
+            jax.ShapeDtypeStruct((3,) + block, F32),
+            jax.ShapeDtypeStruct(block, F32),
+            jax.ShapeDtypeStruct(block, F32),
+            jax.ShapeDtypeStruct(mass.shape, F32),
+        ),
+        in_specs=[VMEM] * 6,
+        out_specs=(ANY,) * 4,
+        scratch_shapes=[pltpu.VMEM(mass.shape, F32), pltpu.SemaphoreType.DMA((3 + block[0],))],
         compiler_params=LIMIT,
         name="droplets",
-    )(*on_chip(mass, above, scale, gain, moved))
+    )(*on_chip(fields, mass, above, scale, gain, moved))
 
 
 def local(wind, heat, soot, mass, count, label, onset):
     chain, width = lax.axis_size("tun"), lax.axis_size("sec")
     pairs_a = [(i, i ^ 1) for i in range(chain)]
     pairs_b = [(i, ((i + 1) ^ 1) - 1) for i in range(1, chain - 1)]
-    msg_b, msg_a = pack_tun(onset, wind, heat, soot, mass, count, label)
-    wind, heat, soot, mass, count, begins = load(onset, wind, heat, soot, mass, count, label, msg_b)
+    msg_b, msg_a, wind, heat, soot, mass, count, begins = pack_tun(onset, wind, heat, soot, mass, count, label)
     got_b = lax.ppermute(msg_b, "tun", pairs_b)
     got_a = lax.ppermute(msg_a, "tun", pairs_a)
-    to_low, to_high, own_low, own_high = pack_sec(wind, heat, soot, mass, count, begins, got_a, got_b)
-    high = lax.ppermute(to_low, "sec", [(i + 1, i) for i in range(width - 1)])
-    low = lax.ppermute(to_high, "sec", [(i, i + 1) for i in range(width - 1)])
-    above = lax.ppermute(pack_mass(mass, got_b), "tun", [(i, i + 1) for i in range(chain - 1)])
+    msg_x, msg_y, own_low, own_high = pack_sec(wind, heat, soot, mass, count, begins, got_a, got_b)
+    got_x = lax.ppermute(msg_x, "sec", [(i, i ^ 1) for i in range(width)])
+    got_y = lax.ppermute(msg_y, "sec", [(i, ((i + 1) ^ 1) - 1) for i in range(1, width - 1)])
+    above = lax.ppermute(pack_mass(mass, begins), "tun", [(i, i + 1) for i in range(chain - 1)])
     count_out, nxt, nxt_nu, keep, loads, spray_0, spray_1 = first(
-        wind, heat, soot, mass, count, begins, got_a, got_b, to_low
+        wind, heat, soot, mass, count, begins, got_a, got_b, msg_x
     )
-    wind_out, heat_out, soot_out, scale, gain, moved = last(
-        high, low, own_low, own_high, count, got_a, got_b, loads, spray_0, spray_1, nxt, nxt_nu, keep
+    fields, scale, gain, moved = last(
+        got_x, got_y, own_low, own_high, count, got_a, got_b, loads, spray_0, spray_1, nxt, nxt_nu, keep
     )
-    mass_out = droplets(mass, above, scale, gain, moved)
+    wind_out, heat_out, soot_out, mass_out = droplets(fields, mass, above, scale, gain, moved)
     return wind_out, heat_out, soot_out, mass_out, count_out
 
 

time: 34.9 us -> 32.2 us (0.923)
  the two profiles are of different devices: /device:TPU:446 before, /device:TPU:160 now
where the time goes in v4:
time: 32.2 us; the launch traced here: 32 us
  starting transfers between devices  23.8 us (74%)
  Pallas kernels  4.71 us (15%)
  waiting for transfers between devices  2.76 us (9%)
  between operations  0.72 us (2%)
    ppermute x1, starting transfers between devices, local(): lax.ppermute(msg_y, 'sec', [(i, (i + 1 ^ 1) - 1) for i in range(1, width...  11.5 us
    ppermute x1, starting transfers between devices, local(): got_b = lax.ppermute(msg_b, 'tun', pairs_b)  6.1 us
    ppermute x1, waiting for transfers between devices, local(): lax.ppermute(msg_y, 'sec', [(i, (i + 1 ^ 1) - 1) for i in range(1, width...  2.73 us
    ppermute x1, starting transfers between devices, local(): lax.ppermute(pack_mass(mass, begins), 'tun', [(i, i + 1) for i in range(c...  2.41 us
    ppermute x1, starting transfers between devices, local(): got_a = lax.ppermute(msg_a, 'tun', pairs_a)  1.92 us
    ppermute x1, starting transfers between devices, local(): got_x = lax.ppermute(msg_x, 'sec', [(i, i ^ 1) for i in range(width)])  1.92 us
    pallas_call x1, Pallas kernels, pack_tun(): pl.pallas_call(pack_tun_kernel, out_shape=(msg, msg) + tuple((pltpu.VMEM(...  1.42 us
    pallas_call x1, Pallas kernels, first(): pl.pallas_call(first_kernel, out_shape=(jax.ShapeDtypeStruct(count.shape,...  1.25 us
  transfers between devices with their start and end apart: 5, of which 1 were waited for; matrix products, arithmetic and copies ran while one was open for 0% of the time, Pallas kernels for 7%

profile of v4, /device:TPU:160, one launch (start us, length us, event | category | flops | bytes accessed | tf_op | source)
XLA Modules:
  0.0 32.0 jit_solution(5080019914306240932)
XLA Ops:
  0.6 1.4 %pack_tun.1 = (f32[8,2,16,128]{3,2,1,0:T(8,128)S(1)}, f32[8,2,16,128]{3,2,1,0:T(8,128)S(1)}, f32[3,8,16,128]{3,2,1,0:T(8,128)S(1)}, f32[8,16,128]{2,1,0:T(8,128)...) custom-call(s32[8]{0:T(128)} %onset.1, ...), custom_call_target="tpu_custom_call" | custom-call | tf_op jit(solution)/shard_map/pack_tun/pallas_call | solution.py:106
  2.1 6.1 %collective-permute-start = (f32[8,2,16,128]{3,2,1,0:T(8,128)S(1)}, f32[8,2,16,128]{3,2,1,0:T(8,128)S(1)}, u32[]{:S(2)}, u32[]{:S(2)}) collective-permute-start(f32[8,2,16,128]{3,2,1,0:T(8,128)S(1)} %get-tuple-element.32), channel_id=1, source_target_pairs={{4,8},{8,4},{12,16},{16,12},{20,24},{24,20},{28,32},{32,28},{36,40... | collective-permute-start | bytes 393224 | tf_op jit(solution)/shard_map/ppermute | solution.py:545
  8.2 1.9 %collective-permute-start.1 = (f32[8,2,16,128]{3,2,1,0:T(8,128)S(1)}, f32[8,2,16,128]{3,2,1,0:T(8,128)S(1)}, u32[]{:S(2)}, u32[]{:S(2)}) collective-permute-start(f32[8,2,16,128]{3,2,1,0:T(8,128)S(1)} %get-tuple-element.33), channel_id=1, source_target_pairs={{0,4},{4,0},{8,12},{12,8},{16,20},{20,16},{24,28},{28,24},{32,36},... | collective-permute-start | bytes 393224 | tf_op jit(solution)/shard_map/ppermute | solution.py:546
  10.1 2.4 %collective-permute-start.4 = (f32[16,2,16,128]{3,2,1,0:T(8,128)S(1)}, f32[16,2,16,128]{3,2,1,0:T(8,128)S(1)}, u32[]{:S(2)}, u32[]{:S(2)}) collective-permute-start(f32[16,2,16,128]{3,2,1,0:T(8,128)S(1)} %pack_mass.1), channel_id=1, source_target_pairs={{0,4},{4,8},{8,12},{12,16},{16,20},{20,24},{24,28},{28,32},{32,36}... | collective-permute-start | bytes 786440 | tf_op jit(solution)/shard_map/ppermute | solution.py:550
  12.5 0.0 collective-permute-done.got_b
  12.6 0.0 collective-permute-done.1.got_a
  12.6 0.1 pack_sec.1
  12.7 1.9 %collective-permute-start.2 = (f32[13,8,128]{2,1,0:T(8,128)S(1)}, f32[13,8,128]{2,1,0:T(8,128)S(1)}, u32[]{:S(2)}, u32[]{:S(2)}) collective-permute-start(f32[13,8,128]{2,1,0:T(8,128)S(1)} %get-tuple-element.40.after), channel_id=1, source_target_pairs={{0,1},{1,0},{2,3},{3,2},{4,5},{5,4},{6,7},{7,6},{8,9},{9,8},{10,11... | collective-permute-start | bytes 159752 | tf_op jit(solution)/shard_map/ppermute | solution.py:548
  14.6 11.5 %collective-permute-start.3 = (f32[13,8,128]{2,1,0:T(8,128)S(1)}, f32[13,8,128]{2,1,0:T(8,128)S(1)}, u32[]{:S(2)}, u32[]{:S(2)}) collective-permute-start(f32[13,8,128]{2,1,0:T(8,128)S(1)} %get-tuple-element.41), channel_id=1, source_target_pairs={{1,2},{2,1},{5,6},{6,5},{9,10},{10,9},{13,14},{14,13},{17,18},{18,... | collective-permute-start | bytes 159752 | tf_op jit(solution)/shard_map/ppermute | solution.py:549
  26.1 1.2 %first_substep.1 = (s32[8,16,128]{2,1,0:T(8,128)}, f32[1600,128]{1,0:T(8,128)S(1)}, f32[320,128]{1,0:T(8,128)S(1)}, f32[144,128]{1,0:T(8,128)S(1)}, f32[9,16,128...) custom-call(f32[3,8,16,128]{3,2,1,0:T(8,128)S(1)} %get-tuple-element.34.wind, ...), custom_call_target="tpu_custom_call" | custom-call | tf_op jit(solution)/shard_map/first_substep/pallas_call | solution.py:329
  27.4 0.0 collective-permute-done.2.got_x
  27.4 2.7 %collective-permute-done.3.got_y = f32[13,8,128]{2,1,0:T(8,128)S(1)} collective-permute-done((f32[13,8,128]{2,1,0:T(8,128)S(1)}, f32[13,8,128]{2,1,0:T(8,128)S(1)}, u32[]{:S(2)}, u32[]{:S(2)}) %collective-permute-start.3) | collective-permute-done | bytes 53280 | tf_op jit(solution)/shard_map/ppermute | solution.py:549
  30.1 0.7 %last_substep.1 = (f32[5,8,16,128]{3,2,1,0:T(8,128)S(1)}, f32[8,16,128]{2,1,0:T(8,128)S(1)}, f32[8,16,128]{2,1,0:T(8,128)S(1)}, s32[8,16,128]{2,1,0:T(8,128)S(1)...) custom-call(f32[13,8,128]{2,1,0:T(8,128)S(1)} %collective-permute-do, ...), custom_call_target="tpu_custom_call", output_to_operand_aliasing={{4}: (10, {}), {5}: (11, {}), {6}: (12, {})} | custom-call | flops 1000000000 | bytes 1000000 | tf_op jit(solution)/shard_map/last_substep/pallas_call | solution.py:486
  30.8 0.0 collective-permute-done.4.above
  30.8 1.2 %droplets.1 = (f32[3,8,16,128]{3,2,1,0:T(8,128)}, f32[8,16,128]{2,1,0:T(8,128)}, f32[8,16,128]{2,1,0:T(8,128)}, f32[16,8,16,128]{3,2,1,0:T(8,128)}) custom-call(f32[5,8,16,128]{3,2,1,0:T(8,128)S(1)} %get-tuple-element.50.fields, f32[16,8,16,128]{3,2,1,0:T(8,128)S(1)} %get-tuple-element.37.mass, f32[16,2,16,128]{3,2,1,0:T(8,128)S(1)} %collective-permute-done.4.above, ...), custom_call_target="tpu_custom_call" | custom-call | tf_op jit(solution)/shard_map/droplets/pallas_call | solution.py:524
  (1 shorter events, 0.0 us)
Async XLA Ops:
  2.1 10.5 %collective-permute-start = (f32[8,2,16,128]{3,2,1,0:T(8,128)S(1)}, f32[8,2,16,128]{3,2,1,0:T(8,128)S(1)}, u32[]{:S(2)}, u32[]{:S(2)}) collective-permute-start(f32[8,2,16,128]{3,2,1,0:T(8,128)S(1)} %get-tuple-element.32), channel_id=1, source_target_pairs={{4,8},{8,4},{12,16},{16,12},{20,24},{24,20},{28,32},{32,28},{36,40... | collective-permute-start | bytes 393224 | tf_op jit(solution)/shard_map/ppermute | solution.py:545
  8.2 4.4 %collective-permute-start.1 = (f32[8,2,16,128]{3,2,1,0:T(8,128)S(1)}, f32[8,2,16,128]{3,2,1,0:T(8,128)S(1)}, u32[]{:S(2)}, u32[]{:S(2)}) collective-permute-start(f32[8,2,16,128]{3,2,1,0:T(8,128)S(1)} %get-tuple-element.33), channel_id=1, source_target_pairs={{0,4},{4,0},{8,12},{12,8},{16,20},{20,16},{24,28},{28,24},{32,36},... | collective-permute-start | bytes 393224 | tf_op jit(solution)/shard_map/ppermute | solution.py:546
  10.1 20.7 %collective-permute-start.4 = (f32[16,2,16,128]{3,2,1,0:T(8,128)S(1)}, f32[16,2,16,128]{3,2,1,0:T(8,128)S(1)}, u32[]{:S(2)}, u32[]{:S(2)}) collective-permute-start(f32[16,2,16,128]{3,2,1,0:T(8,128)S(1)} %pack_mass.1), channel_id=1, source_target_pairs={{0,4},{4,8},{8,12},{12,16},{16,20},{20,24},{24,28},{28,32},{32,36}... | collective-permute-start | bytes 786440 | tf_op jit(solution)/shard_map/ppermute | solution.py:550
  12.7 14.7 %collective-permute-start.2 = (f32[13,8,128]{2,1,0:T(8,128)S(1)}, f32[13,8,128]{2,1,0:T(8,128)S(1)}, u32[]{:S(2)}, u32[]{:S(2)}) collective-permute-start(f32[13,8,128]{2,1,0:T(8,128)S(1)} %get-tuple-element.40.after), channel_id=1, source_target_pairs={{0,1},{1,0},{2,3},{3,2},{4,5},{5,4},{6,7},{7,6},{8,9},{9,8},{10,11... | collective-permute-start | bytes 159752 | tf_op jit(solution)/shard_map/ppermute | solution.py:548
  14.6 15.5 %collective-permute-start.3 = (f32[13,8,128]{2,1,0:T(8,128)S(1)}, f32[13,8,128]{2,1,0:T(8,128)S(1)}, u32[]{:S(2)}, u32[]{:S(2)}) collective-permute-start(f32[13,8,128]{2,1,0:T(8,128)S(1)} %get-tuple-element.41), channel_id=1, source_target_pairs={{1,2},{2,1},{5,6},{6,5},{9,10},{10,9},{13,14},{14,13},{17,18},{18,... | collective-permute-start | bytes 159752 | tf_op jit(solution)/shard_map/ppermute | solution.py:549

commit v5 on v4

--- a/solution.py
+++ b/solution.py
@@ -24,7 +24,7 @@
 ROW = 8
 
 
-FIRST_COST, LAST_COST = 0, 1
+FIRST_COST, LAST_COST = 3, 0
 
 
 def cost(units):
@@ -62,7 +62,7 @@
 
 def pack_tun_kernel(
     onset, wind, heat, soot, mass, count, label,
-    msg_b, msg_a, winds, heats, soots, masses, counts, begins, labels, onsets, sems,
+    msg_b, msg_a, winds, heats, soots, tops, counts, begins, labels, onsets, sems,
 ):
     depth = heat.shape[0]
     odd = lax.axis_index("tun") % 2 == 1
@@ -71,7 +71,7 @@
     start_b = top - start_a
     onset_copy, label_copy, count_copy, *others = copies(
         [
-            (onset, onsets), (label, labels), (count, counts), (mass, masses), (wind, winds), (heat, heats), (soot, soots)
+            (onset, onsets), (label, labels), (count, counts), (mass.at[:, top:depth], tops), (wind, winds), (heat, heats), (soot, soots)
         ],
         sems,
     )
@@ -82,7 +82,7 @@
     count_copy.wait()
     others[0].wait()
     held = counts[top:depth]
-    total = live_sum([masses[k, top:depth] for k in range(masses.shape[0])], held)
+    total = live_sum([tops[k] for k in range(tops.shape[0])], held)
     for copy in others[1:]:
         copy.wait()
     for start, msg in ((start_b, msg_b), (start_a, msg_a)):
@@ -105,7 +105,10 @@
     msg = pltpu.VMEM((NF + 3, 2) + heat.shape[1:], F32)
     return pl.pallas_call(
         pack_tun_kernel,
-        out_shape=(msg, msg) + tuple(pltpu.VMEM(a.shape, a.dtype) for a in arrays),
+        out_shape=(msg, msg)
+        + tuple(pltpu.VMEM(a.shape, a.dtype) for a in arrays[:3])
+        + (pltpu.VMEM((mass.shape[0], 2) + mass.shape[2:], F32),)
+        + tuple(pltpu.VMEM(a.shape, a.dtype) for a in arrays[4:]),
         in_specs=[HBM] * 7,
         out_specs=(VMEM,) * 8,
         scratch_shapes=[
@@ -118,16 +121,14 @@
     )(*in_hbm(onset, *arrays))
 
 
-def pack_mass_kernel(mass, after, msg):
-    depth = mass.shape[1]
-    for k in range(mass.shape[0]):
-        msg[k] = mass[k, depth - 2 : depth]
+def pack_mass_kernel(tops, after, msg):
+    msg[...] = tops[...]
 
 
 def pack_mass(mass, after):
     return pl.pallas_call(
         pack_mass_kernel,
-        out_shape=pltpu.VMEM((mass.shape[0], 2) + mass.shape[2:], F32),
+        out_shape=pltpu.VMEM(mass.shape, F32),
         in_specs=[VMEM] * 2,
         out_specs=VMEM,
         compiler_params=LIMIT,
@@ -352,11 +353,11 @@
 
 
 def last_kernel(
-    got_x, got_y, own_low, own_high, count, got_a, got_b, loads, spray_0, spray_1, nxt_in, nxt_nu_in, keep_in,
-    fields, scale, gain, moved, nxt, nxt_nu, keep,
-    beside, low, high,
+    got_x, got_y, above, own_low, own_high, mass, count, got_a, got_b, loads, spray_0, spray_1, nxt_in, nxt_nu_in, keep_in,
+    wind_out, heat_out, soot_out, mass_out, nxt, nxt_nu, keep,
+    beside, low, high, fields, masses, sems,
 ):
-    depth, rows, lanes = count.shape
+    slots, depth, rows, lanes = mass.shape
     tall = rows + 2 * ROW
     planes = depth + 2
     tun, sec = lax.axis_index("tun"), lax.axis_index("sec")
@@ -449,6 +450,8 @@
     def at(ref, plane, shift=0):
         return ref[plane * tall + ROW + shift : plane * tall + ROW + shift + rows, :]
 
+    pending = []
+    half = depth // 2
     for x in range(depth):
         centre = [at(nxt, f * planes + x + 1) for f in range(NF)]
         nu = at(nxt_nu, x + 1)
@@ -476,85 +479,75 @@
         new[4] = new[4] / (1.0 + scavenge * load)
         for f in range(NF):
             fields[f, x] = new[f]
-        moved[x] = held
-        scale[x] = kept * (1.0 - evap)
-        gain[x] = (spray_0[x] * kept + sprays) * (1.0 - evap)
-
-def last(got_x, got_y, own_low, own_high, count, got_a, got_b, loads, spray_0, spray_1, nxt, nxt_nu, keep):
-    block = count.shape
-    operands = on_chip(got_x, got_y, own_low, own_high, count, got_a, got_b, loads, spray_0, spray_1, nxt, nxt_nu, keep)
-    return pl.pallas_call(
-        last_kernel,
-        out_shape=(
-            pltpu.VMEM((NF,) + block, F32),
-            pltpu.VMEM(block, F32),
-            pltpu.VMEM(block, F32),
-            pltpu.VMEM(block, jnp.int32),
-            pltpu.VMEM(nxt.shape, F32),
-            pltpu.VMEM(nxt_nu.shape, F32),
-            pltpu.VMEM(keep.shape, F32),
-        ),
-        in_specs=[VMEM] * 13,
-        out_specs=(VMEM,) * 7,
-        input_output_aliases={10: 4, 11: 5, 12: 6},
-        scratch_shapes=[pltpu.VMEM((2, NF, block[0] + 16, block[2]), F32)] + [pltpu.VMEM(got_x.shape, F32)] * 2,
-        compiler_params=LIMIT,
-        cost_estimate=cost(LAST_COST),
-        name="last_substep",
-    )(*operands)[:4]
-
-
-def droplets_kernel(fields, mass, above, scale, gain, moved, wind_out, heat_out, soot_out, mass_out, masses, sems):
-    slots, depth = mass.shape[:2]
-    pending = copies([(fields.at[0:3], wind_out), (fields.at[3], heat_out), (fields.at[4], soot_out)], sems)
-    for x in range(depth):
-        held, by, plus = moved[x], scale[x], gain[x]
+        by = kept * (1.0 - evap)
+        plus = (spray_0[x] * kept + sprays) * (1.0 - evap)
         for k in range(slots):
             before = above[k, x] if x < 2 else mass[k, x - 2]
             masses[k, x] = jnp.where(held > k, before * by + plus, before)
-        copy = pltpu.make_async_copy(masses.at[:, x], mass_out.at[:, x], sems.at[3 + x])
+        copy = pltpu.make_async_copy(masses.at[:, x], mass_out.at[:, x], sems.at[x])
         copy.start()
         pending.append(copy)
+        if x % half == half - 1:
+            done = slice(x + 1 - half, x + 1)
+            pending += copies(
+                [
+                    (fields.at[0:3, done], wind_out.at[:, done]),
+                    (fields.at[3, done], heat_out.at[done]),
+                    (fields.at[4, done], soot_out.at[done]),
+                ],
+                sems.at[depth + 3 * (x // half) : depth + 3 * (x // half) + 3],
+            )
     for copy in pending:
         copy.wait()
 
-
-def droplets(fields, mass, above, scale, gain, moved):
-    block = moved.shape
+def last(got_x, got_y, above, own_low, own_high, mass, count, got_a, got_b, loads, spray_0, spray_1, nxt, nxt_nu, keep):
+    block = count.shape
+    operands = on_chip(got_x, got_y, above, own_low, own_high, mass, count, got_a, got_b, loads, spray_0, spray_1, nxt, nxt_nu, keep)
     return pl.pallas_call(
-        droplets_kernel,
+        last_kernel,
         out_shape=(
             jax.ShapeDtypeStruct((3,) + block, F32),
             jax.ShapeDtypeStruct(block, F32),
             jax.ShapeDtypeStruct(block, F32),
             jax.ShapeDtypeStruct(mass.shape, F32),
+            pltpu.VMEM(nxt.shape, F32),
+            pltpu.VMEM(nxt_nu.shape, F32),
+            pltpu.VMEM(keep.shape, F32),
         ),
-        in_specs=[VMEM] * 6,
-        out_specs=(ANY,) * 4,
-        scratch_shapes=[pltpu.VMEM(mass.shape, F32), pltpu.SemaphoreType.DMA((3 + block[0],))],
+        in_specs=[VMEM] * 15,
+        out_specs=(ANY,) * 4 + (VMEM,) * 3,
+        input_output_aliases={12: 4, 13: 5, 14: 6},
+        scratch_shapes=[
+            pltpu.VMEM((2, NF, block[0] + 16, block[2]), F32),
+            pltpu.VMEM(got_x.shape, F32),
+            pltpu.VMEM(got_x.shape, F32),
+            pltpu.VMEM((NF,) + block, F32),
+            pltpu.VMEM(mass.shape, F32),
+            pltpu.SemaphoreType.DMA((6 + block[0],)),
+        ],
         compiler_params=LIMIT,
-        name="droplets",
-    )(*on_chip(fields, mass, above, scale, gain, moved))
+        cost_estimate=cost(LAST_COST),
+        name="last_substep",
+    )(*operands)[:4]
 
 
 def local(wind, heat, soot, mass, count, label, onset):
     chain, width = lax.axis_size("tun"), lax.axis_size("sec")
     pairs_a = [(i, i ^ 1) for i in range(chain)]
     pairs_b = [(i, ((i + 1) ^ 1) - 1) for i in range(1, chain - 1)]
-    msg_b, msg_a, wind, heat, soot, mass, count, begins = pack_tun(onset, wind, heat, soot, mass, count, label)
+    msg_b, msg_a, wind, heat, soot, tops, count, begins = pack_tun(onset, wind, heat, soot, mass, count, label)
     got_b = lax.ppermute(msg_b, "tun", pairs_b)
     got_a = lax.ppermute(msg_a, "tun", pairs_a)
     msg_x, msg_y, own_low, own_high = pack_sec(wind, heat, soot, mass, count, begins, got_a, got_b)
     got_x = lax.ppermute(msg_x, "sec", [(i, i ^ 1) for i in range(width)])
     got_y = lax.ppermute(msg_y, "sec", [(i, ((i + 1) ^ 1) - 1) for i in range(1, width - 1)])
-    above = lax.ppermute(pack_mass(mass, begins), "tun", [(i, i + 1) for i in range(chain - 1)])
+    above = lax.ppermute(pack_mass(tops, begins), "tun", [(i, i + 1) for i in range(chain - 1)])
     count_out, nxt, nxt_nu, keep, loads, spray_0, spray_1 = first(
-        wind, heat, soot, mass, count, begins, got_a, got_b, msg_x
+        wind, heat, soot, mass, count, begins, got_a, got_b, own_low
     )
-    fields, scale, gain, moved = last(
-        got_x, got_y, own_low, own_high, count, got_a, got_b, loads, spray_0, spray_1, nxt, nxt_nu, keep
+    wind_out, heat_out, soot_out, mass_out = last(
+        got_x, got_y, above, own_low, own_high, mass, count, got_a, got_b, loads, spray_0, spray_1, nxt, nxt_nu, keep
     )
-    wind_out, heat_out, soot_out, mass_out = droplets(fields, mass, above, scale, gain, moved)
     return wind_out, heat_out, soot_out, mass_out, count_out
 
 

time: 32.2 us -> 31.9 us (level)
  Pallas kernels: 4.71 us -> 4.36 us
    pallas_call x3 -> x2, Pallas kernels: 1.9 us -> 1.71 us  [the longest x1 1.69 us: last(): pl.pallas_call(last_kernel, out_shape=(jax.ShapeDtypeStruct((3,) + block,...]
  transfers between devices with their start and end apart: 5 -> 5, of which waited for: 1 -> 1; matrix products, arithmetic and copies ran while one was open for 0% -> 0% of each run, Pallas kernels for 7% -> 4%
where the time goes in v5:
time: 31.9 us; the launch traced here: 31.7 us
  starting transfers between devices  23.8 us (75%)
  Pallas kernels  4.36 us (14%)
  waiting for transfers between devices  2.77 us (9%)
  between operations  0.72 us (2%)
    ppermute x1, starting transfers between devices, local(): lax.ppermute(msg_y, 'sec', [(i, (i + 1 ^ 1) - 1) for i in range(1, width...  11.5 us
    ppermute x1, starting transfers between devices, local(): got_b = lax.ppermute(msg_b, 'tun', pairs_b)  6.1 us
    ppermute x1, waiting for transfers between devices, local(): lax.ppermute(msg_y, 'sec', [(i, (i + 1 ^ 1) - 1) for i in range(1, width...  2.74 us
    ppermute x1, starting transfers between devices, local(): lax.ppermute(pack_mass(tops, begins), 'tun', [(i, i + 1) for i in range(c...  2.41 us
    ppermute x1, starting transfers between devices, local(): got_a = lax.ppermute(msg_a, 'tun', pairs_a)  1.92 us
    ppermute x1, starting transfers between devices, local(): got_x = lax.ppermute(msg_x, 'sec', [(i, i ^ 1) for i in range(width)])  1.92 us
    pallas_call x1, Pallas kernels, last(): pl.pallas_call(last_kernel, out_shape=(jax.ShapeDtypeStruct((3,) + block,...  1.69 us
    pallas_call x1, Pallas kernels, pack_tun(): pl.pallas_call(pack_tun_kernel, out_shape=(msg, msg) + tuple((pltpu.VMEM(...  1.27 us
  transfers between devices with their start and end apart: 5, of which 1 were waited for; matrix products, arithmetic and copies ran while one was open for 0% of the time, Pallas kernels for 4%

profile of v5, /device:TPU:160, one launch (start us, length us, event | category | flops | bytes accessed | tf_op | source)
XLA Modules:
  0.0 31.7 jit_solution(16922790134049750712)
XLA Ops:
  0.6 0.0 copy-start
  0.6 1.3 %pack_tun.1 = (f32[8,2,16,128]{3,2,1,0:T(8,128)S(1)}, f32[8,2,16,128]{3,2,1,0:T(8,128)S(1)}, f32[3,8,16,128]{3,2,1,0:T(8,128)S(1)}, f32[8,16,128]{2,1,0:T(8,128)...) custom-call(s32[8]{0:T(128)} %onset.1, ...), custom_call_target="tpu_custom_call" | custom-call | tf_op jit(solution)/shard_map/pack_tun/pallas_call | solution.py:106
  1.9 6.1 %collective-permute-start = (f32[8,2,16,128]{3,2,1,0:T(8,128)S(1)}, f32[8,2,16,128]{3,2,1,0:T(8,128)S(1)}, u32[]{:S(2)}, u32[]{:S(2)}) collective-permute-start(f32[8,2,16,128]{3,2,1,0:T(8,128)S(1)} %get-tuple-element.28), channel_id=1, source_target_pairs={{4,8},{8,4},{12,16},{16,12},{20,24},{24,20},{28,32},{32,28},{36,40... | collective-permute-start | bytes 393224 | tf_op jit(solution)/shard_map/ppermute | solution.py:539
  8.0 1.9 %collective-permute-start.1 = (f32[8,2,16,128]{3,2,1,0:T(8,128)S(1)}, f32[8,2,16,128]{3,2,1,0:T(8,128)S(1)}, u32[]{:S(2)}, u32[]{:S(2)}) collective-permute-start(f32[8,2,16,128]{3,2,1,0:T(8,128)S(1)} %get-tuple-element.29), channel_id=1, source_target_pairs={{0,4},{4,0},{8,12},{12,8},{16,20},{20,16},{24,28},{28,24},{32,36},... | collective-permute-start | bytes 393224 | tf_op jit(solution)/shard_map/ppermute | solution.py:540
  10.0 2.4 %collective-permute-start.4 = (f32[16,2,16,128]{3,2,1,0:T(8,128)S(1)}, f32[16,2,16,128]{3,2,1,0:T(8,128)S(1)}, u32[]{:S(2)}, u32[]{:S(2)}) collective-permute-start(f32[16,2,16,128]{3,2,1,0:T(8,128)S(1)} %pack_mass.1), channel_id=1, source_target_pairs={{0,4},{4,8},{8,12},{12,16},{16,20},{20,24},{24,28},{28,32},{32,36}... | collective-permute-start | bytes 786440 | tf_op jit(solution)/shard_map/ppermute | solution.py:544
  12.4 0.0 collective-permute-done.got_b
  12.4 0.0 collective-permute-done.1.got_a
  12.4 0.0 copy-done
  12.4 0.1 pack_sec.1
  12.6 1.9 %collective-permute-start.2 = (f32[13,8,128]{2,1,0:T(8,128)S(1)}, f32[13,8,128]{2,1,0:T(8,128)S(1)}, u32[]{:S(2)}, u32[]{:S(2)}) collective-permute-start(f32[13,8,128]{2,1,0:T(8,128)S(1)} %get-tuple-element.35), channel_id=1, source_target_pairs={{0,1},{1,0},{2,3},{3,2},{4,5},{5,4},{6,7},{7,6},{8,9},{9,8},{10,11... | collective-permute-start | bytes 159752 | tf_op jit(solution)/shard_map/ppermute | solution.py:542
  14.5 11.5 %collective-permute-start.3 = (f32[13,8,128]{2,1,0:T(8,128)S(1)}, f32[13,8,128]{2,1,0:T(8,128)S(1)}, u32[]{:S(2)}, u32[]{:S(2)}) collective-permute-start(f32[13,8,128]{2,1,0:T(8,128)S(1)} %get-tuple-element.36), channel_id=1, source_target_pairs={{1,2},{2,1},{5,6},{6,5},{9,10},{10,9},{13,14},{14,13},{17,18},{18,... | collective-permute-start | bytes 159752 | tf_op jit(solution)/shard_map/ppermute | solution.py:543
  26.0 1.2 %first_substep.1 = (s32[8,16,128]{2,1,0:T(8,128)}, f32[1600,128]{1,0:T(8,128)S(1)}, f32[320,128]{1,0:T(8,128)S(1)}, f32[144,128]{1,0:T(8,128)S(1)}, f32[9,16,128...) custom-call(f32[3,8,16,128]{3,2,1,0:T(8,128)S(1)} %get-tuple-element.30.wind, ...), custom_call_target="tpu_custom_call" | custom-call | flops 3000000000 | bytes 3000000 | tf_op jit(solution)/shard_map/first_substep/pallas_call | solution.py:330
  27.2 0.0 collective-permute-done.2.got_x
  27.2 2.7 %collective-permute-done.3.got_y = f32[13,8,128]{2,1,0:T(8,128)S(1)} collective-permute-done((f32[13,8,128]{2,1,0:T(8,128)S(1)}, f32[13,8,128]{2,1,0:T(8,128)S(1)}, u32[]{:S(2)}, u32[]{:S(2)}) %collective-permute-start.3) | collective-permute-done | bytes 53280 | tf_op jit(solution)/shard_map/ppermute | solution.py:543
  30.0 0.0 collective-permute-done.4.above
  30.0 1.7 %last_substep.1 = (f32[3,8,16,128]{3,2,1,0:T(8,128)}, f32[8,16,128]{2,1,0:T(8,128)}, f32[8,16,128]{2,1,0:T(8,128)}, f32[16,8,16,128]{3,2,1,0:T(8,128)}, f32[1600...) custom-call(f32[13,8,128]{2,1,0:T(8,128)S(1)} %collective-permute-do, ...), custom_call_target="tpu_custom_call", output_to_operand_aliasing={{4}: (12, {}), {5}: (13, {}), {6}: (14, {})} | custom-call | tf_op jit(solution)/shard_map/last_substep/pallas_call | solution.py:506
  (1 shorter events, 0.0 us)
Async XLA Ops:
  0.6 11.8 %copy-start = (f32[16,8,16,128]{3,2,1,0:T(8,128)S(1)}, f32[16,8,16,128]{3,2,1,0:T(8,128)}, u32[]{:S(2)}) copy-start(f32[16,8,16,128]{3,2,1,0:T(8,128)} %mass.7) | copy-start | bytes 3145732
  1.9 10.5 %collective-permute-start = (f32[8,2,16,128]{3,2,1,0:T(8,128)S(1)}, f32[8,2,16,128]{3,2,1,0:T(8,128)S(1)}, u32[]{:S(2)}, u32[]{:S(2)}) collective-permute-start(f32[8,2,16,128]{3,2,1,0:T(8,128)S(1)} %get-tuple-element.28), channel_id=1, source_target_pairs={{4,8},{8,4},{12,16},{16,12},{20,24},{24,20},{28,32},{32,28},{36,40... | collective-permute-start | bytes 393224 | tf_op jit(solution)/shard_map/ppermute | solution.py:539
  8.0 4.4 %collective-permute-start.1 = (f32[8,2,16,128]{3,2,1,0:T(8,128)S(1)}, f32[8,2,16,128]{3,2,1,0:T(8,128)S(1)}, u32[]{:S(2)}, u32[]{:S(2)}) collective-permute-start(f32[8,2,16,128]{3,2,1,0:T(8,128)S(1)} %get-tuple-element.29), channel_id=1, source_target_pairs={{0,4},{4,0},{8,12},{12,8},{16,20},{20,16},{24,28},{28,24},{32,36},... | collective-permute-start | bytes 393224 | tf_op jit(solution)/shard_map/ppermute | solution.py:540
  10.0 20.0 %collective-permute-start.4 = (f32[16,2,16,128]{3,2,1,0:T(8,128)S(1)}, f32[16,2,16,128]{3,2,1,0:T(8,128)S(1)}, u32[]{:S(2)}, u32[]{:S(2)}) collective-permute-start(f32[16,2,16,128]{3,2,1,0:T(8,128)S(1)} %pack_mass.1), channel_id=1, source_target_pairs={{0,4},{4,8},{8,12},{12,16},{16,20},{20,24},{24,28},{28,32},{32,36}... | collective-permute-start | bytes 786440 | tf_op jit(solution)/shard_map/ppermute | solution.py:544
  12.6 14.7 %collective-permute-start.2 = (f32[13,8,128]{2,1,0:T(8,128)S(1)}, f32[13,8,128]{2,1,0:T(8,128)S(1)}, u32[]{:S(2)}, u32[]{:S(2)}) collective-permute-start(f32[13,8,128]{2,1,0:T(8,128)S(1)} %get-tuple-element.35), channel_id=1, source_target_pairs={{0,1},{1,0},{2,3},{3,2},{4,5},{5,4},{6,7},{7,6},{8,9},{9,8},{10,11... | collective-permute-start | bytes 159752 | tf_op jit(solution)/shard_map/ppermute | solution.py:542
  14.5 15.5 %collective-permute-start.3 = (f32[13,8,128]{2,1,0:T(8,128)S(1)}, f32[13,8,128]{2,1,0:T(8,128)S(1)}, u32[]{:S(2)}, u32[]{:S(2)}) collective-permute-start(f32[13,8,128]{2,1,0:T(8,128)S(1)} %get-tuple-element.36), channel_id=1, source_target_pairs={{1,2},{2,1},{5,6},{6,5},{9,10},{10,9},{13,14},{14,13},{17,18},{18,... | collective-permute-start | bytes 159752 | tf_op jit(solution)/shard_map/ppermute | solution.py:543

commit v6 on v5

--- a/solution.py
+++ b/solution.py
@@ -62,36 +62,32 @@
 
 def pack_tun_kernel(
     onset, wind, heat, soot, mass, count, label,
-    msg_b, msg_a, winds, heats, soots, tops, counts, begins, labels, onsets, sems,
+    msg_b, msg_a, tops, begins, held_ref, labels, onsets, sems,
 ):
     depth = heat.shape[0]
     odd = lax.axis_index("tun") % 2 == 1
     top = depth - 2
     start_a = jnp.where(odd, 0, top)
     start_b = top - start_a
-    onset_copy, label_copy, count_copy, *others = copies(
-        [
-            (onset, onsets), (label, labels), (count, counts), (mass.at[:, top:depth], tops), (wind, winds), (heat, heats), (soot, soots)
-        ],
-        sems,
-    )
+    pairs = [
+        (onset, onsets), (label, labels), (count.at[top:depth], held_ref), (mass.at[:, top:depth], tops)
+    ]
+    for start, msg in ((start_b, msg_b), (start_a, msg_a)):
+        here = pl.ds(start, 2)
+        pairs += [(wind.at[:, here], msg.at[0:3]), (heat.at[here], msg.at[3]), (soot.at[here], msg.at[4])]
+    onset_copy, label_copy, count_copy, *others = copies(pairs, sems)
     onset_copy.wait()
     label_copy.wait()
     for x in range(depth):
         begins[x] = onset_of(labels[x], onsets)
     count_copy.wait()
+    held = held_ref[...]
     others[0].wait()
-    held = counts[top:depth]
     total = live_sum([tops[k] for k in range(tops.shape[0])], held)
     for copy in others[1:]:
         copy.wait()
     for start, msg in ((start_b, msg_b), (start_a, msg_a)):
-        here = pl.ds(start, 2)
-        for f in range(3):
-            msg[f] = winds[f, here]
-        msg[3] = heats[here]
-        msg[4] = soots[here]
-        msg[NF] = begins[here].astype(F32)
+        msg[NF] = begins[pl.ds(start, 2)].astype(F32)
         msg[NF + 1] = held.astype(F32)
         msg[NF + 2] = total
 
@@ -105,16 +101,19 @@
     msg = pltpu.VMEM((NF + 3, 2) + heat.shape[1:], F32)
     return pl.pallas_call(
         pack_tun_kernel,
-        out_shape=(msg, msg)
-        + tuple(pltpu.VMEM(a.shape, a.dtype) for a in arrays[:3])
-        + (pltpu.VMEM((mass.shape[0], 2) + mass.shape[2:], F32),)
-        + tuple(pltpu.VMEM(a.shape, a.dtype) for a in arrays[4:]),
+        out_shape=(
+            msg,
+            msg,
+            pltpu.VMEM((mass.shape[0], 2) + mass.shape[2:], F32),
+            pltpu.VMEM(label.shape, jnp.int32),
+        ),
         in_specs=[HBM] * 7,
-        out_specs=(VMEM,) * 8,
+        out_specs=(VMEM,) * 4,
         scratch_shapes=[
+            pltpu.VMEM((2,) + label.shape[1:], jnp.int32),
             pltpu.VMEM(label.shape, jnp.int32),
             pltpu.SMEM(onset.shape, jnp.int32),
-            pltpu.SemaphoreType.DMA((7,)),
+            pltpu.SemaphoreType.DMA((10,)),
         ],
         compiler_params=LIMIT,
         name="pack_tun",
@@ -535,7 +534,7 @@
     chain, width = lax.axis_size("tun"), lax.axis_size("sec")
     pairs_a = [(i, i ^ 1) for i in range(chain)]
     pairs_b = [(i, ((i + 1) ^ 1) - 1) for i in range(1, chain - 1)]
-    msg_b, msg_a, wind, heat, soot, tops, count, begins = pack_tun(onset, wind, heat, soot, mass, count, label)
+    msg_b, msg_a, tops, begins = pack_tun(onset, wind, heat, soot, mass, count, label)
     got_b = lax.ppermute(msg_b, "tun", pairs_b)
     got_a = lax.ppermute(msg_a, "tun", pairs_a)
     msg_x, msg_y, own_low, own_high = pack_sec(wind, heat, soot, mass, count, begins, got_a, got_b)

time: 31.9 us -> 32.1 us (level)
  no operation moved by 1% of the time
where the time goes in v6:
time: 32.1 us; the launch traced here: 31.8 us
  starting transfers between devices  23.9 us (74%)
  Pallas kernels  4.31 us (13%)
  waiting for transfers between devices  2.76 us (9%)
  between operations  0.8 us (2%)
    ppermute x1, starting transfers between devices, local(): lax.ppermute(msg_y, 'sec', [(i, (i + 1 ^ 1) - 1) for i in range(1, width...  11.5 us
    ppermute x1, starting transfers between devices, local(): got_b = lax.ppermute(msg_b, 'tun', pairs_b)  6.1 us
    ppermute x1, waiting for transfers between devices, local(): lax.ppermute(msg_y, 'sec', [(i, (i + 1 ^ 1) - 1) for i in range(1, width...  2.74 us
    ppermute x1, starting transfers between devices, local(): lax.ppermute(pack_mass(tops, begins), 'tun', [(i, i + 1) for i in range(c...  2.54 us
    ppermute x1, starting transfers between devices, local(): got_x = lax.ppermute(msg_x, 'sec', [(i, i ^ 1) for i in range(width)])  1.92 us
    ppermute x1, starting transfers between devices, local(): got_a = lax.ppermute(msg_a, 'tun', pairs_a)  1.92 us
    pallas_call x1, Pallas kernels, last(): pl.pallas_call(last_kernel, out_shape=(jax.ShapeDtypeStruct((3,) + block,...  1.69 us
    pallas_call x1, Pallas kernels, first(): pl.pallas_call(first_kernel, out_shape=(jax.ShapeDtypeStruct(count.shape,...  1.23 us
  transfers between devices with their start and end apart: 5, of which 1 were waited for; matrix products, arithmetic and copies ran while one was open for 0% of the time, Pallas kernels for 4%

profile of v6, /device:TPU:160, one launch (start us, length us, event | category | flops | bytes accessed | tf_op | source)
XLA Modules:
  0.0 31.8 jit_solution(18237260584970098955)
XLA Ops:
  0.6 0.0 copy-start
  0.6 1.2 %pack_tun.1 = (f32[8,2,16,128]{3,2,1,0:T(8,128)S(1)}, f32[8,2,16,128]{3,2,1,0:T(8,128)S(1)}, f32[16,2,16,128]{3,2,1,0:T(8,128)S(1)}, s32[8,16,128]{2,1,0:T(8,128)S(1)}) custom-call(s32[8]{0:T(128)} %onset.1, f32[3,8,16,128]{3,2,1,0:T(8,128)} %wind.5, f32[8,16,128]{2,1,0:T(8,128)} %heat.5, f32[8,16,128]{2,1,0:T(8,128)} %soot.5, f32[16,8,16,128]{3,2,1,0:T(8,128)} %mass.7, ...), custom_call_target="tpu_custom_call" | custom-call | tf_op jit(solution)/shard_map/pack_tun/pallas_call | solution.py:102
  1.9 6.1 %collective-permute-start = (f32[8,2,16,128]{3,2,1,0:T(8,128)S(1)}, f32[8,2,16,128]{3,2,1,0:T(8,128)S(1)}, u32[]{:S(2)}, u32[]{:S(2)}) collective-permute-start(f32[8,2,16,128]{3,2,1,0:T(8,128)S(1)} %get-tuple-element.24), channel_id=1, source_target_pairs={{4,8},{8,4},{12,16},{16,12},{20,24},{24,20},{28,32},{32,28},{36,40... | collective-permute-start | bytes 393224 | tf_op jit(solution)/shard_map/ppermute | solution.py:538
  8.0 1.9 %collective-permute-start.1 = (f32[8,2,16,128]{3,2,1,0:T(8,128)S(1)}, f32[8,2,16,128]{3,2,1,0:T(8,128)S(1)}, u32[]{:S(2)}, u32[]{:S(2)}) collective-permute-start(f32[8,2,16,128]{3,2,1,0:T(8,128)S(1)} %get-tuple-element.25), channel_id=1, source_target_pairs={{0,4},{4,0},{8,12},{12,8},{16,20},{20,16},{24,28},{28,24},{32,36},... | collective-permute-start | bytes 393224 | tf_op jit(solution)/shard_map/ppermute | solution.py:539
  9.9 0.0 copy-start.1
  9.9 0.0 copy-start.2
  9.9 0.0 copy-start.3
  9.9 0.0 copy-start.4
  10.0 2.5 %collective-permute-start.4 = (f32[16,2,16,128]{3,2,1,0:T(8,128)S(1)}, f32[16,2,16,128]{3,2,1,0:T(8,128)S(1)}, u32[]{:S(2)}, u32[]{:S(2)}) collective-permute-start(f32[16,2,16,128]{3,2,1,0:T(8,128)S(1)} %pack_mass.1), channel_id=1, source_target_pairs={{0,4},{4,8},{8,12},{12,16},{16,20},{20,24},{24,28},{28,32},{32,36}... | collective-permute-start | bytes 786440 | tf_op jit(solution)/shard_map/ppermute | solution.py:543
  12.5 0.0 collective-permute-done.got_b
  12.5 0.0 collective-permute-done.1.got_a
  12.5 0.0 copy-done
  12.6 0.0 copy-done.1
  12.6 0.0 copy-done.2
  12.6 0.0 copy-done.3
  12.6 0.0 copy-done.4
  12.6 0.1 pack_sec.1
  12.7 1.9 %collective-permute-start.2 = (f32[13,8,128]{2,1,0:T(8,128)S(1)}, f32[13,8,128]{2,1,0:T(8,128)S(1)}, u32[]{:S(2)}, u32[]{:S(2)}) collective-permute-start(f32[13,8,128]{2,1,0:T(8,128)S(1)} %get-tuple-element.27), channel_id=1, source_target_pairs={{0,1},{1,0},{2,3},{3,2},{4,5},{5,4},{6,7},{7,6},{8,9},{9,8},{10,11... | collective-permute-start | bytes 159752 | tf_op jit(solution)/shard_map/ppermute | solution.py:541
  14.7 11.5 %collective-permute-start.3 = (f32[13,8,128]{2,1,0:T(8,128)S(1)}, f32[13,8,128]{2,1,0:T(8,128)S(1)}, u32[]{:S(2)}, u32[]{:S(2)}) collective-permute-start(f32[13,8,128]{2,1,0:T(8,128)S(1)} %get-tuple-element.28), channel_id=1, source_target_pairs={{1,2},{2,1},{5,6},{6,5},{9,10},{10,9},{13,14},{14,13},{17,18},{18,... | collective-permute-start | bytes 159752 | tf_op jit(solution)/shard_map/ppermute | solution.py:542
  26.1 1.2 %first_substep.1 = (s32[8,16,128]{2,1,0:T(8,128)}, f32[1600,128]{1,0:T(8,128)S(1)}, f32[320,128]{1,0:T(8,128)S(1)}, f32[144,128]{1,0:T(8,128)S(1)}, f32[9,16,128...) custom-call(f32[3,8,16,128]{3,2,1,0:T(8,128)S(1)} %copy-done.1, f32[8,16,128]{2,1,0:T(8,128)S(1)} %copy-done.3, ...), custom_call_target="tpu_custom_call" | custom-call | flops 3000000000 | bytes 3000000 | tf_op jit(solution)/shard_map/first_substep/pallas_call | solution.py:329
  27.4 0.0 collective-permute-done.2.got_x
  27.4 2.7 %collective-permute-done.3.got_y = f32[13,8,128]{2,1,0:T(8,128)S(1)} collective-permute-done((f32[13,8,128]{2,1,0:T(8,128)S(1)}, f32[13,8,128]{2,1,0:T(8,128)S(1)}, u32[]{:S(2)}, u32[]{:S(2)}) %collective-permute-start.3) | collective-permute-done | bytes 53280 | tf_op jit(solution)/shard_map/ppermute | solution.py:542
  30.1 0.0 collective-permute-done.4.above
  30.1 1.7 %last_substep.1 = (f32[3,8,16,128]{3,2,1,0:T(8,128)}, f32[8,16,128]{2,1,0:T(8,128)}, f32[8,16,128]{2,1,0:T(8,128)}, f32[16,8,16,128]{3,2,1,0:T(8,128)}, f32[1600...) custom-call(f32[13,8,128]{2,1,0:T(8,128)S(1)} %collective-permute-do, ...), custom_call_target="tpu_custom_call", output_to_operand_aliasing={{4}: (12, {}), {5}: (13, {}), {6}: (14, {})} | custom-call | tf_op jit(solution)/shard_map/last_substep/pallas_call | solution.py:505
  (1 shorter events, 0.0 us)
Async XLA Ops:
  0.6 11.9 %copy-start = (f32[16,8,16,128]{3,2,1,0:T(8,128)S(1)}, f32[16,8,16,128]{3,2,1,0:T(8,128)}, u32[]{:S(2)}) copy-start(f32[16,8,16,128]{3,2,1,0:T(8,128)} %mass.7) | copy-start | bytes 3145732
  1.9 10.7 %collective-permute-start = (f32[8,2,16,128]{3,2,1,0:T(8,128)S(1)}, f32[8,2,16,128]{3,2,1,0:T(8,128)S(1)}, u32[]{:S(2)}, u32[]{:S(2)}) collective-permute-start(f32[8,2,16,128]{3,2,1,0:T(8,128)S(1)} %get-tuple-element.24), channel_id=1, source_target_pairs={{4,8},{8,4},{12,16},{16,12},{20,24},{24,20},{28,32},{32,28},{36,40... | collective-permute-start | bytes 393224 | tf_op jit(solution)/shard_map/ppermute | solution.py:538
  8.0 4.6 %collective-permute-start.1 = (f32[8,2,16,128]{3,2,1,0:T(8,128)S(1)}, f32[8,2,16,128]{3,2,1,0:T(8,128)S(1)}, u32[]{:S(2)}, u32[]{:S(2)}) collective-permute-start(f32[8,2,16,128]{3,2,1,0:T(8,128)S(1)} %get-tuple-element.25), channel_id=1, source_target_pairs={{0,4},{4,0},{8,12},{12,8},{16,20},{20,16},{24,28},{28,24},{32,36},... | collective-permute-start | bytes 393224 | tf_op jit(solution)/shard_map/ppermute | solution.py:539
  9.9 2.7 %copy-start.1 = (f32[3,8,16,128]{3,2,1,0:T(8,128)S(1)}, f32[3,8,16,128]{3,2,1,0:T(8,128)}, u32[]{:S(2)}) copy-start(f32[3,8,16,128]{3,2,1,0:T(8,128)} %wind.5) | copy-start | bytes 589828
  9.9 2.7 %copy-start.2 = (s32[8,16,128]{2,1,0:T(8,128)S(1)}, s32[8,16,128]{2,1,0:T(8,128)}, u32[]{:S(2)}) copy-start(s32[8,16,128]{2,1,0:T(8,128)} %count.7) | copy-start | bytes 196612
  9.9 2.7 %copy-start.3 = (f32[8,16,128]{2,1,0:T(8,128)S(1)}, f32[8,16,128]{2,1,0:T(8,128)}, u32[]{:S(2)}) copy-start(f32[8,16,128]{2,1,0:T(8,128)} %heat.5) | copy-start | bytes 196612
  9.9 2.6 %copy-start.4 = (f32[8,16,128]{2,1,0:T(8,128)S(1)}, f32[8,16,128]{2,1,0:T(8,128)}, u32[]{:S(2)}) copy-start(f32[8,16,128]{2,1,0:T(8,128)} %soot.5) | copy-start | bytes 196612
  10.0 20.2 %collective-permute-start.4 = (f32[16,2,16,128]{3,2,1,0:T(8,128)S(1)}, f32[16,2,16,128]{3,2,1,0:T(8,128)S(1)}, u32[]{:S(2)}, u32[]{:S(2)}) collective-permute-start(f32[16,2,16,128]{3,2,1,0:T(8,128)S(1)} %pack_mass.1), channel_id=1, source_target_pairs={{0,4},{4,8},{8,12},{12,16},{16,20},{20,24},{24,28},{28,32},{32,36}... | collective-permute-start | bytes 786440 | tf_op jit(solution)/shard_map/ppermute | solution.py:543
  12.7 14.6 %collective-permute-start.2 = (f32[13,8,128]{2,1,0:T(8,128)S(1)}, f32[13,8,128]{2,1,0:T(8,128)S(1)}, u32[]{:S(2)}, u32[]{:S(2)}) collective-permute-start(f32[13,8,128]{2,1,0:T(8,128)S(1)} %get-tuple-element.27), channel_id=1, source_target_pairs={{0,1},{1,0},{2,3},{3,2},{4,5},{5,4},{6,7},{7,6},{8,9},{9,8},{10,11... | collective-permute-start | bytes 159752 | tf_op jit(solution)/shard_map/ppermute | solution.py:541
  14.7 15.5 %collective-permute-start.3 = (f32[13,8,128]{2,1,0:T(8,128)S(1)}, f32[13,8,128]{2,1,0:T(8,128)S(1)}, u32[]{:S(2)}, u32[]{:S(2)}) collective-permute-start(f32[13,8,128]{2,1,0:T(8,128)S(1)} %get-tuple-element.28), channel_id=1, source_target_pairs={{1,2},{2,1},{5,6},{6,5},{9,10},{10,9},{13,14},{14,13},{17,18},{18,... | collective-permute-start | bytes 159752 | tf_op jit(solution)/shard_map/ppermute | solution.py:542
